TPU v7x, 32 devices: a whole 2x2x4 slice. The times are simulated.
32 devices in a mesh: dp: 4 (over z), gx: 2 (over core), gy: 4 (over y, x).
Axes of the slice: x: 2, y: 2, z: 4, core: 2. Of those that a mesh axis runs over, the one named last changes fastest.
Arguments:
- layer_input: bfloat16 [16384, 1280], P(('dp', 'gx', 'gy')), may hold values from -6 to 6
- first_gain: float32 [1280], P('gy'), may hold values from 0.5 to 1.5
- query_scale: float32 [80], replicated, may hold values from -1 to 1
- query_weight: bfloat16 [1280, 1280], P('gy', 'gx'), may hold values from -0.15625 to 0.15625
- key_weight: bfloat16 [1280, 1280], P('gy', 'gx'), may hold values from -0.15625 to 0.15625
- value_weight: bfloat16 [1280, 1280], P('gy', 'gx'), may hold values from -0.15625 to 0.15625
- output_weight: bfloat16 [1280, 1280], P('gx', 'gy'), may hold values from -2 to 2
- second_gain: float32 [1280], P('gy'), may hold values from 0.5 to 1.5
- inner_weight: bfloat16 [1280, 1280], P('gy', 'gx'), may hold values from -0.15625 to 0.15625
- inner_bias: float32 [1280], P('gx'), may hold values from -3 to 3
- outer_weight: bfloat16 [1280, 1280], P('gx', 'gy'), may hold values from -0.15625 to 0.15625
- outer_bias: float32 [1280], P('gy'), may hold values from -3 to 3
- prefix_len: int32 [4], replicated, may hold values from 409 to 2048
- output_cotangent: bfloat16 [16384, 1280], P(('dp', 'gx', 'gy')), may hold values from -6 to 6
Outputs:
- layer_output: bfloat16 [16384, 1280], P(('dp', 'gx', 'gy'))
- input_gradient: bfloat16 [16384, 1280], P(('dp', 'gx', 'gy'))
- first_gain_gradient: float32 [1280], P('gy')
- query_scale_gradient: float32 [80], replicated
- query_weight_gradient: float32 [1280, 1280], P('gy', 'gx')
- key_weight_gradient: float32 [1280, 1280], P('gy', 'gx')
- value_weight_gradient: float32 [1280, 1280], P('gy', 'gx')
- output_weight_gradient: float32 [1280, 1280], P('gx', 'gy')
- second_gain_gradient: float32 [1280], P('gy')
- inner_weight_gradient: float32 [1280, 1280], P('gy', 'gx')
- inner_bias_gradient: float32 [1280], P('gx')
- outer_weight_gradient: float32 [1280, 1280], P('gx', 'gy')
- outer_bias_gradient: float32 [1280], P('gy')
Inputs may be any that keep to these rules, and one draw needn't show every extreme that they name: Each sequence's first prefix_len positions are seen by all its queries.
All inputs are finite; a program needn't handle non-finite values.
Results may differ from a plain program's by a relative error of at most 0.018.
Values may be sent and summed in bfloat16 or wider, within the bound.
A program may use at most 448 MiB of HBM per device.

v0:
```python
import math

import jax
import jax.numpy as jnp
from jax import lax
from jax.sharding import PartitionSpec as P

D = 1280
DH = 80
F = 1280
LEN = 4096


softplus_unit = 1.442695041


def for_sending(array):
    return jax.tree.map(lambda a: a.astype(jnp.bfloat16) if a.dtype == jnp.float32 else a, array)


def relayout(pair):
    return jax.tree.map(
        lambda part, own: part.astype(own.dtype),
        lax.all_to_all(for_sending(pair), "gy", split_axis=1, concat_axis=0, tiled=True),
        pair,
    )


def feature_total(partial_value):
    return lax.psum(partial_value, "gy")


def normalize_local(values, gain):
    total = feature_total(jnp.sum(values * values, axis=-1, keepdims=True))
    inverse = lax.rsqrt(total / D + 1e-06)
    unit = values * inverse
    return (unit, inverse, (unit * gain).astype(jnp.bfloat16))


def normalize_back(upstream, unit, inverse, gain):
    scaled = upstream * gain
    total = feature_total(jnp.sum(scaled * unit, axis=-1, keepdims=True))
    return (inverse * (scaled - unit * (total / D)), jnp.sum(upstream * unit, axis=0))


def group_rows(values):
    return lax.all_gather(values, "gx", axis=0, tiled=True)


def group_tokens(values):
    return lax.all_gather(values, "gy", axis=0, tiled=True)


def multiply(left, right, contract):
    return lax.dot_general(
        left, right, (((1,), (contract,)), ((), ())), preferred_element_type=jnp.float32
    )


def outer_sum(left, right):
    return lax.dot_general(
        left, right, (((0,), (0,)), ((), ())), preferred_element_type=jnp.float32
    )


def product_term(left, right, contract):

    def term(start, count):
        return multiply(left, right, contract)

    return term


def sum_over_y(left, right, contract):
    rows = left.shape[0] // lax.axis_size("gy")
    return lax.psum_scatter(
        product_term(left, right, contract)(jnp.int32(0), lax.axis_size("gy") * rows),
        "gy",
        scatter_dimension=0,
        tiled=True,
    )


def sum_over_x(term, rows):
    return lax.psum_scatter(
        term(jnp.int32(0), rows * lax.axis_size("gx")).astype(jnp.bfloat16),
        "gx",
        scatter_dimension=0,
        tiled=True,
    ).astype(jnp.float32)


def block_scores(rows, keys, first, prefix):
    scores = jnp.einsum("qhd,khd->hqk", rows, keys, preferred_element_type=jnp.float32)
    place = first + jnp.arange(rows.shape[0], dtype=jnp.int32)[:, None]
    column = jnp.arange(keys.shape[0], dtype=jnp.int32)[None, :]
    allowed = (column <= place) | (column < prefix)
    return jnp.where(allowed[None], scores, -1e30)


def attention_forward(queries, keys, values, offset, prefix):
    block = min(512, queries.shape[0])
    shaped = queries.reshape(queries.shape[0] // block, block, queries.shape[1], queries.shape[2])
    firsts = offset + jnp.arange(shaped.shape[0], dtype=jnp.int32) * block

    def one_block(pair):
        scores = block_scores(pair[0], keys, pair[1], prefix)
        largest = jnp.max(scores, axis=-1, keepdims=True)
        raised = jnp.exp(scores - largest)
        total = jnp.sum(raised, axis=-1, keepdims=True)
        weights = (raised / total).astype(jnp.bfloat16)
        mixed = jnp.einsum("hqk,khd->qhd", weights, values, preferred_element_type=jnp.float32)
        return (mixed, largest[..., 0] + jnp.log(total[..., 0]))

    mixed, logsum = lax.map(one_block, (shaped, firsts))
    return (mixed.reshape(queries.shape), logsum)


def attention_backward(queries, keys, values, upstream, logsum, offset, prefix):
    block = min(512, queries.shape[0])
    count = queries.shape[0] // block
    shaped = queries.reshape(count, block, queries.shape[1], queries.shape[2])
    upstream_blocks = upstream.reshape(count, block, queries.shape[1], queries.shape[2])
    firsts = offset + jnp.arange(count, dtype=jnp.int32) * block

    def one_block(carry, item):
        rows, grads, lse_block, first = item
        scores = block_scores(rows, keys, first, prefix)
        weights = jnp.exp(scores - lse_block[..., None])
        along = jnp.einsum("qhd,khd->hqk", grads, values, preferred_element_type=jnp.float32)
        centre = jnp.sum(weights * along, axis=-1, keepdims=True)
        score_low = (weights * (along - centre)).astype(jnp.bfloat16)
        query_part = jnp.einsum("hqk,khd->qhd", score_low, keys, preferred_element_type=jnp.float32)
        key_total = carry[0] + jnp.einsum(
            "hqk,qhd->khd", score_low, rows, preferred_element_type=jnp.float32
        )
        value_total = carry[1] + jnp.einsum(
            "hqk,qhd->khd", weights.astype(jnp.bfloat16), grads, preferred_element_type=jnp.float32
        )
        return ((key_total, value_total), query_part)

    zeros = jnp.zeros(keys.shape, jnp.float32)
    totals, query_parts = lax.scan(
        one_block, (zeros, zeros), (shaped, upstream_blocks, logsum, firsts)
    )
    return (query_parts.reshape(queries.shape), totals[0], totals[1])


def per_device(
    layer_input,
    first_gain,
    query_scale,
    query_weight,
    key_weight,
    value_weight,
    output_weight,
    second_gain,
    inner_weight,
    inner_bias,
    outer_weight,
    outer_bias,
    prefix_len,
    output_cotangent,
):
    y_count = lax.axis_size("gy")
    own_rows = layer_input.shape[0]
    feature_width = D // y_count
    arrived = relayout(
        (
            layer_input.reshape(own_rows, y_count, feature_width),
            output_cotangent.reshape(own_rows, y_count, feature_width),
        )
    )
    input_block = arrived[0].reshape(own_rows * y_count, feature_width)
    cotangent_block = arrived[1].reshape(own_rows * y_count, feature_width)
    width_here = query_weight.shape[1]
    heads_here = width_here // DH
    input_rows = input_block.shape[0]
    group = input_rows * lax.axis_size("gx")
    query_rows = group // lax.axis_size("gy")
    column_index = lax.axis_index("gy")
    head_index = lax.axis_index("gx")
    data_index = lax.axis_index("dp")
    first_row = column_index * query_rows
    sequence_here = first_row // LEN
    offset = first_row % LEN
    per_group = prefix_len.shape[0] // lax.axis_size("dp")
    prefix = lax.dynamic_index_in_dim(
        prefix_len, data_index * per_group + sequence_here, 0, keepdims=False
    )
    factor = jax.nn.softplus(query_scale) * (softplus_unit / math.sqrt(DH))
    joined = jnp.concatenate([query_weight, key_weight, value_weight], axis=1)
    inputs = input_block.astype(jnp.float32)
    unit_one, inverse_one, normed_one = normalize_local(inputs, first_gain)
    gathered_one = group_rows(normed_one)
    projected = sum_over_y(gathered_one, joined, 0)
    queries = projected[:, :width_here].reshape(query_rows, heads_here, DH)
    keys = projected[:, width_here : 2 * width_here].astype(jnp.bfloat16)
    values = projected[:, 2 * width_here :].astype(jnp.bfloat16)
    scaled = (queries * factor).astype(jnp.bfloat16)
    all_keys, all_values = (
        lax.all_gather(keys, "gy", axis=0, tiled=True),
        lax.all_gather(values, "gy", axis=0, tiled=True),
    )
    sequence_keys = all_keys.reshape(LEN, heads_here, DH)
    sequence_values = all_values.reshape(LEN, heads_here, DH)
    mixed, logsum = attention_forward(scaled, sequence_keys, sequence_values, offset, prefix)
    attended = mixed.reshape(query_rows, width_here).astype(jnp.bfloat16)
    attended_all = group_tokens(attended)
    middle = inputs + sum_over_x(product_term(attended_all, output_weight, 0), input_rows)
    unit_two, inverse_two, normed_two = normalize_local(middle, second_gain)
    gathered_two = group_rows(normed_two)
    before = sum_over_y(gathered_two, inner_weight, 0) + inner_bias
    hidden = jax.nn.silu(before).astype(jnp.bfloat16)
    hidden_all = group_tokens(hidden)
    outer = sum_over_x(product_term(hidden_all, outer_weight, 0), input_rows)
    output_block = (middle + outer + outer_bias).astype(jnp.bfloat16)
    upstream = cotangent_block.astype(jnp.float32)
    outer_bias_part = jnp.sum(upstream, axis=0)
    cotangent_all = group_rows(cotangent_block)
    outer_gradient = outer_sum(hidden_all, cotangent_all)
    hidden_gradient = sum_over_y(cotangent_all, outer_weight, 1)
    sigmoid_value = jax.nn.sigmoid(before)
    before_gradient = hidden_gradient * sigmoid_value * (1.0 + before * (1.0 - sigmoid_value))
    inner_bias_part = jnp.sum(before_gradient, axis=0)
    before_low = before_gradient.astype(jnp.bfloat16)
    before_all = group_tokens(before_low)
    normed_two_gradient = sum_over_x(product_term(before_all, inner_weight, 1), input_rows)
    inner_gradient = outer_sum(gathered_two, before_all)
    middle_part, second_gain_part = normalize_back(
        normed_two_gradient, unit_two, inverse_two, second_gain
    )
    middle_gradient = upstream + middle_part
    branch_all = group_rows(middle_gradient.astype(jnp.bfloat16))
    output_gradient = outer_sum(attended_all, branch_all)
    attended_gradient = sum_over_y(branch_all, output_weight, 1).astype(jnp.bfloat16)
    scaled_gradient, key_part, value_part = attention_backward(
        scaled,
        sequence_keys,
        sequence_values,
        attended_gradient.reshape(query_rows, heads_here, DH),
        logsum,
        offset,
        prefix,
    )
    scale_part = jnp.sum(scaled_gradient * queries, axis=(0, 1))
    query_gradient = (scaled_gradient * factor).reshape(query_rows, width_here).astype(jnp.bfloat16)
    key_full = key_part.reshape(LEN, width_here)
    value_full = value_part.reshape(LEN, width_here)
    key_sum, value_sum = (
        lax.psum_scatter(
            key_full.astype(jnp.bfloat16), "gy", scatter_dimension=0, tiled=True
        ).astype(jnp.float32),
        lax.psum_scatter(
            value_full.astype(jnp.bfloat16), "gy", scatter_dimension=0, tiled=True
        ).astype(jnp.float32),
    )
    joined_gradient = jnp.concatenate(
        [query_gradient, key_sum.astype(jnp.bfloat16), value_sum.astype(jnp.bfloat16)], axis=1
    )
    joined_all = group_tokens(joined_gradient)
    normed_one_gradient = sum_over_x(product_term(joined_all, joined, 1), input_rows)
    joined_weight_gradient = outer_sum(gathered_one, joined_all)
    input_part, first_gain_part = normalize_back(
        normed_one_gradient, unit_one, inverse_one, first_gain
    )
    gradient_block = (middle_gradient + input_part).astype(jnp.bfloat16)
    returned = relayout(
        (
            output_block.reshape(y_count, own_rows, feature_width).transpose(1, 0, 2),
            gradient_block.reshape(y_count, own_rows, feature_width).transpose(1, 0, 2),
        )
    )
    layer_output = (
        returned[0]
        .reshape(y_count, own_rows, feature_width)
        .transpose(1, 0, 2)
        .reshape(own_rows, D)
    )
    input_gradient = (
        returned[1]
        .reshape(y_count, own_rows, feature_width)
        .transpose(1, 0, 2)
        .reshape(own_rows, D)
    )
    summed = (
        lax.psum(joined_weight_gradient.astype(jnp.bfloat16), "dp").astype(jnp.float32),
        lax.psum(output_gradient.astype(jnp.bfloat16), "dp").astype(jnp.float32),
        lax.psum(inner_gradient.astype(jnp.bfloat16), "dp").astype(jnp.float32),
        lax.psum(outer_gradient.astype(jnp.bfloat16), "dp").astype(jnp.float32),
    )
    gain_width = first_gain.shape[0]
    hidden_width = inner_bias.shape[0]
    feature_start = column_index * gain_width
    hidden_start = head_index * hidden_width
    wide_zero = jnp.zeros((D,), jnp.float32)
    small = lax.psum(
        (
            lax.dynamic_update_slice_in_dim(
                jnp.zeros((F,), jnp.float32), inner_bias_part, hidden_start, 0
            ),
            lax.dynamic_update_slice_in_dim(wide_zero, first_gain_part, feature_start, 0),
            lax.dynamic_update_slice_in_dim(wide_zero, second_gain_part, feature_start, 0),
            lax.dynamic_update_slice_in_dim(wide_zero, outer_bias_part, feature_start, 0),
            scale_part,
        ),
        ("dp", "gx", "gy"),
    )
    query_scale_gradient = small[4] * (softplus_unit / math.sqrt(DH)) * jax.nn.sigmoid(query_scale)
    return (
        layer_output,
        input_gradient,
        lax.dynamic_slice_in_dim(small[1], feature_start, gain_width, 0),
        query_scale_gradient,
        summed[0][:, :width_here],
        summed[0][:, width_here : 2 * width_here],
        summed[0][:, 2 * width_here :],
        summed[1],
        lax.dynamic_slice_in_dim(small[2], feature_start, gain_width, 0),
        summed[2],
        lax.dynamic_slice_in_dim(small[0], hidden_start, hidden_width, 0),
        summed[3],
        lax.dynamic_slice_in_dim(small[3], feature_start, gain_width, 0),
    )


def solution(mesh):
    placed = (
        P(("dp", "gx", "gy"), None),
        P("gy"),
        P(),
        P("gy", "gx"),
        P("gy", "gx"),
        P("gy", "gx"),
        P("gx", "gy"),
        P("gy"),
        P("gy", "gx"),
        P("gx"),
        P("gx", "gy"),
        P("gy"),
        P(),
        P(("dp", "gx", "gy"), None),
    )
    return jax.shard_map(
        per_device,
        mesh=mesh,
        in_specs=placed,
        out_specs=(
            P(("dp", "gx", "gy"), None),
            P(("dp", "gx", "gy"), None),
            P("gy"),
            P(),
            P("gy", "gx"),
            P("gy", "gx"),
            P("gy", "gx"),
            P("gx", "gy"),
            P("gy"),
            P("gy", "gx"),
            P("gx"),
            P("gx", "gy"),
            P("gy"),
        ),
        check_vma=False,
    )
```

profile of v0, /device:TPU:0, one launch (start us, length us, event | category | flops | bytes accessed | tf_op | source)
XLA Modules:
  0.0 2210.7 jit_solution(5604287375422138272)
XLA Ops:
  8.9 21.9 all_to_all.42
  46.1 11.5 all-gather.11.cloned.1.call-done
  57.6 16.8 fusion.53
  74.4 274.0 %reduce-scatter.11.cloned.1.call-done = f32[1024,1920]{1,0:T(8,128)} async-done(((f32[4096,1920]{1,0:T(8,128)}), f32[1024,1920]{1,0:T(8,128)}) %reduce-scatter.11.cloned.1.call-update) | async-done | bytes 7864336 | tf_op jit(solution)/shard_map/reduce_scatter | solution.py:76
  365.6 49.7 %all-gather.15.cloned.1.call-done = bf16[4096,640]{1,0:T(8,128)(2,1)} async-done(((bf16[1024,640]{1,0:T(8,128)(2,1)}), bf16[4096,640]{1,0:T(8,128)(2,1)}) %all-gather.15.cloned.1.call-update) | async-done | bytes 5242896 | tf_op jit(solution)/shard_map/all_gather | solution.py:203
  423.2 55.1 %all-gather.13.cloned.1.call-done = bf16[4096,640]{1,0:T(8,128)(2,1)} async-done(((bf16[1024,640]{1,0:T(8,128)(2,1)}), bf16[4096,640]{1,0:T(8,128)(2,1)}) %all-gather.13.cloned.1.call-update) | async-done | bytes 5242896 | tf_op jit(solution)/shard_map/all_gather | solution.py:202
  486.3 159.4 %while.27 = (s32[]{:T(128)}, bf16[2,512,8,80]{1,3,2,0:T(8,128)(2,1)}, f32[2,8,512]{2,1,0:T(8,128)S(1)}, s32[2]{0:T(128)S(1)}, s32[]{:T(128)}, /*index=5*/bf16[2,...) while((s32[]{:T(128)}, ...), condition=%wide.region_6.7_spmd, body=%wide.region_3.6_spmd.sunk | while | flops 5523898880 | bytes 222310512 | solution.py:115
  490.0 26.9 %select_reduce_fusion.2 = (f32[8,512]{1,0:T(8,128)S(1)}, f32[8,512,4096]{2,1,0:T(8,128)}) fusion(pred[512,4096]{1,0:T(8,128)(4,1)S(1)} %fusion.107, bf16[4096,8,80]{0,2,1:T(8,128)(2,1)} %get-tuple-element.423, bf16[2,512,8,80]{1,3,2,0:T(8,128)(2,1)} %get-tuple-element.422, s32[]{:T(128)S(6)} %copy.90), kind=kOutput, calls=%fused_computation.2.clone.1 | convolution fusion | flops 2717904896 | bytes 75120640 | tf_op jit(solution)/shard_map/while/body/eval_jaxpr/qhd,khd->hqk/dot_general | solution.py:94
  516.9 21.5 fusion.108
  538.5 27.5 %fusion.109 = bf16[2,512,8,80]{1,3,2,0:T(8,128)(2,1)} fusion(bf16[2,512,8,80]{1,3,2,0:T(8,128)(2,1)} %get-tuple-element.409, s32[]{:T(128)S(6)} %copy.90, bf16[4096,8,80]{0,2,1:T(8,128)(2,1)} %get-tuple-element.424, f32[8,512,4096]{2,1,0:T(8,128)} %get-tuple-element.384, f32[8,512]{1,0:T(8,128)S(1)} %fusion.108, ...), kind=kOutput, calls=%fused_computation.8.clone.1 | convolution fusion | flops 2751463424 | bytes 75792384 | tf_op jit(solution)/shard_map/while/body/eval_jaxpr/hqk,khd->qhd/dot_general | solution.py:112
  569.7 26.9 %select_reduce_fusion.2 = (f32[8,512]{1,0:T(8,128)S(1)}, f32[8,512,4096]{2,1,0:T(8,128)}) fusion(pred[512,4096]{1,0:T(8,128)(4,1)S(1)} %fusion.107, bf16[4096,8,80]{0,2,1:T(8,128)(2,1)} %get-tuple-element.423, bf16[2,512,8,80]{1,3,2,0:T(8,128)(2,1)} %get-tuple-element.422, s32[]{:T(128)S(6)} %copy.90), kind=kOutput, calls=%fused_computation.2.clone.1 | convolution fusion | flops 2717904896 | bytes 75120640 | tf_op jit(solution)/shard_map/while/body/eval_jaxpr/qhd,khd->hqk/dot_general | solution.py:94
  596.7 21.5 fusion.108
  618.2 27.5 %fusion.109 = bf16[2,512,8,80]{1,3,2,0:T(8,128)(2,1)} fusion(bf16[2,512,8,80]{1,3,2,0:T(8,128)(2,1)} %get-tuple-element.409, s32[]{:T(128)S(6)} %copy.90, bf16[4096,8,80]{0,2,1:T(8,128)(2,1)} %get-tuple-element.424, f32[8,512,4096]{2,1,0:T(8,128)} %get-tuple-element.384, f32[8,512]{1,0:T(8,128)S(1)} %fusion.108, ...), kind=kOutput, calls=%fused_computation.8.clone.1 | convolution fusion | flops 2751463424 | bytes 75792384 | tf_op jit(solution)/shard_map/while/body/eval_jaxpr/hqk,khd->qhd/dot_general | solution.py:112
  650.2 61.0 %all-gather.17.cloned.1.call-done = bf16[4096,640]{0,1:T(8,128)(2,1)} async-done(((bf16[1024,640]{0,1:T(8,128)(2,1)}), bf16[4096,640]{0,1:T(8,128)(2,1)}) %all-gather.17.cloned.1.call-update) | async-done | bytes 5242896 | tf_op jit(solution)/shard_map/all_gather | solution.py:51
  719.4 19.5 all_to_all.43
  755.3 9.8 fusion.55
  775.8 98.7 %reduce-scatter.19.cloned.1.call-done = f32[1024,640]{1,0:T(8,128)} async-done(((f32[4096,640]{1,0:T(8,128)}), f32[1024,640]{1,0:T(8,128)}) %reduce-scatter.19.cloned.1.call-update) | async-done | bytes 2621456 | tf_op jit(solution)/shard_map/reduce_scatter | solution.py:76
  874.5 106.5 %reduce-scatter.15.cloned.1.call-done = f32[1024,640]{1,0:T(8,128)} async-done(((f32[4096,640]{1,0:T(8,128)}), f32[1024,640]{1,0:T(8,128)}) %reduce-scatter.15.cloned.1.call-update) | async-done | bytes 2621456 | tf_op jit(solution)/shard_map/reduce_scatter | solution.py:76
  986.9 61.4 %all-gather.25.cloned.1.call-done = bf16[4096,640]{1,0:T(8,128)(2,1)} async-done(((bf16[1024,640]{1,0:T(8,128)(2,1)}), bf16[4096,640]{1,0:T(8,128)(2,1)}) %all-gather.25.cloned.1.call-update) | async-done | bytes 5242896 | tf_op jit(solution)/shard_map/all_gather | solution.py:51
  1054.6 10.4 reduce-scatter.21.cloned.1.call-done
  1068.3 10.3 psum.93
  1083.2 10.5 all-gather.27.cloned.1.call-done
  1102.8 104.7 %reduce-scatter.23.cloned.1.call-done = f32[1024,640]{1,0:T(8,128)} async-done(((f32[4096,640]{1,0:T(8,128)}), f32[1024,640]{1,0:T(8,128)}) %reduce-scatter.23.cloned.1.call-update) | async-done | bytes 2621456 | tf_op jit(solution)/shard_map/reduce_scatter | solution.py:76
  1216.7 445.6 %while.28 = (s32[]{:T(128)}, f32[4096,8,80]{0,2,1:T(8,128)}, f32[4096,8,80]{0,2,1:T(8,128)}, f32[2,512,8,80]{1,0,3,2:T(2,128)}, bf16[2,512,8,80]{1,3,2,0:T(8,128...) while((s32[]{:T(128)}, f32[4096,8,80]{0,2,1:T(8,128)}, ...), condition=%wide.region_19.20_spmd.clone, body=%wide.region_17.19_spmd.clone.sunk | while | flops 13637779456 | bytes 584184064 | solution.py:143
  1220.9 26.4 %fusion.119 = f32[8,512,4096]{2,1,0:T(8,128)} fusion(bf16[4096,8,80]{0,2,1:T(8,128)(2,1)} %get-tuple-element.459, bf16[2,512,8,80]{1,3,2,0:T(8,128)(2,1)} %get-tuple-element.456, s32[]{:T(128)S(6)} %copy.100), kind=kOutput, calls=%fused_computation.34.clone.1 | convolution fusion | flops 2684354560 | bytes 73007104 | tf_op jit(solution)/shard_map/while/body/eval_jaxpr/qhd,khd->hqk/dot_general | solution.py:94
  1247.3 28.1 %bitcast_add_fusion.5 = f32[4096,8,80]{0,2,1:T(8,128)} fusion(f32[4096,8,80]{0,2,1:T(8,128)} %get-tuple-element.441, f32[8,512,4096]{2,1,0:T(8,128)} %fusion.119, f32[8,512]{1,0:T(8,128)S(1)} %dynamic-slice_bitcast_fusion.2, pred[512,4096]{1,0:T(8,128)(4,1)S(1)} %fusion.120, pred[]{:T(512)S(6)} %compare.6, ...), kind=kOutput, calls=%fused_computation.25.clone.1 | convolution fusion | flops 2739929088 | bytes 90849288 | tf_op jit(solution)/shard_map/while/body/eval_jaxpr/hqk,qhd->khd/dot_general | solution.py:137
  1275.4 47.5 %multiply_reduce_fusion.4 = (f32[8,512]{1,0:T(8,128)S(1)}, f32[8,512,4096]{2,1,0:T(8,128)}) fusion(f32[8,512,4096]{2,1,0:T(8,128)} %fusion.119, f32[8,512]{1,0:T(8,128)S(1)} %dynamic-slice_bitcast_fusion.2, pred[512,4096]{1,0:T(8,128)(4,1)S(1)} %fusion.120, bf16[4096,8,80]{0,2,1:T(8,128)(2,1)} %get-tuple-element.462, ...), kind=kOutput, calls=%fused_computation.18.clone.2 | convolution fusion | flops 2751459328 | bytes 142245888 | tf_op jit(solution)/shard_map/while/body/eval_jaxpr/qhd,khd->hqk/dot_general | solution.py:130
  1322.9 52.6 %multiply_convert_fusion.7 = bf16[8,512,4096]{2,1,0:T(8,128)(2,1)} fusion(f32[8,512,4096]{2,1,0:T(8,128)} %get-tuple-element.397, f32[8,512,4096]{2,1,0:T(8,128)} %fusion.119, f32[8,512]{1,0:T(8,128)S(1)} %get-tuple-element.398, f32[8,512]{1,0:T(8,128)S(1)} %dynamic-slice_bitcast_fusion.2, pred[512,4096]{1,0:T(8,128)(4,1)S(1)} %fusion.120), kind=kLoop, calls=%fused_computation.17.clone.1 | loop fusion | flops 83886080 | bytes 169902080 | tf_op jit(solution)/shard_map/while/body/eval_jaxpr/convert_element_type | solution.py:132
  1375.5 17.4 convolution_bitcast_fusion.2
  1392.9 17.7 bitcast_add_fusion.4
  1412.0 24.2 %dynamic_update_slice.35 = f32[2,512,8,80]{1,0,3,2:T(2,128)} dynamic-update-slice(f32[2,512,8,80]{1,0,3,2:T(2,128)} %get-tuple-element.442, f32[1,512,8,80]{1,0,3,2:T(1,128)S(1)} %copy.81, s32[]{:T(128)S(6)} %copy.100, s32[]{:T(128)} %constant.88.clone.1..sunk, s32[]{:T(128)} %constant.88.clone.1..sunk, s32[]{:T(128)} %constant.88.clone.1..sunk) | dynamic-update-slice | bytes 2621444 | tf_op jit(solution)/shard_map/while/body/jit(dynamic_update_index_in_dim)/dynamic_update_slice | solution.py:115
  1440.0 26.4 %fusion.119 = f32[8,512,4096]{2,1,0:T(8,128)} fusion(bf16[4096,8,80]{0,2,1:T(8,128)(2,1)} %get-tuple-element.459, bf16[2,512,8,80]{1,3,2,0:T(8,128)(2,1)} %get-tuple-element.456, s32[]{:T(128)S(6)} %copy.100), kind=kOutput, calls=%fused_computation.34.clone.1 | convolution fusion | flops 2684354560 | bytes 73007104 | tf_op jit(solution)/shard_map/while/body/eval_jaxpr/qhd,khd->hqk/dot_general | solution.py:94
  1466.4 31.9 %bitcast_add_fusion.5 = f32[4096,8,80]{0,2,1:T(8,128)} fusion(f32[4096,8,80]{0,2,1:T(8,128)} %get-tuple-element.441, f32[8,512,4096]{2,1,0:T(8,128)} %fusion.119, f32[8,512]{1,0:T(8,128)S(1)} %dynamic-slice_bitcast_fusion.2, pred[512,4096]{1,0:T(8,128)(4,1)S(1)} %fusion.120, pred[]{:T(512)S(6)} %compare.6, ...), kind=kOutput, calls=%fused_computation.25.clone.1 | convolution fusion | flops 2739929088 | bytes 90849288 | tf_op jit(solution)/shard_map/while/body/eval_jaxpr/hqk,qhd->khd/dot_general | solution.py:137
  1498.3 47.5 %multiply_reduce_fusion.4 = (f32[8,512]{1,0:T(8,128)S(1)}, f32[8,512,4096]{2,1,0:T(8,128)}) fusion(f32[8,512,4096]{2,1,0:T(8,128)} %fusion.119, f32[8,512]{1,0:T(8,128)S(1)} %dynamic-slice_bitcast_fusion.2, pred[512,4096]{1,0:T(8,128)(4,1)S(1)} %fusion.120, bf16[4096,8,80]{0,2,1:T(8,128)(2,1)} %get-tuple-element.462, ...), kind=kOutput, calls=%fused_computation.18.clone.2 | convolution fusion | flops 2751459328 | bytes 142245888 | tf_op jit(solution)/shard_map/while/body/eval_jaxpr/qhd,khd->hqk/dot_general | solution.py:130
  1545.8 52.6 %multiply_convert_fusion.7 = bf16[8,512,4096]{2,1,0:T(8,128)(2,1)} fusion(f32[8,512,4096]{2,1,0:T(8,128)} %get-tuple-element.397, f32[8,512,4096]{2,1,0:T(8,128)} %fusion.119, f32[8,512]{1,0:T(8,128)S(1)} %get-tuple-element.398, f32[8,512]{1,0:T(8,128)S(1)} %dynamic-slice_bitcast_fusion.2, pred[512,4096]{1,0:T(8,128)(4,1)S(1)} %fusion.120), kind=kLoop, calls=%fused_computation.17.clone.1 | loop fusion | flops 83886080 | bytes 169902080 | tf_op jit(solution)/shard_map/while/body/eval_jaxpr/convert_element_type | solution.py:132
  1598.4 17.4 convolution_bitcast_fusion.2
  1615.8 20.8 bitcast_add_fusion.4
  1637.9 24.2 %dynamic_update_slice.35 = f32[2,512,8,80]{1,0,3,2:T(2,128)} dynamic-update-slice(f32[2,512,8,80]{1,0,3,2:T(2,128)} %get-tuple-element.442, f32[1,512,8,80]{1,0,3,2:T(1,128)S(1)} %copy.81, s32[]{:T(128)S(6)} %copy.100, s32[]{:T(128)} %constant.88.clone.1..sunk, s32[]{:T(128)} %constant.88.clone.1..sunk, s32[]{:T(128)} %constant.88.clone.1..sunk) | dynamic-update-slice | bytes 2621444 | tf_op jit(solution)/shard_map/while/body/jit(dynamic_update_index_in_dim)/dynamic_update_slice | solution.py:115
  1679.4 51.5 %reduce-scatter.25.cloned.1.call-done = bf16[1024,640]{0,1:T(8,128)(2,1)} async-done(((bf16[4096,640]{0,1:T(8,128)(2,1)}), bf16[1024,640]{0,1:T(8,128)(2,1)}) %reduce-scatter.25.cloned.1.call-update) | async-done | bytes 1310736 | tf_op jit(solution)/shard_map/reduce_scatter | solution.py:251
  1730.9 64.2 %reduce-scatter.27.cloned.1.call-done = bf16[1024,640]{0,1:T(8,128)(2,1)} async-done(((bf16[4096,640]{0,1:T(8,128)(2,1)}), bf16[1024,640]{0,1:T(8,128)(2,1)}) %reduce-scatter.27.cloned.1.call-update) | async-done | bytes 1310736 | tf_op jit(solution)/shard_map/reduce_scatter | solution.py:254
  1799.2 148.1 %all-gather.29.cloned.1.call-done = bf16[4096,1920]{0,1:T(8,128)(2,1)} async-done(((bf16[1024,1920]{0,1:T(8,128)(2,1)}), bf16[4096,1920]{0,1:T(8,128)(2,1)}) %all-gather.29.cloned.1.call-update) | async-done | bytes 15728656 | tf_op jit(solution)/shard_map/all_gather | solution.py:51
  1947.3 12.5 convolution_convert_fusion
  1959.8 50.4 %all-gather.21.cloned.1.call-done = bf16[4096,640]{1,0:T(8,128)(2,1)} async-done(((bf16[1024,640]{1,0:T(8,128)(2,1)}), bf16[4096,640]{1,0:T(8,128)(2,1)}) %all-gather.21.cloned.1.call-update) | async-done | bytes 5242896 | tf_op jit(solution)/shard_map/all_gather | solution.py:51
  2032.6 17.8 convolution_convert_fusion.4
  2052.7 9.5 psum.94
  2076.9 10.6 all-to-all-done.1
  2095.5 53.9 %all-reduce.4.cloned.1.call-done = (bf16[320,1920]{1,0:T(8,128)(2,1)}, bf16[640,320]{0,1:T(8,128)(2,1)}, bf16[320,640]{1,0:T(8,128)(2,1)}, bf16[640,320]{0,1:T(8,128)(2,1)}) async-done(((bf16[320,1920]{1,0:T(8,128)(2,1)}, bf16[640,320]{0,1:T(8,128)(2,1)}, bf16[320,640]{1,0:T(8,128)(2,1)}, bf16[640,320]{0,1:T(8,128)(2,1)}), (bf16[320,1920]{1,0:T(8,128)(2,1)}, bf16[640,320]{0,1:T(8,128)(2,1)}, ...) | async-done | bytes 2457616 | tf_op jit(solution)/shard_map/psum | solution.py:287
  2156.0 39.5 %all-reduce = (f32[1280]{0:T(1024)S(1)}, f32[80]{0:T(128)S(1)}, f32[1280]{0:T(1024)S(1)}, f32[1280]{0:T(1024)S(1)}, f32[1280]{0:T(1024)S(1)}) all-reduce(f32[1280]{0:T(1024)S(1)} %dynamic_update_slice.23, f32[80]{0:T(128)S(1)} %multiply_reduce_fusion.1, ...), channel_id=1, replica_groups=mesh['dp'=4,'gx'=2,'gy'=4] {'dp','gx','gy'}, use_global_device_ids=true, to_apply=%region_26.27 | all-reduce | flops 5200 | bytes 41600 | tf_op jit(solution)/shard_map/psum | solution.py:297
  (266 shorter events, 228.2 us)
Async XLA Ops:
  7.2 759.6 %copy-start = (bf16[320,640]{1,0:T(8,128)(2,1)S(1)}, bf16[320,640]{1,0:T(8,128)(2,1)}, u32[]{:S(2)}) copy-start(bf16[320,640]{1,0:T(8,128)(2,1)} %param.26) | copy-start | bytes 1228804
  7.2 50.4 %all-gather.11.cloned.1.call-start = ((), (), s32[]{:S(2)}) async-start(), calls=%async_computation.14 | async-start | bytes 3932160 | tf_op jit(solution)/shard_map/all_gather | solution.py:47
  45.8 302.6 %reduce-scatter.11.cloned.1.call-start = ((), (), s32[]{:S(2)}) async-start(), calls=%async_computation.15 | async-start | bytes 39321600 | tf_op jit(solution)/shard_map/reduce_scatter | solution.py:76
  46.1 28.3 %copy-start.14 = (bf16[320,1920]{1,0:T(8,128)(2,1)}, bf16[320,1920]{1,0:T(8,128)(2,1)S(1)}, u32[]{:S(2)}) copy-start(bf16[320,1920]{1,0:T(8,128)(2,1)S(1)} %constant_dynamic-update-slice_fusion) | copy-start | bytes 3686404
  74.4 340.9 %all-gather.15.cloned.1.call-start = ((), (), s32[]{:S(2)}) async-start(), calls=%async_computation.17 | async-start | bytes 6553600 | tf_op jit(solution)/shard_map/all_gather | solution.py:203
  353.8 124.5 %all-gather.13.cloned.1.call-start = ((), (), s32[]{:S(2)}) async-start(), calls=%async_computation.16 | async-start | bytes 6553600 | tf_op jit(solution)/shard_map/all_gather | solution.py:202
  354.4 356.9 %all-gather.17.cloned.1.call-start = ((), (), s32[]{:S(2)}) async-start(), calls=%async_computation.18 | async-start | bytes 6553600 | tf_op jit(solution)/shard_map/all_gather | solution.py:51
  648.4 62.9 %copy-start.21 = (bf16[640,320]{0,1:T(8,128)(2,1)S(1)}, bf16[640,320]{0,1:T(8,128)(2,1)}, u32[]{:S(2)}) copy-start(bf16[640,320]{0,1:T(8,128)(2,1)} %param.24) | copy-start | bytes 1228804
  649.8 91.6 %reduce-scatter.13.cloned.1.call-start = ((), (), s32[]{:S(2)}) async-start(), calls=%async_computation.19 | async-start | bytes 3932160 | tf_op jit(solution)/shard_map/reduce_scatter | solution.py:85
  717.4 37.9 %all-gather.23.cloned.1.call-start = ((), (), s32[]{:S(2)}) async-start(), calls=%async_computation.24 | async-start | bytes 3932160 | tf_op jit(solution)/shard_map/all_gather | solution.py:47
  741.4 25.4 %all-gather.19.cloned.1.call-start = ((), (), s32[]{:S(2)}) async-start(), calls=%async_computation.20 | async-start | bytes 3932160 | tf_op jit(solution)/shard_map/all_gather | solution.py:47
  752.4 326.3 %copy-start.25 = (f32[2048,1]{0,1:T(1,128)}, f32[2048,1]{0,1:T(1,128)S(1)}, u32[]{:S(2)}) copy-start(f32[2048,1]{0,1:T(1,128)S(1)} %add_rsqrt_fusion) | copy-start | bytes 24580
  755.2 119.3 %reduce-scatter.19.cloned.1.call-start = ((), (), s32[]{:S(2)}) async-start(), calls=%async_computation.25 | async-start | bytes 13107200 | tf_op jit(solution)/shard_map/reduce_scatter | solution.py:76
  765.1 215.9 %reduce-scatter.15.cloned.1.call-start = ((), (), s32[]{:S(2)}) async-start(), calls=%async_computation.21 | async-start | bytes 13107200 | tf_op jit(solution)/shard_map/reduce_scatter | solution.py:76
  775.6 205.4 %copy-start.37 = (f32[640]{0:T(1024)S(1)}, f32[640]{0:T(1024)}, u32[]{:S(2)}) copy-start(f32[640]{0:T(1024)} %param.27) | copy-start | bytes 7684
  775.6 272.7 %all-gather.25.cloned.1.call-start = ((), (), s32[]{:S(2)}) async-start(), calls=%async_computation.26 | async-start | bytes 6553600 | tf_op jit(solution)/shard_map/all_gather | solution.py:51
  986.9 78.2 %reduce-scatter.21.cloned.1.call-start = ((), (), s32[]{:S(2)}) async-start(), calls=%async_computation.27 | async-start | bytes 3932160 | tf_op jit(solution)/shard_map/reduce_scatter | solution.py:85
  1054.6 39.1 %all-gather.27.cloned.1.call-start = ((), (), s32[]{:S(2)}) async-start(), calls=%async_computation.28 | async-start | bytes 3932160 | tf_op jit(solution)/shard_map/all_gather | solution.py:47
  1083.1 124.4 %reduce-scatter.23.cloned.1.call-start = ((), (), s32[]{:S(2)}) async-start(), calls=%async_computation.29 | async-start | bytes 13107200 | tf_op jit(solution)/shard_map/reduce_scatter | solution.py:76
  1102.7 628.2 %reduce-scatter.25.cloned.1.call-start = ((), (), s32[]{:S(2)}) async-start(), calls=%async_computation.30 | async-start | bytes 6553600 | tf_op jit(solution)/shard_map/reduce_scatter | solution.py:251
  1217.1 30.2 %copy-start.23 = (f32[2,8,512]{2,1,0:T(8,128)}, f32[2,8,512]{2,1,0:T(8,128)S(1)}, u32[]{:S(2)}) copy-start(f32[2,8,512]{2,1,0:T(8,128)S(1)} %get-tuple-element.460) | copy-start | bytes 98308 | tf_op jit(solution)/shard_map/while
  1217.1 30.1 %copy-start.44 = (s32[2]{0:T(128)}, s32[2]{0:T(128)S(1)}, u32[]{:S(2)}) copy-start(s32[2]{0:T(128)S(1)} %get-tuple-element.457) | copy-start | bytes 28 | tf_op jit(solution)/shard_map/while
  1375.5 17.4 copy-start.5
  1410.6 25.6 %copy-start.24 = (f32[2,8,512]{2,1,0:T(8,128)S(1)}, f32[2,8,512]{2,1,0:T(8,128)}, u32[]{:S(2)}) copy-start(f32[2,8,512]{2,1,0:T(8,128)} %copy-done.23) | copy-start | bytes 98308 | tf_op jit(solution)/shard_map/while
  1410.6 25.6 %copy-start.45 = (s32[2]{0:T(128)S(1)}, s32[2]{0:T(128)}, u32[]{:S(2)}) copy-start(s32[2]{0:T(128)} %copy-done.44) | copy-start | bytes 28 | tf_op jit(solution)/shard_map/while
  1436.2 30.1 %copy-start.23 = (f32[2,8,512]{2,1,0:T(8,128)}, f32[2,8,512]{2,1,0:T(8,128)S(1)}, u32[]{:S(2)}) copy-start(f32[2,8,512]{2,1,0:T(8,128)S(1)} %get-tuple-element.460) | copy-start | bytes 98308 | tf_op jit(solution)/shard_map/while
  1436.2 30.1 %copy-start.44 = (s32[2]{0:T(128)}, s32[2]{0:T(128)S(1)}, u32[]{:S(2)}) copy-start(s32[2]{0:T(128)S(1)} %get-tuple-element.457) | copy-start | bytes 28 | tf_op jit(solution)/shard_map/while
  1598.4 17.4 copy-start.5
  1636.6 25.6 %copy-start.24 = (f32[2,8,512]{2,1,0:T(8,128)S(1)}, f32[2,8,512]{2,1,0:T(8,128)}, u32[]{:S(2)}) copy-start(f32[2,8,512]{2,1,0:T(8,128)} %copy-done.23) | copy-start | bytes 98308 | tf_op jit(solution)/shard_map/while
  1636.6 25.6 %copy-start.45 = (s32[2]{0:T(128)S(1)}, s32[2]{0:T(128)}, u32[]{:S(2)}) copy-start(s32[2]{0:T(128)} %copy-done.44) | copy-start | bytes 28 | tf_op jit(solution)/shard_map/while
  1669.4 125.7 %reduce-scatter.27.cloned.1.call-start = ((), (), s32[]{:S(2)}) async-start(), calls=%async_computation.31 | async-start | bytes 6553600 | tf_op jit(solution)/shard_map/reduce_scatter | solution.py:254
  1676.9 270.4 %all-gather.29.cloned.1.call-start = ((), (), s32[]{:S(2)}) async-start(), calls=%async_computation.32 | async-start | bytes 19660800 | tf_op jit(solution)/shard_map/all_gather | solution.py:51
  1798.5 148.8 %copy-start.15 = (bf16[320,1920]{1,0:T(8,128)(2,1)S(1)}, bf16[320,1920]{1,0:T(8,128)(2,1)}, u32[]{:S(2)}) copy-start(bf16[320,1920]{1,0:T(8,128)(2,1)} %copy-done.14) | copy-start | bytes 3686404
  1798.5 211.8 %all-gather.21.cloned.1.call-start = ((), (), s32[]{:S(2)}) async-start(), calls=%async_computation.22 | async-start | bytes 6553600 | tf_op jit(solution)/shard_map/all_gather | solution.py:51
  1799.1 251.4 %reduce-scatter.29.cloned.1.call-start = ((), (), s32[]{:S(2)}) async-start(), calls=%async_computation.33 | async-start | bytes 3932160 | tf_op jit(solution)/shard_map/reduce_scatter | solution.py:85
  1959.8 50.5 %copy-start.22 = (bf16[640,320]{0,1:T(8,128)(2,1)S(1)}, bf16[640,320]{0,1:T(8,128)(2,1)}, u32[]{:S(2)}) copy-start(bf16[640,320]{0,1:T(8,128)(2,1)} %param.28) | copy-start | bytes 1228804
  1959.8 102.4 %reduce-scatter.17.cloned.1.call-start = ((), (), s32[]{:S(2)}) async-start(), calls=%async_computation.23 | async-start | bytes 3932160 | tf_op jit(solution)/shard_map/reduce_scatter | solution.py:85
  2016.5 132.8 %all-reduce.4.cloned.1.call-start = ((), (), s32[]{:S(2)}) async-start(), calls=%async_computation.34 | async-start | bytes 4915200 | tf_op jit(solution)/shard_map/psum | solution.py:287
  2016.8 12.8 slice-start.1
  2032.6 17.9 copy-start.4
  2032.6 17.9 copy-start.28
  2032.6 17.9 copy-start.34
  2050.4 11.8 copy-start.32
  2050.4 11.8 copy-start.38
  2068.3 19.2 all-to-all-start.1
  2074.2 17.7 copy-start.7
  2087.5 113.6 %all-to-all-start.3 = ((bf16[512,4,320]{0,2,1:T(8,128)(2,1)}), bf16[512,4,320]{0,2,1:T(8,128)(2,1)}, u32[]{:S(2)}, u32[]{:S(2)}) async-start(bf16[512,4,320]{0,2,1:T(8,128)(2,1)} %bitcast.196), calls=%async_computation.13 | async-start | bytes 2621440 | tf_op jit(solution)/shard_map/all_to_all | solution.py:24
  2154.3 43.9 %copy-start.43 = (f32[80]{0:T(128)S(1)}, f32[80]{0:T(128)}, u32[]{:S(2)}) copy-start(f32[80]{0:T(128)} %param.20) | copy-start | bytes 964
  (29 other events, 123.1 us)
Sparse Core Ops, SparseCore 0:
  46.0 11.5 all-gather.10
  74.5 273.8 reduce-scatter.10
  353.9 61.2 all-gather.14
  417.0 61.2 all-gather.12
  649.9 61.2 all-gather.16
  717.5 10.3 reduce-scatter.12
  741.5 10.7 all-gather.22
  755.4 11.3 all-gather.18
  769.8 104.6 reduce-scatter.18
  877.5 103.4 reduce-scatter.14
  987.0 61.3 all-gather.24
  1054.7 10.3 reduce-scatter.20
  1083.2 10.4 all-gather.26
  1102.8 104.6 reduce-scatter.22
  1669.6 61.2 reduce-scatter.24
  1733.7 61.3 reduce-scatter.26
  1798.7 148.5 all-gather.28
  1949.0 61.2 all-gather.20
  2012.5 10.3 reduce-scatter.28
  2025.0 11.5 reduce-scatter.16
  2050.6 98.7 all-reduce.3
where the time goes:
time: 2220 us; the launch traced here: 2210 us
  waiting for transfers between devices  1230 us (55%)
  matrix products  499 us (22%)
  other arithmetic  223 us (10%)
  local copies, waits for them, and re-layouts  119 us (5%)
  blocking collectives  118 us (5%)
    reduce_scatter x4, waiting for transfers between devices, sum_over_y(): lax.psum_scatter(product_term(left, right, contract)(jnp.int32(0), lax.ax...  584 us
    all_gather x4, waiting for transfers between devices, group_tokens(): return lax.all_gather(values, 'gy', axis=0, tiled=True)  321 us
    dot_general x4, matrix products, block_scores(): jnp.einsum('qhd,khd->hqk', rows, keys, preferred_element_type=jnp.float32)  107 us
    convert_element_type x2, other arithmetic, one_block(): score_low = (weights * (along - centre)).astype(jnp.bfloat16)  105 us
    dot_general x2, matrix products, one_block(): jnp.einsum('qhd,khd->hqk', grads, values, preferred_element_type=jnp.floa...  95 us
    dot_general x8, matrix products, multiply(): lax.dot_general(left, right, (((1,), (contract,)), ((), ())), preferred_e...  75.4 us
    reduce_scatter x1, waiting for transfers between devices, per_device(): lax.psum_scatter(value_full.astype(jnp.bfloat16), 'gy', scatter_dimension...  64.2 us
    dot_general x2, matrix products, one_block(): jnp.einsum('hqk,qhd->khd', weights.astype(jnp.bfloat16), grads, preferred...  60.1 us
  transfers between devices with their start and end apart: 23, of which 18 were waited for; matrix products, arithmetic and copies ran while one was open for 6% of the time, Pallas kernels for 0%

commit v1 on v0

v1 whole, which is shorter than its diff:
```python
import functools
import math

import jax
import jax.numpy as jnp
from jax import lax
from jax.experimental import pallas as pl
from jax.experimental.pallas import tpu as pltpu
from jax.sharding import PartitionSpec as P

DH = 80
softplus_unit = 1.442695041
NN = (((1,), (0,)), ((), ()))
NT = (((1,), (1,)), ((), ()))
TN = (((0,), (0,)), ((), ()))


def dot(left, right, how):
    return lax.dot_general(left, right, how, preferred_element_type=jnp.float32)


def visible(scores, i, j, bq, bk, prefix):
    key = j * bk + lax.broadcasted_iota(jnp.int32, scores.shape, 0)
    query = i * bq + lax.broadcasted_iota(jnp.int32, scores.shape, 1)
    return jnp.where((key <= query) | (key < prefix), scores, -1e30)


def block_range(i, bq, bk, prefix):
    whole = jnp.maximum((i * bq + 1) // bk, prefix // bk)
    seen = jnp.maximum(((i + 1) * bq + bk - 1) // bk, (prefix + bk - 1) // bk)
    return whole, seen


def forward_kernel(bq, bk, heads, prefix_ref, q_t, k, v_t, o_t, lse):
    i = pl.program_id(0)
    prefix = prefix_ref[0]
    whole, seen = block_range(i, bq, bk, prefix)

    def step(masked, j, carry):
        out = []
        rows = pl.ds(pl.multiple_of(j * bk, bk), bk)
        scores = [dot(k[h, rows, :], q_t[h], NN) for h in range(heads)]
        for h in range(heads):
            largest, total, mixed = carry[h]
            s = visible(scores[h], i, j, bq, bk, prefix) if masked else scores[h]
            now = jnp.maximum(largest, jnp.max(s, axis=0, keepdims=True))
            raised = jnp.exp(s - now)
            shrink = jnp.exp(largest - now)
            total = total * shrink + jnp.sum(raised, axis=0, keepdims=True)
            mixed = mixed * shrink + dot(v_t[h, :, rows], raised.astype(jnp.bfloat16), NN)
            out.append((now, total, mixed))
        return tuple(out)

    start = tuple(
        (
            jnp.full((1, bq), -1e30, jnp.float32),
            jnp.zeros((1, bq), jnp.float32),
            jnp.zeros((DH, bq), jnp.float32),
        )
        for _ in range(heads)
    )
    done = lax.fori_loop(0, whole, functools.partial(step, False), start)
    done = lax.fori_loop(whole, seen, functools.partial(step, True), done)
    for h in range(heads):
        largest, total, mixed = done[h]
        o_t[h] = mixed / total
        lse[h] = largest + jnp.log(total)


def attention_forward(q_t, k, v_t, prefix):
    heads, _, length = q_t.shape
    bq = bk = min(512, length)
    columns = lambda n: pl.BlockSpec((heads, n, bq), lambda i, p: (0, 0, i))
    whole = lambda a: pl.BlockSpec(a.shape, lambda i, p: (0, 0, 0))
    return pl.pallas_call(
        functools.partial(forward_kernel, bq, bk, heads),
        grid_spec=pltpu.PrefetchScalarGridSpec(
            num_scalar_prefetch=1,
            grid=(length // bq,),
            in_specs=[columns(DH), whole(k), whole(v_t)],
            out_specs=[columns(DH), columns(1)],
        ),
        out_shape=[
            jax.ShapeDtypeStruct((heads, DH, length), jnp.float32),
            jax.ShapeDtypeStruct((heads, 1, length), jnp.float32),
        ],
        cost_estimate=pl.CostEstimate(
            flops=heads * length * length * 256 * 2,
            transcendentals=heads * length * length // 2,
            bytes_accessed=heads * length * DH * 12,
        ),
        name="attention_forward",
    )(prefix, q_t, k, v_t)


def backward_kernel(
    bq, bk, heads, count, prefix_ref, q_t, k, k_t, v, g_t, o_t, lse, dq_t, dk, dv, dk_sum, dv_sum
):
    i = pl.program_id(0)
    prefix = prefix_ref[0]
    whole, seen = block_range(i, bq, bk, prefix)

    @pl.when(i == 0)
    def _():
        dk_sum[...] = jnp.zeros_like(dk_sum)
        dv_sum[...] = jnp.zeros_like(dv_sum)

    centre = [
        jnp.sum(g_t[h].astype(jnp.float32) * o_t[h], axis=0, keepdims=True) for h in range(heads)
    ]

    def step(masked, j, carry):
        rows = pl.ds(pl.multiple_of(j * bk, bk), bk)
        out = []
        scores = [dot(k[h, rows, :], q_t[h], NN) for h in range(heads)]
        along = [dot(v[h, rows, :], g_t[h], NN) for h in range(heads)]
        for h in range(heads):
            s = visible(scores[h], i, j, bq, bk, prefix) if masked else scores[h]
            weights = jnp.exp(s - lse[h])
            low = (weights * (along[h] - centre[h])).astype(jnp.bfloat16)
            dv_sum[h, rows, :] += dot(weights.astype(jnp.bfloat16), g_t[h], NT)
            dk_sum[h, rows, :] += dot(low, q_t[h], NT)
            out.append(carry[h] + dot(k_t[h, :, rows], low, NN))
        return tuple(out)

    done = tuple(jnp.zeros((DH, bq), jnp.float32) for _ in range(heads))
    done = lax.fori_loop(0, whole, functools.partial(step, False), done)
    done = lax.fori_loop(whole, seen, functools.partial(step, True), done)
    for h in range(heads):
        dq_t[h] = done[h]

    @pl.when(i == count - 1)
    def _():
        dk[...] = dk_sum[...].astype(jnp.bfloat16)
        dv[...] = dv_sum[...].astype(jnp.bfloat16)


def attention_backward(q_t, k, k_t, v, g_t, o_t, lse, prefix):
    heads, _, length = q_t.shape
    bq = bk = min(512, length)
    columns = lambda n: pl.BlockSpec((heads, n, bq), lambda i, p: (0, 0, i))
    whole = lambda a: pl.BlockSpec(a.shape, lambda i, p: (0, 0, 0))
    return pl.pallas_call(
        functools.partial(backward_kernel, bq, bk, heads, length // bq),
        grid_spec=pltpu.PrefetchScalarGridSpec(
            num_scalar_prefetch=1,
            grid=(length // bq,),
            in_specs=[
                columns(DH), whole(k), whole(k_t), whole(v), columns(DH), columns(DH), columns(1)
            ],
            out_specs=[columns(DH), whole(k), whole(k)],
            scratch_shapes=[pltpu.VMEM(k.shape, jnp.float32)] * 2,
        ),
        out_shape=[
            jax.ShapeDtypeStruct(q_t.shape, jnp.float32),
            jax.ShapeDtypeStruct(k.shape, jnp.bfloat16),
            jax.ShapeDtypeStruct(k.shape, jnp.bfloat16),
        ],
        cost_estimate=pl.CostEstimate(
            flops=heads * length * length * 256 * 5,
            transcendentals=heads * length * length // 2,
            bytes_accessed=heads * length * DH * 24,
        ),
        name="attention_backward",
    )(prefix, q_t, k, k_t, v, g_t, o_t, lse)


def normalize(values, gain):
    inverse = lax.rsqrt(jnp.mean(values * values, axis=-1, keepdims=True) + 1e-06)
    unit = values * inverse
    return unit, inverse, (unit * gain).astype(jnp.bfloat16)


def normalize_back(upstream, unit, inverse, gain):
    scaled = upstream * gain
    mean = jnp.mean(scaled * unit, axis=-1, keepdims=True)
    return inverse * (scaled - unit * mean), jnp.sum(upstream * unit, axis=0)


def per_device(
    layer_input,
    first_gain,
    query_scale,
    query_weight,
    key_weight,
    value_weight,
    output_weight,
    second_gain,
    inner_weight,
    inner_bias,
    outer_weight,
    outer_bias,
    prefix_len,
    output_cotangent,
):
    gx, gy = lax.axis_size("gx"), lax.axis_size("gy")
    both = ("gx", "gy")
    rows, width = layer_input.shape
    group = rows * gx * gy
    all_heads = query_weight.shape[1] * gx // DH
    split = all_heads % (gx * gy) == 0
    heads = all_heads // (gx * gy if split else gy)
    assert prefix_len.shape[0] == lax.axis_size("dp")
    assert heads * (gx * gy if split else gy) == all_heads
    x_index, y_index = lax.axis_index("gx"), lax.axis_index("gy")
    prefix = lax.dynamic_slice_in_dim(prefix_len, lax.axis_index("dp"), 1, 0)

    def to_heads(columns):
        if split:
            return lax.all_to_all(columns, both, split_axis=0, concat_axis=1, tiled=True)
        half = lax.all_to_all(columns, "gy", split_axis=0, concat_axis=1, tiled=True)
        return lax.all_gather(half, "gx", axis=1, tiled=True)

    def to_tokens(columns):
        if split:
            return lax.all_to_all(columns, both, split_axis=1, concat_axis=0, tiled=True)
        half = lax.dynamic_slice_in_dim(columns, x_index * (group // gx), group // gx, 1)
        return lax.all_to_all(half, "gy", split_axis=1, concat_axis=0, tiled=True)

    def weight_to_heads(stack):
        if not split:
            stack = lax.all_gather(stack, "gx", axis=2, tiled=True)
        return lax.all_to_all(stack, "gy", split_axis=2, concat_axis=1, tiled=True)

    def weight_from_heads(stack):
        stack = lax.all_to_all(stack, "gy", split_axis=1, concat_axis=2, tiled=True)
        if not split:
            own = stack.shape[2] // gx
            stack = lax.dynamic_slice_in_dim(stack, x_index * own, own, 2)
        return stack

    everyone = lax.all_gather(lax.all_gather(layer_input, "gy", axis=0, tiled=True), "gx", axis=0, tiled=True)
    own_weights = weight_to_heads(jnp.stack([query_weight, key_weight, value_weight]))
    gains = lax.all_gather(jnp.stack([first_gain, second_gain, outer_bias]), "gy", axis=1, tiled=True)
    inner_bias_all = lax.all_gather(inner_bias, "gx", axis=0, tiled=True)
    first_gain_all, second_gain_all, outer_bias_all = gains[0], gains[1], gains[2]

    late = jnp.stack([output_weight.T, inner_weight, outer_weight.T])
    late = lax.all_gather(lax.all_gather(late, "gy", axis=1, tiled=True), "gx", axis=2, tiled=True)
    output_all, inner_all, outer_all = late[0], late[1], late[2]

    _, _, normed_one = normalize(everyone.astype(jnp.float32), first_gain_all)
    factor = jax.nn.softplus(query_scale) * (softplus_unit / math.sqrt(DH))
    own = heads * DH
    wq, wk, wv = own_weights[0], own_weights[1], own_weights[2]
    turned = dot(jnp.concatenate([wq, wk, wv], axis=1), normed_one, (((0,), (1,)), ((), ())))
    queries_t = turned[:own].reshape(heads, DH, group)
    k_t = turned[own : 2 * own].reshape(heads, DH, group).astype(jnp.bfloat16)
    v_t = turned[2 * own :].reshape(heads, DH, group).astype(jnp.bfloat16)
    q_t = (queries_t * factor[None, :, None]).astype(jnp.bfloat16)
    k = jnp.swapaxes(k_t, 1, 2)
    v = jnp.swapaxes(v_t, 1, 2)
    o_t, lse = attention_forward(q_t, k, v_t, prefix)
    attended = to_tokens(o_t.reshape(own, group).astype(jnp.bfloat16))

    inputs = layer_input.astype(jnp.float32)
    middle = inputs + dot(attended, output_all, (((0,), (1,)), ((), ())))
    unit_two, inverse_two, normed_two = normalize(middle, second_gain_all)
    before = dot(normed_two, inner_all, NN) + inner_bias_all
    sigmoid = jax.nn.sigmoid(before)
    hidden = (before * sigmoid).astype(jnp.bfloat16)
    layer_output = (middle + dot(hidden, outer_all, NT) + outer_bias_all).astype(jnp.bfloat16)

    upstream = output_cotangent.astype(jnp.float32)
    hidden_gradient = dot(output_cotangent, outer_all, NN)
    before_gradient = hidden_gradient * sigmoid * (1.0 + before * (1.0 - sigmoid))
    before_low = before_gradient.astype(jnp.bfloat16)
    middle_part, second_gain_part = normalize_back(
        dot(before_low, inner_all, NT), unit_two, inverse_two, second_gain_all
    )
    middle_gradient = upstream + middle_part
    branch_low = middle_gradient.astype(jnp.bfloat16)
    g_t = to_heads(dot(output_all, branch_low, (((0,), (1,)), ((), ()))).astype(jnp.bfloat16))

    late_gradient = jnp.stack(
        [
            dot(branch_low, attended, (((0,), (1,)), ((), ()))).astype(jnp.bfloat16),
            dot(normed_two, before_low, TN).astype(jnp.bfloat16),
            dot(output_cotangent, hidden, TN).astype(jnp.bfloat16),
        ]
    )
    late_gradient = lax.psum_scatter(late_gradient, "gx", scatter_dimension=2, tiled=True)
    late_gradient = lax.psum_scatter(late_gradient, "gy", scatter_dimension=1, tiled=True)
    late_gradient = lax.psum(late_gradient, "dp").astype(jnp.float32)

    dq_t, dk, dv = attention_backward(
        q_t, k, k_t, v, g_t.reshape(heads, DH, group), o_t, lse, prefix
    )
    scale_part = jnp.sum(dq_t * queries_t, axis=(0, 2))
    if not split:
        scale_part = scale_part / gx
    joined = jnp.concatenate(
        [
            (dq_t * factor[None, :, None]).astype(jnp.bfloat16).reshape(own, group),
            jnp.swapaxes(dk, 1, 2).reshape(own, group),
            jnp.swapaxes(dv, 1, 2).reshape(own, group),
        ],
        axis=0,
    )
    back = dot(joined, jnp.concatenate([wq, wk, wv], axis=1), (((0,), (1,)), ((), ())))
    back = back.astype(jnp.bfloat16)
    if split:
        back = lax.psum_scatter(back, "gx", scatter_dimension=0, tiled=True)
    else:
        back = lax.dynamic_slice_in_dim(back, x_index * (group // gx), group // gx, 0)
    back = lax.psum_scatter(back, "gy", scatter_dimension=0, tiled=True).astype(jnp.float32)
    early_gradient = dot(normed_one, joined, (((0,), (1,)), ((), ()))).astype(jnp.bfloat16)
    early_gradient = jnp.stack(
        [early_gradient[:, :own], early_gradient[:, own : 2 * own], early_gradient[:, 2 * own :]]
    )
    early_gradient = lax.psum(weight_from_heads(early_gradient), "dp").astype(jnp.float32)

    unit_one, inverse_one, _ = normalize(inputs, first_gain_all)
    input_part, first_gain_part = normalize_back(back, unit_one, inverse_one, first_gain_all)
    input_gradient = (middle_gradient + input_part).astype(jnp.bfloat16)

    small = lax.psum(
        (
            first_gain_part,
            second_gain_part,
            jnp.sum(upstream, axis=0),
            jnp.sum(before_gradient, axis=0),
            scale_part,
        ),
        ("dp", "gx", "gy"),
    )
    gain_width, bias_width = first_gain.shape[0], inner_bias.shape[0]
    at_y = lambda a: lax.dynamic_slice_in_dim(a, y_index * gain_width, gain_width, 0)
    return (
        layer_output,
        input_gradient,
        at_y(small[0]),
        small[4] * (softplus_unit / math.sqrt(DH)) * jax.nn.sigmoid(query_scale),
        early_gradient[0],
        early_gradient[1],
        early_gradient[2],
        late_gradient[0].T,
        at_y(small[1]),
        late_gradient[1],
        lax.dynamic_slice_in_dim(small[3], x_index * bias_width, bias_width, 0),
        late_gradient[2].T,
        at_y(small[2]),
    )


def solution(mesh):
    placed = (
        P(("dp", "gx", "gy"), None),
        P("gy"),
        P(),
        P("gy", "gx"),
        P("gy", "gx"),
        P("gy", "gx"),
        P("gx", "gy"),
        P("gy"),
        P("gy", "gx"),
        P("gx"),
        P("gx", "gy"),
        P("gy"),
        P(),
        P(("dp", "gx", "gy"), None),
    )
    return jax.shard_map(
        per_device,
        mesh=mesh,
        in_specs=placed,
        out_specs=(
            P(("dp", "gx", "gy"), None),
            P(("dp", "gx", "gy"), None),
            P("gy"),
            P(),
            P("gy", "gx"),
            P("gy", "gx"),
            P("gy", "gx"),
            P("gx", "gy"),
            P("gy"),
            P("gy", "gx"),
            P("gx"),
            P("gx", "gy"),
            P("gy"),
        ),
        check_vma=False,
    )
```

time: 2220 us -> 803 us (0.36)
  waiting for transfers between devices: 1230 us -> 336 us
  matrix products: 499 us -> 70 us
  other arithmetic: 223 us -> 31.4 us
  Pallas kernels: 0 us -> 116 us
  blocking collectives: 118 us -> 90.1 us
    reduce_scatter x10 -> x3, waiting for transfers between devices: 710 us -> 54 us  [the longest x1 53.9 us: per_device(): lax.psum_scatter(back, 'gy', scatter_dimension=0, tiled=True)]
    dot_general x26 -> x12, matrix products: 499 us -> 70 us  [dot(): return lax.dot_general(left, right, how, preferred_element_type=jnp.float32)]
    all_gather x10 -> x4, waiting for transfers between devices: 449 us -> 124 us  [the longest x1 63.4 us: per_device(): lax.all_gather(layer_input, 'gy', axis=0, tiled=True)]
    convert_element_type x15 -> x5, other arithmetic: 143 us -> 8.51 us  [the longest x1 3.58 us: per_device(): input_gradient = (middle_gradient + input_part).astype(jnp.bfloat16)]
    pallas_call x0 -> x2, Pallas kernels: none -> 116 us  [the longest x1 69 us: attention_backward(): pl.pallas_call(functools.partial(backward_kernel, bq, bk, heads, length /...]
    unnamed x98 -> x79, local copies, waits for them, and re-layouts: 19.5 us -> 74.8 us
    dynamic_update_slice x8 -> x0, local copies, waits for them, and re-layouts: 52.1 us -> none  [the longest x4 51.1 us: attention_forward(): mixed, logsum = lax.map(one_block, (shaped, firsts))]
    reduce_sum x9 -> x5, other arithmetic: 60.2 us -> 14 us  [the longest x2 8.49 us: normalize(): jnp.mean(values * values, axis=-1, keepdims=True) + 1e-06]
  transfers between devices with their start and end apart: 23 -> 12, of which waited for: 18 -> 7; matrix products, arithmetic and copies ran while one was open for 6% -> 15% of each run, Pallas kernels for 0% -> 15%
where the time goes in v1:
time: 803 us; the launch traced here: 792 us
  waiting for transfers between devices  336 us (42%)
  local copies, waits for them, and re-layouts  121 us (15%)
  Pallas kernels  116 us (14%)
  blocking collectives  90.1 us (11%)
  matrix products  70 us (9%)
  other arithmetic  31.4 us (4%)
  between operations  14.9 us (2%)
  starting transfers between devices  12.9 us (2%)
    psum x1, waiting for transfers between devices, per_device(): lax.psum(weight_from_heads(early_gradient), 'dp').astype(jnp.float32)  96.3 us
    unnamed x79, local copies, waits for them, and re-layouts  74.8 us
    dot_general x12, matrix products, dot(): return lax.dot_general(left, right, how, preferred_element_type=jnp.float32)  70 us
    pallas_call x1, Pallas kernels, attention_backward(): pl.pallas_call(functools.partial(backward_kernel, bq, bk, heads, length /...  69 us
    all_gather x1, waiting for transfers between devices, per_device(): lax.all_gather(layer_input, 'gy', axis=0, tiled=True)  63.4 us
    all_gather x1, waiting for transfers between devices, per_device(): lax.all_gather(late, 'gy', axis=1, tiled=True)  60.9 us
    reduce_scatter x1, waiting for transfers between devices, per_device(): lax.psum_scatter(back, 'gy', scatter_dimension=0, tiled=True)  53.9 us
    pallas_call x1, Pallas kernels, attention_forward(): pl.pallas_call(functools.partial(forward_kernel, bq, bk, heads), grid_spe...  46.5 us
  transfers between devices with their start and end apart: 12, of which 7 were waited for; matrix products, arithmetic and copies ran while one was open for 15% of the time, Pallas kernels for 15%

profile of v1, /device:TPU:0, one launch (start us, length us, event | category | flops | bytes accessed | tf_op | source)
XLA Modules:
  0.0 792.2 jit_solution(13532235885187911628)
XLA Ops:
  8.0 2.4 pad_maximum_fusion.5
  10.5 63.4 %all-gather.7.cloned.1.call-done = bf16[2048,1280]{1,0:T(8,128)(2,1)} async-done(((bf16[512,1280]{1,0:T(8,128)(2,1)}), bf16[2048,1280]{1,0:T(8,128)(2,1)}) %all-gather.7.cloned.1.call-update) | async-done | bytes 5242896 | tf_op jit(solution)/shard_map/all_gather | solution.py:232
  74.0 60.9 %all-gather.11.cloned.1.call-done = bf16[3,1280,640]{2,1,0:T(8,128)(2,1)} async-done(((bf16[3,320,640]{2,1,0:T(8,128)(2,1)}), bf16[3,1280,640]{2,1,0:T(8,128)(2,1)}) %all-gather.11.cloned.1.call-update) | async-done | bytes 4915216 | tf_op jit(solution)/shard_map/all_gather | solution.py:239
  135.1 3.0 copy.72
  138.2 3.7 all-to-all-start
  142.0 26.7 %all-gather = f32[4,320,3]{1,2,0:T(4,128)S(1)} all-gather(f32[1,320,3]{1,2,0:T(4,128)S(1)} %maximum_bitcast_fusion), channel_id=1, replica_groups=mesh['dp'=4,'gx'=2,'gy'=4] {'gy'}, dimensions={0}, use_global_device_ids=true | all-gather | bytes 19200 | tf_op jit(solution)/shard_map/all_gather | solution.py:234
  172.6 8.2 %fusion = f32[4096]{0:T(1024)S(1)} fusion(bf16[4096,1280]{1,0:T(8,128)(2,1)} %all-gather.9.cloned.1.call-done), kind=kLoop, calls=%fused_computation.2 | loop fusion | flops 15724544 | bytes 10502144 | tf_op jit(solution)/shard_map/reduce_sum | solution.py:169
  182.3 7.6 fusion.37
  193.5 3.7 copy.78.k
  198.6 46.5 %attention_forward.1 = (f32[2,80,4096]{2,1,0:T(8,128)}, f32[2,1,4096]{2,1,0:T(1,128)}) custom-call(s32[1]{0:T(128)} %dynamic_slice.15.prefix_ref, bf16[2,80,4096]{2,1,0:T(8,128)(2,1)} %multiply_convert_fusion.3.q_t, bf16[2,4096,80]{2,1,0:T(8,128)(2,1)} %copy.78.k, bf16[2,80,4096]{2,1,0:T(8,128)(2,1)} %bitcast.128), custom_call_target="tpu_custom_call" | custom-call | flops 17179869184 | bytes 7864320 | tf_op jit(solution)/shard_map/attention_forward/pallas_call | solution.py:75
  249.0 4.3 all-to-all-start.1
  253.3 2.1 all-gather.1
  255.5 15.4 %all-to-all-done.1 = bf16[160,8,512]{2,0,1:T(8,128)(2,1)} async-done(((bf16[160,8,512]{2,0,1:T(8,128)(2,1)}), bf16[160,8,512]{2,0,1:T(8,128)(2,1)}, u32[]{:S(2)}, u32[]{:S(2)}) %all-to-all-start.1) | async-done | bytes 1310752 | tf_op jit(solution)/shard_map/all_to_all | solution.py:216
  270.8 4.9 multiply_reduce_fusion.3
  280.3 2.9 fusion.38
  283.2 2.0 fusion.4
  285.2 2.1 multiply_reduce_fusion
  288.2 14.8 %fusion.3 = bf16[1,1280,1280]{2,1,0:T(8,128)(2,1)S(1)} fusion(bf16[1280,512]{1,0:T(8,128)(2,1)} %bitcast.14, f32[512,1280]{1,0:T(8,128)S(1)} %get-tuple-element.90), kind=kOutput, calls=%fused_computation.10 | convolution fusion | flops 1680015360 | bytes 7208960 | tf_op jit(solution)/shard_map/dot_general | solution.py:19
  303.1 4.5 pad_maximum_fusion
  307.6 20.2 %copy.92 = bf16[3,1280,1280]{1,0,2:T(4,128)(2,1)} copy(bf16[3,1280,1280]{2,1,0:T(8,128)(2,1)} %pad_maximum_fusion) | data formatting | bytes 19660800
  327.7 12.2 %copy.95 = bf16[160,8,3,1280]{3,1,2,0:T(8,128)(2,1)} copy(bf16[160,8,3,1280]{3,2,1,0:T(4,128)(2,1)} %bitcast.117) | data formatting | bytes 19660800
  340.0 16.7 %reduce-scatter.13.cloned.1.call-done = bf16[640,3840]{1,0:T(8,128)(2,1)} async-done(((bf16[1280,3840]{1,0:T(8,128)(2,1)}), bf16[640,3840]{1,0:T(8,128)(2,1)}) %reduce-scatter.13.cloned.1.call-update) | async-done | bytes 4915216
  356.8 11.4 %reshape.105 = bf16[640,3,1280]{2,1,0:T(4,128)(2,1)} reshape(bf16[640,3840]{1,0:T(8,128)(2,1)} %reduce-scatter.13.cloned.1.call-done) | data formatting | bytes 9830400
  368.2 11.8 %copy.93 = bf16[3,1280,640]{2,1,0:T(8,128)(2,1)} copy(bf16[3,1280,640]{1,0,2:T(4,128)(2,1)} %bitcast.119) | data formatting | bytes 9830400
  380.0 5.7 convolution_convert_fusion.4
  385.7 4.4 all-to-all-start.2
  390.1 3.8 copy.80
  393.9 28.4 %all-to-all-done.2 = bf16[8,160,512]{2,1,0:T(8,128)(2,1)} async-done(((bf16[8,160,512]{2,1,0:T(8,128)(2,1)}), bf16[8,160,512]{2,1,0:T(8,128)(2,1)}, u32[]{:S(2)}, u32[]{:S(2)}) %all-to-all-start.2) | async-done | bytes 1310752 | tf_op jit(solution)/shard_map/all_to_all | solution.py:210
  422.3 3.1 copy.81
  425.4 3.3 reshape.96.g_t
  428.6 69.0 %attention_backward.1 = (f32[2,80,4096]{2,1,0:T(8,128)}, bf16[2,4096,80]{2,1,0:T(8,128)(2,1)}, bf16[2,4096,80]{2,1,0:T(8,128)(2,1)}) custom-call(s32[1]{0:T(128)} %dynamic_slice.15.prefix_ref, bf16[2,80,4096]{2,1,0:T(8,128)(2,1)} %multiply_convert_fusion.3.q_t, bf16[2,4096,80]{2,1,0:T(8,128)(2,1)} %copy.78.k, bf16[2,80,4096]{2,1,0:T(8,128)(2,1)} %bitcast.127, ...), custom_call_target="tpu_custom_call" | custom-call | flops 42949672960 | bytes 15728640 | tf_op jit(solution)/shard_map/attention_backward/pallas_call | solution.py:143
  497.6 3.8 copy.84
  501.4 3.8 copy.83
  505.3 2.4 multiply_reduce_fusion.1
  508.7 8.2 %convolution_convert_fusion = bf16[4096,1280]{1,0:T(8,128)(2,1)} fusion(bf16[1280,480]{0,1:T(8,128)(2,1)S(1)} %copy-done.16, bf16[160,4096]{1,0:T(8,128)(2,1)S(1)} %bitcast.135, bf16[160,4096]{1,0:T(8,128)(2,1)S(1)} %bitcast.137, bf16[160,4096]{1,0:T(8,128)(2,1)S(1)} %bitcast.140), kind=kOutput, calls=%fused_computation.5 | convolution fusion | flops 5050204160 | bytes 15646720 | tf_op jit(solution)/shard_map/dot_general | solution.py:19
  518.6 10.6 %fusion.18 = bf16[1280,480]{0,1:T(8,128)(2,1)S(1)} fusion(bf16[4096,1280]{1,0:T(8,128)(2,1)} %all-gather.9.cloned.1.call-done, f32[1280]{0:T(1024)S(1)} %copy-done.18, f32[4096]{0:T(1024)S(1)} %copy-done.20, bf16[160,4096]{1,0:T(8,128)(2,1)S(1)} %bitcast.136, bf16[160,4096]{1,0:T(8,128)(2,1)S(1)} %bitcast.138, bf16[160,4096]{1,0:T(8,128)(2,1)} %bitcast.141), kind=kOutput, calls=%fused_computation.37 | convolution fusion | flops 5066547200 | bytes 15668224 | tf_op jit(solution)/shard_map/dot_general | solution.py:19
  530.5 3.9 copy.85
  534.5 3.9 reshape.110
  538.3 21.4 %all_to_all.65 = bf16[4,2,76800]{2,1,0:T(2,128)(2,1)} all-to-all(bf16[4,2,76800]{2,1,0:T(2,128)(2,1)} %reshape.110), channel_id=1, replica_groups=mesh['dp'=4,'gx'=2,'gy'=4] {'gy'}, dimensions={0} | all-to-all | bytes 2457600 | tf_op jit(solution)/shard_map/all_to_all | solution.py:226
  559.7 4.3 reshape.111
  564.0 3.7 copy.86
  569.4 7.3 fusion.17
  576.7 96.3 %all-reduce.4.cloned.1.call-done = (bf16[3,320,640]{1,2,0:T(8,128)(2,1)}, bf16[3,320,640]{2,1,0:T(8,128)(2,1)}) async-done(((bf16[3,320,640]{1,2,0:T(8,128)(2,1)}, bf16[3,320,640]{2,1,0:T(8,128)(2,1)}), (bf16[3,320,640]{1,2,0:T(8,128)(2,1)}, bf16[3,320,640]{2,1,0:T(8,128)(2,1)})) %all-reduce.4.cloned.1.call-update) | async-done | bytes 2457616 | tf_op jit(solution)/shard_map/psum | solution.py:311
  675.7 2.4 copy.88
  682.4 53.9 %reduce-scatter.9.cloned.1.call-done = bf16[512,1280]{1,0:T(8,128)(2,1)} async-done(((bf16[2048,1280]{1,0:T(8,128)(2,1)}), bf16[512,1280]{1,0:T(8,128)(2,1)}) %reduce-scatter.9.cloned.1.call-update) | async-done | bytes 1310736 | tf_op jit(solution)/shard_map/reduce_scatter | solution.py:306
  736.3 2.3 fusion.26
  738.7 39.9 %all-reduce = (f32[1280]{0:T(1024)S(1)}, f32[80]{0:T(128)S(1)}, f32[1280]{0:T(1024)S(1)}, f32[1280]{0:T(1024)S(1)}, f32[1280]{0:T(1024)S(1)}) all-reduce(f32[1280]{0:T(1024)S(1)} %get-tuple-element.64, f32[80]{0:T(128)S(1)} %get-tuple-element.81, ...), channel_id=1, replica_groups=mesh['dp'=4,'gx'=2,'gy'=4] {'dp','gx','gy'}, use_global_device_ids=true, to_apply=%region_8.9 | all-reduce | flops 5200 | bytes 41600 | tf_op jit(solution)/shard_map/psum | solution.py:317
  781.7 3.6 fusion.24
  (139 shorter events, 36.6 us)
Async XLA Ops:
  7.2 66.7 %all-gather.7.cloned.1.call-start = ((), (), s32[]{:S(2)}) async-start(), calls=%async_computation.8 | async-start | bytes 6553600 | tf_op jit(solution)/shard_map/all_gather | solution.py:232
  7.9 127.0 %all-gather.11.cloned.1.call-start = ((), (), s32[]{:S(2)}) async-start(), calls=%async_computation.10 | async-start | bytes 6144000 | tf_op jit(solution)/shard_map/all_gather | solution.py:239
  10.4 162.1 %all-gather.9.cloned.1.call-start = ((), (), s32[]{:S(2)}) async-start(), calls=%async_computation.9 | async-start | bytes 15728640 | tf_op jit(solution)/shard_map/all_gather | solution.py:232
  73.9 61.0 %copy-start.12 = (bf16[320,640]{1,0:T(8,128)(2,1)S(1)}, bf16[320,640]{1,0:T(8,128)(2,1)}, u32[]{:S(2)}) copy-start(bf16[320,640]{1,0:T(8,128)(2,1)} %param.19) | copy-start | bytes 1228804
  73.9 61.0 %copy-start.13 = (bf16[320,640]{1,0:T(8,128)(2,1)S(1)}, bf16[320,640]{1,0:T(8,128)(2,1)}, u32[]{:S(2)}) copy-start(bf16[320,640]{1,0:T(8,128)(2,1)} %param.18) | copy-start | bytes 1228804
  73.9 61.0 %copy-start.14 = (bf16[320,640]{1,0:T(8,128)(2,1)S(1)}, bf16[320,640]{1,0:T(8,128)(2,1)}, u32[]{:S(2)}) copy-start(bf16[320,640]{1,0:T(8,128)(2,1)} %param.17) | copy-start | bytes 1228804
  73.9 181.5 %all-gather.13.cloned.1.call-start = ((), (), s32[]{:S(2)}) async-start(), calls=%async_computation.11 | async-start | bytes 14745600 | tf_op jit(solution)/shard_map/all_gather | solution.py:239
  138.1 3.8 copy-start.24
  138.1 3.8 copy-start.25
  138.1 3.8 copy-start.26
  138.1 30.7 %copy-start.28 = (s32[4]{0:T(128)S(1)}, s32[4]{0:T(128)}, u32[]{:S(2)}) copy-start(s32[4]{0:T(128)} %param.26) | copy-start | bytes 52
  138.1 31.9 %copy-start.29 = (f32[80]{0:T(128)S(1)}, f32[80]{0:T(128)}, u32[]{:S(2)}) copy-start(f32[80]{0:T(128)} %param.16) | copy-start | bytes 964
  138.2 31.9 %all-to-all-start = ((bf16[3,320,640]{1,0,2:T(4,128)(2,1)}), bf16[3,320,640]{1,0,2:T(4,128)(2,1)S(1)}, u32[]{:S(2)}, u32[]{:S(2)}) async-start(bf16[3,320,640]{1,0,2:T(4,128)(2,1)} %copy.72), calls=%async_computation | async-start | bytes 3932160 | tf_op jit(solution)/shard_map/all_to_all | solution.py:223
  170.1 10.7 %copy-start.17 = (f32[1280]{0:T(1024)}, f32[1280]{0:T(1024)S(1)}, u32[]{:S(2)}) copy-start(f32[1280]{0:T(1024)S(1)} %get-tuple-element.68) | copy-start | bytes 15364
  172.5 8.2 %copy-start.15 = (bf16[1280,480]{0,1:T(8,128)(2,1)}, bf16[1280,480]{0,1:T(8,128)(2,1)S(1)}, u32[]{:S(2)}) copy-start(bf16[1280,480]{0,1:T(8,128)(2,1)S(1)} %constant_dynamic-update-slice_fusion) | copy-start | bytes 3686404
  172.6 9.7 %copy-start.1 = (bf16[4096,1280]{1,0:T(8,128)(2,1)S(1)}, bf16[4096,1280]{1,0:T(8,128)(2,1)}, u32[]{:S(2)}) copy-start(bf16[4096,1280]{1,0:T(8,128)(2,1)} %all-gather.9.cloned.1.call-done) | copy-start | bytes 31457284
  180.8 9.1 %copy-start.19 = (f32[4096]{0:T(1024)}, f32[4096]{0:T(1024)S(1)}, u32[]{:S(2)}) copy-start(f32[4096]{0:T(1024)S(1)} %add_rsqrt_fusion) | copy-start | bytes 49156
  247.5 5.8 copy-start.23
  249.0 21.9 %all-to-all-start.1 = ((bf16[160,8,512]{2,0,1:T(8,128)(2,1)}), bf16[160,8,512]{2,0,1:T(8,128)(2,1)}, u32[]{:S(2)}, u32[]{:S(2)}) async-start(bf16[160,8,512]{2,0,1:T(8,128)(2,1)} %copy.79), calls=%async_computation.1 | async-start | bytes 2621440 | tf_op jit(solution)/shard_map/all_to_all | solution.py:216
  253.2 103.5 %reduce-scatter.13.cloned.1.call-start = ((), (), s32[]{:S(2)}) async-start(), calls=%async_computation.15 | async-start | bytes 14745600
  270.8 5.6 copy-start.27
  275.7 11.6 %copy-start.4 = (f32[512,1280]{1,0:T(8,128)}, f32[512,1280]{1,0:T(8,128)S(1)}, u32[]{:S(2)}) copy-start(f32[512,1280]{1,0:T(8,128)S(1)} %get-tuple-element.97) | copy-start | bytes 7864324
  276.4 1.9 copy-start.10
  278.3 2.0 copy-start.31
  288.2 14.8 %copy-start.2 = (f32[512,1280]{1,0:T(8,128)}, f32[512,1280]{1,0:T(8,128)S(1)}, u32[]{:S(2)}) copy-start(f32[512,1280]{1,0:T(8,128)S(1)} %get-tuple-element.90) | copy-start | bytes 7864324
  340.0 227.7 %reduce-scatter.11.cloned.1.call-start = ((), (), s32[]{:S(2)}) async-start(), calls=%async_computation.14 | async-start | bytes 6144000 | tf_op jit(solution)/shard_map/reduce_scatter | solution.py:283
  385.7 36.5 %all-to-all-start.2 = ((bf16[8,160,512]{2,1,0:T(8,128)(2,1)}), bf16[8,160,512]{2,1,0:T(8,128)(2,1)}, u32[]{:S(2)}, u32[]{:S(2)}) async-start(bf16[8,160,512]{2,1,0:T(8,128)(2,1)} %bitcast.139), calls=%async_computation.2 | async-start | bytes 2621440 | tf_op jit(solution)/shard_map/all_to_all | solution.py:210
  390.1 177.7 %reduce-scatter.7.cloned.1.call-start = ((), (), s32[]{:S(2)}) async-start(), calls=%async_computation.12 | async-start | bytes 15728640 | tf_op jit(solution)/shard_map/reduce_scatter | solution.py:303
  505.3 3.4 copy-start.5
  505.3 3.4 copy-start.7
  505.3 3.4 copy-start.16
  507.6 1.1 copy-start.9
  516.9 1.3 copy-start.6
  516.9 1.7 copy-start.8
  516.9 1.7 copy-start.18
  516.9 1.7 copy-start.20
  516.9 156.1 %all-reduce.4.cloned.1.call-start = ((), (), s32[]{:S(2)}) async-start(), calls=%async_computation.16 | async-start | bytes 5406720 | tf_op jit(solution)/shard_map/psum | solution.py:311
  567.7 168.6 %reduce-scatter.9.cloned.1.call-start = ((), (), s32[]{:S(2)}) async-start(), calls=%async_computation.13 | async-start | bytes 6553600 | tf_op jit(solution)/shard_map/reduce_scatter | solution.py:306
  567.8 1.3 copy-start
  567.8 1.7 copy-start.21
  679.3 1.4 copy-start.11
  680.8 57.8 %copy-start.22 = (f32[1280]{0:T(1024)S(1)}, f32[1280]{0:T(1024)}, u32[]{:S(2)}) copy-start(f32[1280]{0:T(1024)} %get-tuple-element.99) | copy-start | bytes 15364
  680.9 97.7 %copy-start.30 = (f32[80]{0:T(128)S(1)}, f32[80]{0:T(128)}, u32[]{:S(2)}) copy-start(f32[80]{0:T(128)} %param.16) | copy-start | bytes 964
  736.3 45.4 %copy-start.3 = (bf16[512,1280]{1,0:T(8,128)(2,1)S(1)}, bf16[512,1280]{1,0:T(8,128)(2,1)}, u32[]{:S(2)}) copy-start(bf16[512,1280]{1,0:T(8,128)(2,1)} %reduce-scatter.9.cloned.1.call-done) | copy-start | bytes 3932164
Sparse Core Ops, SparseCore 0:
  9.8 64.0 all-gather.6
  76.3 58.5 all-gather.10
  136.5 22.6 all-gather.8
  160.6 23.1 all-gather.12
  340.1 16.6 reduce-scatter.12
  380.1 73.9 reduce-scatter.10
  517.1 17.0 reduce-scatter.6
  567.8 105.1 all-reduce.3
  676.0 60.3 reduce-scatter.8

commit v2 on v1

--- a/solution.py
+++ b/solution.py
@@ -163,6 +163,44 @@
         ),
         name="attention_backward",
     )(prefix, q_t, k, k_t, v, g_t, o_t, lse)
+
+
+def late_gradient_kernel(left_a, right_a, left_b, right_b, left_c, right_c, out):
+    for n, (left, right) in enumerate(((left_a, right_a), (left_b, right_b), (left_c, right_c))):
+
+        @pl.when(pl.program_id(0) == n)
+        def _():
+            out[0, :, 0] = (
+                dot(left[...], right[...], TN).reshape(out.shape[1:2] + out.shape[3:]).astype(out.dtype)
+            )
+
+
+def late_gradients(pairs, gx, gy):
+    rows, wide = pairs[0][0].shape
+    tall, own = wide // gy, wide // gx
+    left = pl.BlockSpec((rows, wide), lambda w, x: (0, 0))
+    right = pl.BlockSpec((rows, own), lambda w, x: (0, x))
+    return pl.pallas_call(
+        late_gradient_kernel,
+        grid=(3, gx),
+        in_specs=[left, right] * 3,
+        out_specs=pl.BlockSpec((1, gy, 1, tall, own), lambda w, x: (x, 0, w, 0, 0)),
+        out_shape=jax.ShapeDtypeStruct((gx, gy, 3, tall, own), jnp.bfloat16),
+        cost_estimate=pl.CostEstimate(
+            flops=6 * rows * wide * wide,
+            transcendentals=0,
+            bytes_accessed=12 * rows * wide + 6 * wide * wide,
+        ),
+        name="late_gradients",
+    )(*[a for pair in pairs for a in pair])
+
+def into(left, blocks):
+    return jnp.concatenate([dot(left, b, NN) for b in blocks], axis=1)
+
+
+def out_of(left, blocks):
+    n = blocks.shape[2]
+    return sum(dot(left[:, i * n : (i + 1) * n], b, NT) for i, b in enumerate(blocks))
 
 
 def normalize(values, gain):
@@ -229,15 +267,18 @@
             stack = lax.dynamic_slice_in_dim(stack, x_index * own, own, 2)
         return stack
 
-    everyone = lax.all_gather(lax.all_gather(layer_input, "gy", axis=0, tiled=True), "gx", axis=0, tiled=True)
+    everyone = lax.all_gather(layer_input, both, axis=0, tiled=True)
     own_weights = weight_to_heads(jnp.stack([query_weight, key_weight, value_weight]))
     gains = lax.all_gather(jnp.stack([first_gain, second_gain, outer_bias]), "gy", axis=1, tiled=True)
     inner_bias_all = lax.all_gather(inner_bias, "gx", axis=0, tiled=True)
     first_gain_all, second_gain_all, outer_bias_all = gains[0], gains[1], gains[2]
 
-    late = jnp.stack([output_weight.T, inner_weight, outer_weight.T])
-    late = lax.all_gather(lax.all_gather(late, "gy", axis=1, tiled=True), "gx", axis=2, tiled=True)
-    output_all, inner_all, outer_all = late[0], late[1], late[2]
+    late = (output_weight.T, inner_weight, outer_weight.T)
+    late, everyone = lax.optimization_barrier((late, everyone))
+    output_all, inner_all, outer_all = (
+        lax.all_gather(w, both, axis=0, tiled=False).reshape(gx, gy * w.shape[0], w.shape[1])
+        for w in late
+    )
 
     _, _, normed_one = normalize(everyone.astype(jnp.float32), first_gain_all)
     factor = jax.nn.softplus(query_scale) * (softplus_unit / math.sqrt(DH))
@@ -254,34 +295,31 @@
     attended = to_tokens(o_t.reshape(own, group).astype(jnp.bfloat16))
 
     inputs = layer_input.astype(jnp.float32)
-    middle = inputs + dot(attended, output_all, (((0,), (1,)), ((), ())))
+    attended = attended.T
+    middle = inputs + out_of(attended, output_all)
     unit_two, inverse_two, normed_two = normalize(middle, second_gain_all)
-    before = dot(normed_two, inner_all, NN) + inner_bias_all
+    before = into(normed_two, inner_all) + inner_bias_all
     sigmoid = jax.nn.sigmoid(before)
     hidden = (before * sigmoid).astype(jnp.bfloat16)
-    layer_output = (middle + dot(hidden, outer_all, NT) + outer_bias_all).astype(jnp.bfloat16)
+    layer_output = (middle + out_of(hidden, outer_all) + outer_bias_all).astype(jnp.bfloat16)
 
     upstream = output_cotangent.astype(jnp.float32)
-    hidden_gradient = dot(output_cotangent, outer_all, NN)
+    hidden_gradient = into(output_cotangent, outer_all)
     before_gradient = hidden_gradient * sigmoid * (1.0 + before * (1.0 - sigmoid))
     before_low = before_gradient.astype(jnp.bfloat16)
     middle_part, second_gain_part = normalize_back(
-        dot(before_low, inner_all, NT), unit_two, inverse_two, second_gain_all
+        out_of(before_low, inner_all), unit_two, inverse_two, second_gain_all
     )
     middle_gradient = upstream + middle_part
     branch_low = middle_gradient.astype(jnp.bfloat16)
-    g_t = to_heads(dot(output_all, branch_low, (((0,), (1,)), ((), ()))).astype(jnp.bfloat16))
-
-    late_gradient = jnp.stack(
-        [
-            dot(branch_low, attended, (((0,), (1,)), ((), ()))).astype(jnp.bfloat16),
-            dot(normed_two, before_low, TN).astype(jnp.bfloat16),
-            dot(output_cotangent, hidden, TN).astype(jnp.bfloat16),
-        ]
-    )
-    late_gradient = lax.psum_scatter(late_gradient, "gx", scatter_dimension=2, tiled=True)
-    late_gradient = lax.psum_scatter(late_gradient, "gy", scatter_dimension=1, tiled=True)
-    late_gradient = lax.psum(late_gradient, "dp").astype(jnp.float32)
+    g_t = to_heads(into(branch_low, output_all).astype(jnp.bfloat16).T)
+
+    late_gradient = late_gradients(
+        ((branch_low, attended), (normed_two, before_low), (output_cotangent, hidden)), gx, gy
+    )
+    late_gradient = late_gradient.reshape((gx * gy,) + late_gradient.shape[2:])
+    late_gradient = lax.psum_scatter(late_gradient, both, scatter_dimension=0, tiled=False)
+    late_gradient = lax.psum(late_gradient, "dp")
 
     dq_t, dk, dv = attention_backward(
         q_t, k, k_t, v, g_t.reshape(heads, DH, group), o_t, lse, prefix
@@ -308,7 +346,10 @@
     early_gradient = jnp.stack(
         [early_gradient[:, :own], early_gradient[:, own : 2 * own], early_gradient[:, 2 * own :]]
     )
-    early_gradient = lax.psum(weight_from_heads(early_gradient), "dp").astype(jnp.float32)
+    early_gradient = weight_from_heads(early_gradient)
+    early_gradient, late_gradient = lax.optimization_barrier((early_gradient, late_gradient))
+    early_gradient = lax.psum(early_gradient, "dp").astype(jnp.float32)
+    late_gradient = late_gradient.astype(jnp.float32)
 
     unit_one, inverse_one, _ = normalize(inputs, first_gain_all)
     input_part, first_gain_part = normalize_back(back, unit_one, inverse_one, first_gain_all)

time: 803 us -> 651 us (0.81)
  waiting for transfers between devices: 336 us -> 230 us
  local copies, waits for them, and re-layouts: 121 us -> 72.1 us
  matrix products: 70 us -> 58.5 us
    all_gather x4, waiting for transfers between devices: 124 us -> 67.8 us  [the longest x1 67.8 us: per_device(): everyone = lax.all_gather(layer_input, both, axis=0, tiled=True)]
    unnamed x79 -> x69, local copies, waits for them, and re-layouts: 74.8 us -> 20.8 us
    psum x1 -> x2, waiting for transfers between devices: 96.3 us -> 60.6 us  [the longest x1 60.6 us: per_device(): early_gradient = lax.psum(early_gradient, 'dp').astype(jnp.float32)]
    reduce_scatter x1, waiting for transfers between devices: 0.02 us -> 18.9 us  [per_device(): back = lax.psum_scatter(back, 'gx', scatter_dimension=0, tiled=True)]
    unnamed x10 -> x9, waiting for transfers between devices: 18.2 us -> 1.48 us
    all_to_all x1, waiting for transfers between devices: 28.4 us -> 13.6 us  [to_heads(): lax.all_to_all(columns, both, split_axis=0, concat_axis=1, tiled=True)]
    pallas_call x0 -> x1, Pallas kernels: none -> 13.8 us  [late_gradients(): pl.pallas_call(late_gradient_kernel, grid=(3, gx), in_specs=[left, right]...]
    dot_general x12 -> x15, matrix products: 70 us -> 58.5 us  [dot(): return lax.dot_general(left, right, how, preferred_element_type=jnp.float32)]
  transfers between devices with their start and end apart: 12 -> 12, of which waited for: 7 -> 6; matrix products, arithmetic and copies ran while one was open for 15% -> 22% of each run, Pallas kernels for 15% -> 17%
where the time goes in v2:
time: 651 us; the launch traced here: 640 us
  waiting for transfers between devices  230 us (35%)
  Pallas kernels  122 us (19%)
  blocking collectives  95.6 us (15%)
  local copies, waits for them, and re-layouts  72.1 us (11%)
  matrix products  58.5 us (9%)
  other arithmetic  34.2 us (5%)
  between operations  14.7 us (2%)
  starting transfers between devices  12.5 us (2%)
    all_gather x1, waiting for transfers between devices, per_device(): everyone = lax.all_gather(layer_input, both, axis=0, tiled=True)  67.8 us
    pallas_call x1, Pallas kernels, attention_backward(): pl.pallas_call(functools.partial(backward_kernel, bq, bk, heads, length /...  65.1 us
    psum x1, waiting for transfers between devices, per_device(): early_gradient = lax.psum(early_gradient, 'dp').astype(jnp.float32)  60.6 us
    dot_general x15, matrix products, dot(): return lax.dot_general(left, right, how, preferred_element_type=jnp.float32)  58.5 us
    reduce_scatter x1, waiting for transfers between devices, per_device(): lax.psum_scatter(back, 'gy', scatter_dimension=0, tiled=True)  52.8 us
    pallas_call x1, Pallas kernels, attention_forward(): pl.pallas_call(functools.partial(forward_kernel, bq, bk, heads), grid_spe...  43.6 us
    psum x1, blocking collectives, per_device(): lax.psum((first_gain_part, second_gain_part, jnp.sum(upstream, axis=0), j...  39.8 us
    all_gather x1, blocking collectives, per_device(): lax.all_gather(jnp.stack([first_gain, second_gain, outer_bias]), 'gy', ax...  31.9 us
  transfers between devices with their start and end apart: 12, of which 6 were waited for; matrix products, arithmetic and copies ran while one was open for 22% of the time, Pallas kernels for 17%

profile of v2, /device:TPU:0, one launch (start us, length us, event | category | flops | bytes accessed | tf_op | source)
XLA Modules:
  0.0 640.5 jit_solution(17955543815136366885)
XLA Ops:
  8.0 67.8 %all-gather.10.cloned.1.call-done = bf16[4096,1280]{1,0:T(8,128)(2,1)} async-done(((bf16[512,1280]{1,0:T(8,128)(2,1)}), bf16[4096,1280]{1,0:T(8,128)(2,1)}) %all-gather.10.cloned.1.call-update) | async-done | bytes 10485776 | tf_op jit(solution)/shard_map/all_gather | solution.py:270
  77.9 3.1 copy.80
  81.0 3.8 all-to-all-start
  85.0 31.9 %all-gather.3 = f32[4,320,3]{1,2,0:T(4,128)S(1)} all-gather(f32[1,320,3]{1,2,0:T(4,128)S(1)} %maximum_bitcast_fusion.1), channel_id=1, replica_groups=mesh['dp'=4,'gx'=2,'gy'=4] {'gy'}, dimensions={0}, use_global_device_ids=true | all-gather | bytes 19200 | tf_op jit(solution)/shard_map/all_gather | solution.py:272
  120.7 6.7 %fusion = f32[4096]{0:T(1024)S(1)} fusion(bf16[4096,1280]{1,0:T(8,128)(2,1)} %all-gather.10.cloned.1.call-done), kind=kLoop, calls=%fused_computation.2 | loop fusion | flops 15724544 | bytes 10502144 | tf_op jit(solution)/shard_map/reduce_sum | solution.py:207
  127.4 8.4 %fusion.71 = (bf16[480,4096]{1,0:T(8,128)(2,1)S(1)}, f32[480,4096]{1,0:T(8,128)S(1)}) fusion(bf16[1280,480]{0,1:T(8,128)(2,1)S(1)} %constant_dynamic-update-slice_fusion, bf16[4096,1280]{1,0:T(8,128)(2,1)} %all-gather.10.cloned.1.call-done, f32[1280]{0:T(1024)S(1)} %get-tuple-element.80, f32[4096]{0:T(1024)S(1)} %add_rsqrt_fusion), kind=kOutput, calls=%fused_computation.108 | convolution fusion | flops 5056102400 | bytes 23532544 | tf_op jit(solution)/shard_map/dot_general | solution.py:19
  137.8 3.7 copy.86.k
  142.9 43.6 %attention_forward.1 = (f32[2,80,4096]{2,1,0:T(8,128)}, f32[2,1,4096]{2,1,0:T(1,128)}) custom-call(s32[1]{0:T(128)} %dynamic_slice.15.prefix_ref, bf16[2,80,4096]{2,1,0:T(8,128)(2,1)} %multiply_convert_fusion.3.q_t, bf16[2,4096,80]{2,1,0:T(8,128)(2,1)} %copy.86.k, bf16[2,80,4096]{2,1,0:T(8,128)(2,1)} %bitcast.94), custom_call_target="tpu_custom_call" | custom-call | flops 17179869184 | bytes 7864320 | tf_op jit(solution)/shard_map/attention_forward/pallas_call | solution.py:75
  190.4 3.6 all-to-all-start.1
  194.0 2.3 all-gather.4
  196.4 15.1 %all-to-all-done.1 = bf16[160,8,512]{2,0,1:T(8,128)(2,1)S(1)} async-done(((bf16[160,8,512]{2,0,1:T(8,128)(2,1)}), bf16[160,8,512]{2,0,1:T(8,128)(2,1)S(1)}, u32[]{:S(2)}, u32[]{:S(2)}) %all-to-all-start.1) | async-done | bytes 1310752 | tf_op jit(solution)/shard_map/all_to_all | solution.py:254
  213.2 3.4 fusion.41
  216.6 2.5 multiply_reduce_fusion.3
  220.6 4.2 fusion.31
  224.8 2.2 fusion.34
  227.0 3.2 fusion.48
  232.0 2.1 fusion.67
  236.9 1.9 fusion.66.left_a
  238.8 13.8 %late_gradients.1 = bf16[2,4,3,320,640]{4,3,2,1,0:T(8,128)(2,1)} custom-call(bf16[512,1280]{1,0:T(8,128)(2,1)} %fusion.66.left_a, bf16[512,1280]{1,0:T(8,128)(2,1)} %bitcast.102, bf16[512,1280]{1,0:T(8,128)(2,1)} %multiply_convert_fusion.2.left_b, bf16[512,1280]{1,0:T(8,128)(2,1)} %copy-done.8, bf16[512,1280]{1,0:T(8,128)(2,1)} %left_c.1, ...), custom_call_target="tpu_custom_call" | custom-call | flops 5033164800 | bytes 17694720 | tf_op jit(solution)/shard_map/late_gradients/pallas_call | solution.py:183
  252.7 3.2 fusion.54
  258.2 2.7 copy.92
  261.0 4.3 all-to-all-start.2
  265.4 4.0 copy.91
  269.4 13.6 %all-to-all-done.2 = bf16[8,160,512]{2,1,0:T(8,128)(2,1)} async-done(((bf16[8,160,512]{2,1,0:T(8,128)(2,1)}), bf16[8,160,512]{2,1,0:T(8,128)(2,1)}, u32[]{:S(2)}, u32[]{:S(2)}) %all-to-all-start.2) | async-done | bytes 1310752 | tf_op jit(solution)/shard_map/all_to_all | solution.py:248
  283.0 3.1 copy.93
  286.1 3.3 reshape.114.g_t
  289.4 65.1 %attention_backward.1 = (f32[2,80,4096]{2,1,0:T(8,128)}, bf16[2,4096,80]{2,1,0:T(8,128)(2,1)}, bf16[2,4096,80]{2,1,0:T(8,128)(2,1)}) custom-call(s32[1]{0:T(128)} %dynamic_slice.15.prefix_ref, bf16[2,80,4096]{2,1,0:T(8,128)(2,1)} %multiply_convert_fusion.3.q_t, bf16[2,4096,80]{2,1,0:T(8,128)(2,1)} %copy.86.k, bf16[2,80,4096]{2,1,0:T(8,128)(2,1)} %bitcast.93, ...), custom_call_target="tpu_custom_call" | custom-call | flops 42949672960 | bytes 15728640 | tf_op jit(solution)/shard_map/attention_backward/pallas_call | solution.py:143
  354.5 3.8 copy.96
  358.3 3.8 copy.95
  362.1 4.2 multiply_reduce_fusion.1
  366.3 10.1 %convolution_convert_fusion = bf16[4096,1280]{1,0:T(8,128)(2,1)} fusion(bf16[1280,480]{0,1:T(8,128)(2,1)} %copy-done.20, bf16[160,4096]{1,0:T(8,128)(2,1)} %bitcast.106, bf16[160,4096]{1,0:T(8,128)(2,1)} %bitcast.108, bf16[160,4096]{1,0:T(8,128)(2,1)} %bitcast.110), kind=kOutput, calls=%fused_computation.5 | convolution fusion | flops 5050204160 | bytes 15646720 | tf_op jit(solution)/shard_map/dot_general | solution.py:19
  376.7 10.8 %fusion.14 = bf16[1280,480]{0,1:T(8,128)(2,1)S(1)} fusion(bf16[4096,1280]{1,0:T(8,128)(2,1)} %all-gather.10.cloned.1.call-done, f32[1280]{0:T(1024)S(1)} %get-tuple-element.80, f32[4096]{0:T(1024)S(1)} %add_rsqrt_fusion, bf16[160,4096]{1,0:T(8,128)(2,1)} %bitcast.107, bf16[160,4096]{1,0:T(8,128)(2,1)} %bitcast.109, bf16[160,4096]{1,0:T(8,128)(2,1)} %bitcast.111), kind=kOutput, calls=%fused_computation.25 | convolution fusion | flops 5066547200 | bytes 15668224 | tf_op jit(solution)/shard_map/dot_general | solution.py:19
  388.8 4.9 copy.97
  393.7 5.4 reshape.142
  399.1 21.5 %all_to_all.65 = bf16[4,2,76800]{2,1,0:T(2,128)(2,1)} all-to-all(bf16[4,2,76800]{2,1,0:T(2,128)(2,1)} %reshape.142), channel_id=1, replica_groups=mesh['dp'=4,'gx'=2,'gy'=4] {'gy'}, dimensions={0} | all-to-all | bytes 2457600 | tf_op jit(solution)/shard_map/all_to_all | solution.py:264
  420.6 5.4 reshape.143
  426.0 5.3 copy.98
  431.7 18.9 %reduce-scatter.4.cloned.1.call-done = bf16[2048,1280]{1,0:T(8,128)(2,1)} async-done(((bf16[4096,1280]{1,0:T(8,128)(2,1)}), bf16[2048,1280]{1,0:T(8,128)(2,1)}) %reduce-scatter.4.cloned.1.call-update) | async-done | bytes 5242896 | tf_op jit(solution)/shard_map/reduce_scatter | solution.py:341
  452.3 3.0 fusion.27
  455.4 2.4 fusion.13
  459.4 60.6 %all-reduce.6.cloned.1.call-done = bf16[3,320,640]{1,2,0:T(8,128)(2,1)} async-done(((bf16[3,320,640]{1,2,0:T(8,128)(2,1)}), bf16[3,320,640]{1,2,0:T(8,128)(2,1)}) %all-reduce.6.cloned.1.call-update) | async-done | bytes 1228816 | tf_op jit(solution)/shard_map/psum | solution.py:351
  523.3 2.4 copy.99
  525.7 2.4 copy.100
  528.1 2.7 copy.101
  530.8 52.8 %reduce-scatter.6.cloned.1.call-done = bf16[512,1280]{1,0:T(8,128)(2,1)} async-done(((bf16[2048,1280]{1,0:T(8,128)(2,1)}), bf16[512,1280]{1,0:T(8,128)(2,1)}) %reduce-scatter.6.cloned.1.call-update) | async-done | bytes 1310736 | tf_op jit(solution)/shard_map/reduce_scatter | solution.py:344
  583.6 2.7 fusion.21
  586.4 4.3 convert_reduce_fusion
  590.7 39.8 %all-reduce = (f32[1280]{0:T(1024)S(1)}, f32[80]{0:T(128)S(1)}, f32[1280]{0:T(1024)S(1)}, f32[1280]{0:T(1024)S(1)}, f32[1280]{0:T(1024)S(1)}) all-reduce(f32[1280]{0:T(1024)S(1)} %get-tuple-element.76, f32[80]{0:T(128)S(1)} %get-tuple-element.94, ...), channel_id=1, replica_groups=mesh['dp'=4,'gx'=2,'gy'=4] {'dp','gx','gy'}, use_global_device_ids=true, to_apply=%region_8.9 | all-reduce | flops 5200 | bytes 41600 | tf_op jit(solution)/shard_map/psum | solution.py:358
  (136 shorter events, 35.7 us)
Async XLA Ops:
  7.2 68.6 %all-gather.10.cloned.1.call-start = ((), (), s32[]{:S(2)}) async-start(), calls=%async_computation.7 | async-start | bytes 11796480 | tf_op jit(solution)/shard_map/all_gather | solution.py:270
  7.9 204.2 %all-gather.12.cloned.1.call-start = ((), (), s32[]{:S(2)}) async-start(), calls=%async_computation.13 | async-start | bytes 3686400 | tf_op jit(solution)/shard_map/all_gather | solution.py:279
  75.8 144.8 %all-gather.14.cloned.1.call-start = ((), (), s32[]{:S(2)}) async-start(), calls=%async_computation.14 | async-start | bytes 3686400 | tf_op jit(solution)/shard_map/all_gather | solution.py:279
  81.0 3.9 copy-start.23
  81.0 3.9 copy-start.24
  81.0 3.9 copy-start.25
  81.0 36.0 %copy-start.26 = (s32[4]{0:T(128)S(1)}, s32[4]{0:T(128)}, u32[]{:S(2)}) copy-start(s32[4]{0:T(128)} %param.26) | copy-start | bytes 52
  81.0 37.2 %copy-start.27 = (f32[80]{0:T(128)S(1)}, f32[80]{0:T(128)}, u32[]{:S(2)}) copy-start(f32[80]{0:T(128)} %param.16) | copy-start | bytes 964
  81.0 37.2 %all-to-all-start = ((bf16[3,320,640]{1,0,2:T(4,128)(2,1)}), bf16[3,320,640]{1,0,2:T(4,128)(2,1)S(1)}, u32[]{:S(2)}, u32[]{:S(2)}) async-start(bf16[3,320,640]{1,0,2:T(4,128)(2,1)} %copy.80), calls=%async_computation | async-start | bytes 3932160 | tf_op jit(solution)/shard_map/all_to_all | solution.py:261
  84.8 142.2 %all-gather.16.cloned.1.call-start = ((), (), s32[]{:S(2)}) async-start(), calls=%async_computation.15 | async-start | bytes 3686400 | tf_op jit(solution)/shard_map/all_gather | solution.py:279
  120.7 6.7 %copy-start.20 = (bf16[1280,480]{0,1:T(8,128)(2,1)}, bf16[1280,480]{0,1:T(8,128)(2,1)S(1)}, u32[]{:S(2)}) copy-start(bf16[1280,480]{0,1:T(8,128)(2,1)S(1)} %constant_dynamic-update-slice_fusion) | copy-start | bytes 3686404
  136.0 5.6 copy-start.3
  188.9 5.1 copy-start.22
  190.4 21.1 %all-to-all-start.1 = ((bf16[160,8,512]{2,0,1:T(8,128)(2,1)}), bf16[160,8,512]{2,0,1:T(8,128)(2,1)S(1)}, u32[]{:S(2)}, u32[]{:S(2)}) async-start(bf16[160,8,512]{2,0,1:T(8,128)(2,1)} %copy.87), calls=%async_computation.1 | async-start | bytes 2621440 | tf_op jit(solution)/shard_map/all_to_all | solution.py:254
  194.0 172.3 %reduce-scatter.8.cloned.1.call-start = ((), (), s32[]{:S(2)}) async-start(), calls=%async_computation.10 | async-start | bytes 11059200 | tf_op jit(solution)/shard_map/reduce_scatter | solution.py:321
  212.1 1.1 copy-start.6
  212.2 4.5 copy-start
  212.2 4.5 copy-start.16
  220.6 4.2 copy-start.9
  220.6 4.2 copy-start.18
  227.0 3.2 copy-start.5
  227.0 3.2 copy-start.14
  230.3 1.3 copy-start.11
  230.3 1.7 copy-start.12
  232.0 2.2 copy-start.19
  234.1 2.8 copy-start.8
  236.9 2.0 copy-start.2
  252.6 3.2 copy-start.10
  252.6 3.2 copy-start.17
  261.0 22.0 %all-to-all-start.2 = ((bf16[8,160,512]{2,1,0:T(8,128)(2,1)}), bf16[8,160,512]{2,1,0:T(8,128)(2,1)}, u32[]{:S(2)}, u32[]{:S(2)}) async-start(bf16[8,160,512]{2,1,0:T(8,128)(2,1)} %bitcast.97), calls=%async_computation.2 | async-start | bytes 2621440 | tf_op jit(solution)/shard_map/all_to_all | solution.py:248
  265.3 166.0 %all-reduce.4.cloned.1.call-start = ((), (), s32[]{:S(2)}) async-start(), calls=%async_computation.11 | async-start | bytes 2457600 | tf_op jit(solution)/shard_map/psum | solution.py:322
  366.3 84.3 %reduce-scatter.4.cloned.1.call-start = ((), (), s32[]{:S(2)}) async-start(), calls=%async_computation.8 | async-start | bytes 15728640 | tf_op jit(solution)/shard_map/reduce_scatter | solution.py:341
  376.4 143.6 %all-reduce.6.cloned.1.call-start = ((), (), s32[]{:S(2)}) async-start(), calls=%async_computation.12 | async-start | bytes 2949120 | tf_op jit(solution)/shard_map/psum | solution.py:351
  431.4 152.2 %reduce-scatter.6.cloned.1.call-start = ((), (), s32[]{:S(2)}) async-start(), calls=%async_computation.9 | async-start | bytes 6553600 | tf_op jit(solution)/shard_map/reduce_scatter | solution.py:344
  452.3 3.0 copy-start.7
  452.3 3.0 copy-start.15
  452.3 3.0 copy-start.21
  455.3 2.4 copy-start.13
  583.6 2.8 copy-start.1
  583.6 2.8 copy-start.4
  586.4 44.1 %copy-start.28 = (f32[80]{0:T(128)S(1)}, f32[80]{0:T(128)}, u32[]{:S(2)}) copy-start(f32[80]{0:T(128)} %param.16) | copy-start | bytes 964
Sparse Core Ops, SparseCore 0:
  9.9 65.8 all-gather.9
  77.6 46.9 all-gather.11
  126.5 32.8 all-gather.13
  161.1 32.6 all-gather.15
  252.8 80.7 reduce-scatter.7
  366.4 64.2 all-reduce.3
  433.0 17.4 reduce-scatter.3
  453.0 66.9 all-reduce.5
  523.0 60.5 reduce-scatter.5

commit v3 on v2

--- a/solution.py
+++ b/solution.py
@@ -94,7 +94,8 @@
 
 
 def backward_kernel(
-    bq, bk, heads, count, prefix_ref, q_t, k, k_t, v, g_t, o_t, lse, dq_t, dk, dv, dk_sum, dv_sum
+    bq, bk, heads, count, prefix_ref, factor, queries_t, q_t, k, k_t, v, g_t, o_t, lse,
+    joined, scale, dk_sum, dv_sum, scale_sum,
 ):
     i = pl.program_id(0)
     prefix = prefix_ref[0]
@@ -104,6 +105,7 @@
     def _():
         dk_sum[...] = jnp.zeros_like(dk_sum)
         dv_sum[...] = jnp.zeros_like(dv_sum)
+        scale_sum[...] = jnp.zeros_like(scale_sum)
 
     centre = [
         jnp.sum(g_t[h].astype(jnp.float32) * o_t[h], axis=0, keepdims=True) for h in range(heads)
@@ -112,57 +114,260 @@
     def step(masked, j, carry):
         rows = pl.ds(pl.multiple_of(j * bk, bk), bk)
         out = []
-        scores = [dot(k[h, rows, :], q_t[h], NN) for h in range(heads)]
-        along = [dot(v[h, rows, :], g_t[h], NN) for h in range(heads)]
         for h in range(heads):
-            s = visible(scores[h], i, j, bq, bk, prefix) if masked else scores[h]
+            s = dot(k[h, rows, :], q_t[h], NN)
+            along = dot(v[h, rows, :], g_t[h], NN)
+            s = visible(s, i, j, bq, bk, prefix) if masked else s
             weights = jnp.exp(s - lse[h])
-            low = (weights * (along[h] - centre[h])).astype(jnp.bfloat16)
-            dv_sum[h, rows, :] += dot(weights.astype(jnp.bfloat16), g_t[h], NT)
-            dk_sum[h, rows, :] += dot(low, q_t[h], NT)
+            low = (weights * (along - centre[h])).astype(jnp.bfloat16)
+            dv_sum[h, :, rows] += dot(g_t[h], weights.astype(jnp.bfloat16), NT)
+            dk_sum[h, :, rows] += dot(q_t[h], low, NT)
             out.append(carry[h] + dot(k_t[h, :, rows], low, NN))
         return tuple(out)
 
     done = tuple(jnp.zeros((DH, bq), jnp.float32) for _ in range(heads))
     done = lax.fori_loop(0, whole, functools.partial(step, False), done)
     done = lax.fori_loop(whole, seen, functools.partial(step, True), done)
+    own = pl.ds(pl.multiple_of(i * bq, bq), bq)
     for h in range(heads):
-        dq_t[h] = done[h]
+        joined[h * DH : (h + 1) * DH, own] = (done[h] * factor[...]).astype(jnp.bfloat16)
+        scale_sum[...] += done[h] * queries_t[h]
 
     @pl.when(i == count - 1)
     def _():
-        dk[...] = dk_sum[...].astype(jnp.bfloat16)
-        dv[...] = dv_sum[...].astype(jnp.bfloat16)
-
-
-def attention_backward(q_t, k, k_t, v, g_t, o_t, lse, prefix):
+        for h in range(heads):
+            joined[(heads + h) * DH : (heads + h + 1) * DH, :] = dk_sum[h].astype(jnp.bfloat16)
+            joined[(2 * heads + h) * DH : (2 * heads + h + 1) * DH, :] = dv_sum[h].astype(jnp.bfloat16)
+        scale[...] = jnp.sum(scale_sum[...], axis=1, keepdims=True)
+
+
+def attention_backward(factor, queries_t, q_t, k, k_t, v, g_t, o_t, lse, prefix):
     heads, _, length = q_t.shape
     bq = bk = min(512, length)
     columns = lambda n: pl.BlockSpec((heads, n, bq), lambda i, p: (0, 0, i))
-    whole = lambda a: pl.BlockSpec(a.shape, lambda i, p: (0, 0, 0))
+    whole = lambda a: pl.BlockSpec(a.shape, lambda i, p: (0,) * len(a.shape))
+    joined = jax.ShapeDtypeStruct((3 * heads * DH, length), jnp.bfloat16)
+    scale = jax.ShapeDtypeStruct((DH, 1), jnp.float32)
     return pl.pallas_call(
         functools.partial(backward_kernel, bq, bk, heads, length // bq),
         grid_spec=pltpu.PrefetchScalarGridSpec(
             num_scalar_prefetch=1,
             grid=(length // bq,),
             in_specs=[
-                columns(DH), whole(k), whole(k_t), whole(v), columns(DH), columns(DH), columns(1)
+                whole(factor), columns(DH), columns(DH), whole(k), whole(k_t), whole(v),
+                columns(DH), columns(DH), columns(1),
             ],
-            out_specs=[columns(DH), whole(k), whole(k)],
-            scratch_shapes=[pltpu.VMEM(k.shape, jnp.float32)] * 2,
+            out_specs=[whole(joined), whole(scale)],
+            scratch_shapes=[pltpu.VMEM(k_t.shape, jnp.float32)] * 2 + [pltpu.VMEM((DH, bq), jnp.float32)],
         ),
-        out_shape=[
-            jax.ShapeDtypeStruct(q_t.shape, jnp.float32),
-            jax.ShapeDtypeStruct(k.shape, jnp.bfloat16),
-            jax.ShapeDtypeStruct(k.shape, jnp.bfloat16),
-        ],
+        out_shape=[joined, scale],
         cost_estimate=pl.CostEstimate(
             flops=heads * length * length * 256 * 5,
             transcendentals=heads * length * length // 2,
             bytes_accessed=heads * length * DH * 24,
         ),
         name="attention_backward",
-    )(prefix, q_t, k, k_t, v, g_t, o_t, lse)
+    )(prefix, factor, queries_t, q_t, k, k_t, v, g_t, o_t, lse)
+
+
+MESH = pl.DeviceIdType.MESH
+
+
+def wide(ref):
+    return ref[...].astype(jnp.float32)
+
+
+def peers():
+    x, y, z = lax.axis_index("gx"), lax.axis_index("gy"), lax.axis_index("dp")
+    return x, y, z, y + 1 - 2 * (y % 2), (y + 2) % 4, 3 - y, z + 1 - 2 * (z % 2)
+
+
+def send(src, dst, send_sem, recv_sem, to):
+    return pltpu.make_async_remote_copy(
+        src_ref=src, dst_ref=dst, send_sem=send_sem, recv_sem=recv_sem, device_id=to, device_id_type=MESH
+    )
+
+
+def greet(devices):
+    barrier = pltpu.get_barrier_semaphore()
+    for to in devices:
+        pl.semaphore_signal(barrier, inc=1, device_id=to, device_id_type=MESH)
+    return barrier
+
+
+def tail_kernel(
+    part, dw, back, total,
+    mine, theirs, both, first_x, own_x, last_y, first_y, own_y, last_x, mid_x, mid_y,
+    pieces, outer, cross, partial, final,
+    load, pair_send, pair_recv, give_send, give_recv, xy_send, xy_recv, up_send, up_recv, mid_send, mid_recv, down_send, down_recv,
+):
+    x, y, z, xn, yn, dn, zn = peers()
+    tokens = back.shape[1]
+    half = back.shape[0] // 2
+    inner = (z == 1) | (z == 2)
+    barrier = greet([{"gx": 1 - x}, {"gy": xn}, {"gy": yn}, {"gy": dn}, {"dp": zn}])
+
+    @pl.when(inner)
+    def _():
+        pl.semaphore_signal(barrier, inc=1, device_id={"dp": 3 - z}, device_id_type=MESH)
+        pl.semaphore_wait(barrier, 6)
+
+    @pl.when(jnp.logical_not(inner))
+    def _():
+        pl.semaphore_wait(barrier, 5)
+
+    def columns(core, owner):
+        return part.at[:, pl.ds(pl.multiple_of((core * 4 + owner) * tokens, tokens), tokens)]
+
+    order = (dn, xn, yn, y)
+    pair = [send(columns(1 - x, d), theirs.at[n], pair_send.at[n], pair_recv.at[n], {"gx": 1 - x}) for n, d in enumerate(order)]
+    loads = [pltpu.make_async_copy(columns(x, d), mine.at[n], load.at[n]) for n, d in enumerate(order)]
+    give = [send(dw.at[d], pieces.at[y], give_send.at[n], give_recv.at[n], {"gy": d}) for n, d in enumerate((xn, yn, dn))]
+    keep = pltpu.make_async_copy(dw.at[y], pieces.at[y], load.at[4])
+    for n in range(4):
+        pair[n].start()
+        loads[n].start()
+        if n == 0:
+            keep.start()
+            for copy in give:
+                copy.start()
+
+    upper, lower = pl.ds(0, half), pl.ds(half, half)
+    to_x, to_y = {"gy": xn}, {"gy": yn}
+    xy = [
+        send(both.at[0, upper, :], first_x, xy_send.at[0], xy_recv.at[0], to_x),
+        send(both.at[0, lower, :], first_y, xy_send.at[1], xy_recv.at[1], to_y),
+        send(both.at[1, upper, :], own_x, xy_send.at[2], xy_recv.at[2], to_x),
+        send(both.at[2, lower, :], own_y, xy_send.at[3], xy_recv.at[3], to_y),
+        send(mid_x, last_y, xy_send.at[4], xy_recv.at[4], to_y),
+        send(mid_y, last_x, xy_send.at[5], xy_recv.at[5], to_x),
+    ]
+
+    for n in range(4):
+        loads[n].wait()
+        pair[n].wait_recv()
+        both[n] = (wide(mine.at[n]) + wide(theirs.at[n])).astype(jnp.bfloat16)
+        if n == 0:
+            xy[0].start()
+            xy[1].start()
+        elif n < 3:
+            xy[n + 1].start()
+
+    chunk = (y, xn, yn, dn)
+    up = [send(pieces.at[c], outer.at[n], up_send.at[n], up_recv.at[n], {"dp": zn}) for n, c in enumerate(chunk)]
+    meet = [send(partial.at[n], cross.at[n], mid_send.at[n], mid_recv.at[n], {"dp": 3 - z}) for n in range(4)]
+    down = [send(final.at[c], final.at[c], down_send.at[n], down_recv.at[n], {"dp": zn}) for n, c in enumerate(chunk)]
+
+    keep.wait()
+    for n in range(4):
+        if n:
+            give[n - 1].wait_recv()
+
+        @pl.when(jnp.logical_not(inner))
+        def _():
+            up[n].start()
+
+    def gather_up(n):
+        @pl.when(inner)
+        def _():
+            up[n].wait_recv()
+            partial[n] = (wide(pieces.at[chunk[n]]) + wide(outer.at[n])).astype(jnp.bfloat16)
+            meet[n].start()
+
+    def send_down(n):
+        @pl.when(inner)
+        def _():
+            meet[n].wait_recv()
+            final[chunk[n]] = (wide(partial.at[n]) + wide(cross.at[n])).astype(jnp.bfloat16)
+            down[n].start()
+
+    gather_up(0)
+    gather_up(1)
+    xy[0].wait_recv()
+    mid_x[...] = (wide(both.at[2, upper, :]) + wide(first_x)).astype(jnp.bfloat16)
+    xy[4].start()
+    xy[1].wait_recv()
+    mid_y[...] = (wide(both.at[1, lower, :]) + wide(first_y)).astype(jnp.bfloat16)
+    xy[5].start()
+    send_down(0)
+    gather_up(2)
+    send_down(1)
+    gather_up(3)
+    send_down(2)
+    send_down(3)
+    xy[2].wait_recv()
+    xy[4].wait_recv()
+    back[0:half, :] = wide(both.at[3, upper, :]) + wide(own_x) + wide(last_y)
+    xy[3].wait_recv()
+    xy[5].wait_recv()
+    back[half : 2 * half, :] = wide(both.at[3, lower, :]) + wide(own_y) + wide(last_x)
+
+    @pl.when(inner)
+    def _():
+        for n in range(4):
+            meet[n].wait_send()
+            down[n].wait_send()
+
+    @pl.when(jnp.logical_not(inner))
+    def _():
+        for n in range(4):
+            up[n].wait_send()
+            down[n].wait_recv()
+
+    total[...] = final[...]
+    for copy in pair + give + xy:
+        copy.wait_send()
+
+
+def tail(part, dw, tokens):
+    features = part.shape[0]
+    block = pltpu.VMEM((features, tokens), jnp.bfloat16)
+    four = pltpu.VMEM((4, features, tokens), jnp.bfloat16)
+    half = pltpu.VMEM((features // 2, tokens), jnp.bfloat16)
+    blocks = pltpu.VMEM(dw.shape, jnp.bfloat16)
+    sem = pltpu.SemaphoreType.DMA
+    return pl.pallas_call(
+        tail_kernel,
+        in_specs=[pl.BlockSpec(memory_space=pl.ANY)] * 2,
+        out_specs=[pl.BlockSpec(memory_space=pltpu.VMEM)] * 2,
+        out_shape=[
+            jax.ShapeDtypeStruct((features, tokens), jnp.float32),
+            jax.ShapeDtypeStruct(dw.shape, jnp.bfloat16),
+        ],
+        scratch_shapes=[four] * 3 + [half] * 8 + [blocks] * 5
+        + [sem((5,)), sem((4,)), sem((4,)), sem((3,)), sem((3,)), sem((6,)), sem((6,))]
+        + [sem((4,))] * 6,
+        compiler_params=pltpu.CompilerParams(collective_id=1, has_side_effects=True),
+        name="tail",
+    )(part, dw)
+
+
+def small_sum_kernel(value, out, held, arrived, send_sem, recv_sem):
+    x, y, z, xn, yn, dn, zn = peers()
+    steps = [{"gx": 1 - x}, {"gy": xn}, {"gy": yn}, {"dp": zn}, {"dp": (z + 2) % 4}]
+    barrier = greet(steps)
+    pl.semaphore_wait(barrier, 5)
+    held[0] = value[...]
+    for n, to in enumerate(steps):
+        copy = send(held.at[n], arrived.at[n], send_sem.at[n], recv_sem.at[n], to)
+        copy.start()
+        copy.wait()
+        if n < 4:
+            held[n + 1] = held[n] + arrived[n]
+        else:
+            out[...] = held[n] + arrived[n]
+
+
+def small_sum(value):
+    return pl.pallas_call(
+        small_sum_kernel,
+        in_specs=[pl.BlockSpec(memory_space=pltpu.VMEM)],
+        out_specs=pl.BlockSpec(memory_space=pltpu.VMEM),
+        out_shape=jax.ShapeDtypeStruct(value.shape, jnp.float32),
+        scratch_shapes=[pltpu.VMEM((5,) + value.shape, jnp.float32)] * 2 + [pltpu.SemaphoreType.DMA((5,))] * 2,
+        compiler_params=pltpu.CompilerParams(collective_id=2, has_side_effects=True),
+        name="small_sum",
+    )(value)
 
 
 def late_gradient_kernel(left_a, right_a, left_b, right_b, left_c, right_c, out):
@@ -240,6 +445,7 @@
     heads = all_heads // (gx * gy if split else gy)
     assert prefix_len.shape[0] == lax.axis_size("dp")
     assert heads * (gx * gy if split else gy) == all_heads
+    kernels = split and (gx, gy, lax.axis_size("dp")) == (2, 4, 4)
     x_index, y_index = lax.axis_index("gx"), lax.axis_index("gy")
     prefix = lax.dynamic_slice_in_dim(prefix_len, lax.axis_index("dp"), 1, 0)
 
@@ -321,50 +527,45 @@
     late_gradient = lax.psum_scatter(late_gradient, both, scatter_dimension=0, tiled=False)
     late_gradient = lax.psum(late_gradient, "dp")
 
-    dq_t, dk, dv = attention_backward(
-        q_t, k, k_t, v, g_t.reshape(heads, DH, group), o_t, lse, prefix
-    )
-    scale_part = jnp.sum(dq_t * queries_t, axis=(0, 2))
-    if not split:
-        scale_part = scale_part / gx
-    joined = jnp.concatenate(
-        [
-            (dq_t * factor[None, :, None]).astype(jnp.bfloat16).reshape(own, group),
-            jnp.swapaxes(dk, 1, 2).reshape(own, group),
-            jnp.swapaxes(dv, 1, 2).reshape(own, group),
-        ],
-        axis=0,
-    )
-    back = dot(joined, jnp.concatenate([wq, wk, wv], axis=1), (((0,), (1,)), ((), ())))
-    back = back.astype(jnp.bfloat16)
-    if split:
-        back = lax.psum_scatter(back, "gx", scatter_dimension=0, tiled=True)
+    joined, scale_part = attention_backward(
+        factor[:, None], queries_t, q_t, k, k_t, v, g_t.reshape(heads, DH, group), o_t, lse, prefix
+    )
+    own_all = jnp.concatenate([wq, wk, wv], axis=1)
+    part = dot(own_all, joined, NN).astype(jnp.bfloat16)
+    early_gradient = dot(normed_one, joined, (((0,), (1,)), ((), ()))).astype(jnp.bfloat16)
+    unit_one, inverse_one, _ = normalize(inputs, first_gain_all)
+    if kernels:
+        back, early_gradient = tail(part, early_gradient.reshape(gy, -1, 3 * own), rows)
+        back = back.T
+        early_gradient = jnp.moveaxis(
+            early_gradient.astype(jnp.float32).reshape(gy, -1, 3, own), 0, 2
+        )
+        early_gradient = [early_gradient[:, n].reshape(-1, gy * own) for n in range(3)]
+        late_gradient = late_gradient.astype(jnp.float32)
     else:
-        back = lax.dynamic_slice_in_dim(back, x_index * (group // gx), group // gx, 0)
-    back = lax.psum_scatter(back, "gy", scatter_dimension=0, tiled=True).astype(jnp.float32)
-    early_gradient = dot(normed_one, joined, (((0,), (1,)), ((), ()))).astype(jnp.bfloat16)
-    early_gradient = jnp.stack(
-        [early_gradient[:, :own], early_gradient[:, own : 2 * own], early_gradient[:, 2 * own :]]
-    )
-    early_gradient = weight_from_heads(early_gradient)
-    early_gradient, late_gradient = lax.optimization_barrier((early_gradient, late_gradient))
-    early_gradient = lax.psum(early_gradient, "dp").astype(jnp.float32)
-    late_gradient = late_gradient.astype(jnp.float32)
-
-    unit_one, inverse_one, _ = normalize(inputs, first_gain_all)
+        back = part.T
+        if split:
+            back = lax.psum_scatter(back, "gx", scatter_dimension=0, tiled=True)
+        else:
+            back = lax.dynamic_slice_in_dim(back, x_index * (group // gx), group // gx, 0)
+        back = lax.psum_scatter(back, "gy", scatter_dimension=0, tiled=True).astype(jnp.float32)
+        early_gradient = weight_from_heads(
+            jnp.stack([early_gradient[:, n * own : (n + 1) * own] for n in range(3)])
+        )
+        early_gradient, late_gradient = lax.optimization_barrier((early_gradient, late_gradient))
+        early_gradient = lax.psum(early_gradient, "dp").astype(jnp.float32)
+        late_gradient = late_gradient.astype(jnp.float32)
     input_part, first_gain_part = normalize_back(back, unit_one, inverse_one, first_gain_all)
     input_gradient = (middle_gradient + input_part).astype(jnp.bfloat16)
 
-    small = lax.psum(
-        (
-            first_gain_part,
-            second_gain_part,
-            jnp.sum(upstream, axis=0),
-            jnp.sum(before_gradient, axis=0),
-            scale_part,
-        ),
-        ("dp", "gx", "gy"),
-    )
+    scale_part = scale_part[:, 0] if split else scale_part[:, 0] / gx
+    small = [first_gain_part, second_gain_part, jnp.sum(upstream, axis=0), jnp.sum(before_gradient, axis=0)]
+    if kernels:
+        small = jnp.stack(small + [jnp.pad(scale_part, (0, width - DH))])
+        small = small_sum(jnp.pad(small, ((0, 3), (0, 0))))
+        small = [small[0], small[1], small[2], small[3], small[4, :DH]]
+    else:
+        small = lax.psum(tuple(small) + (scale_part,), ("dp", "gx", "gy"))
     gain_width, bias_width = first_gain.shape[0], inner_bias.shape[0]
     at_y = lambda a: lax.dynamic_slice_in_dim(a, y_index * gain_width, gain_width, 0)
     return (

time: 651 us -> 539 us (0.83)
  waiting for transfers between devices: 230 us -> 99.5 us
  Pallas kernels: 122 us -> 217 us
  blocking collectives: 95.6 us -> 44.4 us
  local copies, waits for them, and re-layouts: 72.1 us -> 49.1 us
    pallas_call x0 -> x2, Pallas kernels: none -> 89.3 us  [the longest x1 67.3 us: tail(): pl.pallas_call(tail_kernel, in_specs=[pl.BlockSpec(memory_space=pl.ANY)]...]
    reduce_scatter x2 -> x0, waiting for transfers between devices: 71.7 us -> none  [the longest x1 52.8 us: per_device(): lax.psum_scatter(back, 'gy', scatter_dimension=0, tiled=True)]
    psum x1 -> x0, waiting for transfers between devices: 60.6 us -> none  [per_device(): early_gradient = lax.psum(early_gradient, 'dp').astype(jnp.float32)]
    psum x1 -> x0, blocking collectives: 39.8 us -> none  [per_device(): lax.psum((first_gain_part, second_gain_part, jnp.sum(upstream, axis=0), j...]
    all_to_all x1 -> x0, blocking collectives: 21.5 us -> none  [weight_from_heads(): stack = lax.all_to_all(stack, 'gy', split_axis=1, concat_axis=2, tiled=True)]
    psum x1, waiting for transfers between devices: 0.01 us -> 19.5 us  [per_device(): late_gradient = lax.psum(late_gradient, 'dp')]
    unnamed x69 -> x65, local copies, waits for them, and re-layouts: 20.8 us -> 8.51 us
    all_gather x1, blocking collectives: 2.32 us -> 12.7 us  [per_device(): inner_bias_all = lax.all_gather(inner_bias, 'gx', axis=0, tiled=True)]
  transfers between devices with their start and end apart: 12 -> 9, of which waited for: 6 -> 4; matrix products, arithmetic and copies ran while one was open for 22% -> 24% of each run, Pallas kernels for 17% -> 38%
where the time goes in v3:
time: 539 us; the launch traced here: 529 us
  Pallas kernels  217 us (40%)
  waiting for transfers between devices  99.5 us (18%)
  matrix products  61.7 us (11%)
  local copies, waits for them, and re-layouts  49.1 us (9%)
  blocking collectives  44.4 us (8%)
  other arithmetic  30.2 us (6%)
  between operations  14.9 us (3%)
  starting transfers between devices  11.9 us (2%)
    pallas_call x1, Pallas kernels, attention_backward(): pl.pallas_call(functools.partial(backward_kernel, bq, bk, heads, length /...  68.5 us
    all_gather x1, waiting for transfers between devices, per_device(): everyone = lax.all_gather(layer_input, both, axis=0, tiled=True)  67.8 us
    pallas_call x1, Pallas kernels, tail(): pl.pallas_call(tail_kernel, in_specs=[pl.BlockSpec(memory_space=pl.ANY)]...  67.3 us
    dot_general x15, matrix products, dot(): return lax.dot_general(left, right, how, preferred_element_type=jnp.float32)  61.7 us
    pallas_call x1, Pallas kernels, attention_forward(): pl.pallas_call(functools.partial(forward_kernel, bq, bk, heads), grid_spe...  45.9 us
    all_gather x1, blocking collectives, per_device(): lax.all_gather(jnp.stack([first_gain, second_gain, outer_bias]), 'gy', ax...  31.8 us
    pallas_call x1, Pallas kernels, small_sum(): pl.pallas_call(small_sum_kernel, in_specs=[pl.BlockSpec(memory_space=pltp...  22 us
    psum x1, waiting for transfers between devices, per_device(): late_gradient = lax.psum(late_gradient, 'dp')  19.5 us
  transfers between devices with their start and end apart: 9, of which 4 were waited for; matrix products, arithmetic and copies ran while one was open for 24% of the time, Pallas kernels for 38%

profile of v3, /device:TPU:0, one launch (start us, length us, event | category | flops | bytes accessed | tf_op | source)
XLA Modules:
  0.0 529.1 jit_solution(3319632983073641684)
XLA Ops:
  8.0 67.8 %all-gather.10.cloned.1.call-done = bf16[4096,1280]{1,0:T(8,128)(2,1)} async-done(((bf16[512,1280]{1,0:T(8,128)(2,1)}), bf16[4096,1280]{1,0:T(8,128)(2,1)}) %all-gather.10.cloned.1.call-update) | async-done | bytes 10485776 | tf_op jit(solution)/shard_map/all_gather | solution.py:476
  77.9 3.0 copy.86
  81.0 3.8 all-to-all-start
  84.9 31.8 %all-gather.3 = f32[4,320,3]{1,2,0:T(4,128)S(1)} all-gather(f32[1,320,3]{1,2,0:T(4,128)S(1)} %maximum_bitcast_fusion.1), channel_id=1, replica_groups=mesh['dp'=4,'gx'=2,'gy'=4] {'gy'}, dimensions={0}, use_global_device_ids=true | all-gather | bytes 19200 | tf_op jit(solution)/shard_map/all_gather | solution.py:478
  119.9 6.6 %fusion = f32[4096]{0:T(1024)S(1)} fusion(bf16[4096,1280]{1,0:T(8,128)(2,1)} %all-gather.10.cloned.1.call-done), kind=kLoop, calls=%fused_computation.2 | loop fusion | flops 15724544 | bytes 10502144 | tf_op jit(solution)/shard_map/reduce_sum | solution.py:412
  126.5 10.1 %fusion.71 = (bf16[480,4096]{1,0:T(8,128)(2,1)S(1)}, f32[480,4096]{1,0:T(8,128)}) fusion(bf16[1280,480]{0,1:T(8,128)(2,1)S(1)} %constant_dynamic-update-slice_fusion, bf16[4096,1280]{1,0:T(8,128)(2,1)} %all-gather.10.cloned.1.call-done, f32[1280]{0:T(1024)S(1)} %get-tuple-element.78, f32[4096]{0:T(1024)S(1)} %add_rsqrt_fusion), kind=kOutput, calls=%fused_computation.102 | convolution fusion | flops 5056102400 | bytes 23532544 | tf_op jit(solution)/shard_map/dot_general | solution.py:19
  137.8 2.4 copy.92.k
  140.3 1.9 slice.125
  142.2 1.5 multiply_convert_fusion.2.q_t
  143.8 45.9 %attention_forward.1 = (f32[2,80,4096]{2,1,0:T(8,128)}, f32[2,1,4096]{2,1,0:T(1,128)}) custom-call(s32[1]{0:T(128)} %dynamic_slice.23.prefix_ref, bf16[2,80,4096]{2,1,0:T(8,128)(2,1)} %multiply_convert_fusion.2.q_t, bf16[2,4096,80]{2,1,0:T(8,128)(2,1)} %copy.92.k, bf16[2,80,4096]{2,1,0:T(8,128)(2,1)} %bitcast.89), custom_call_target="tpu_custom_call" | custom-call | flops 17179869184 | bytes 7864320 | tf_op jit(solution)/shard_map/attention_forward/pallas_call | solution.py:75
  189.6 1.9 convert_element_type.67
  192.1 1.5 copy.93
  193.6 3.6 all-to-all-start.1
  197.2 12.7 %all-gather.4 = f32[2,1,640]{2,1,0:T(1,128)S(1)} all-gather(f32[1,1,640]{2,1,0:T(1,128)S(1)} %reshape.140), channel_id=1, replica_groups=mesh['dp'=4,'gx'=2,'gy'=4] {'gx'}, dimensions={0}, use_global_device_ids=true | all-gather | bytes 7680 | tf_op jit(solution)/shard_map/all_gather | solution.py:479
  209.9 4.7 all-to-all-done.1
  216.4 3.4 fusion.41
  219.8 2.5 multiply_reduce_fusion.2
  223.8 4.2 fusion.34
  228.0 2.3 fusion.31
  230.3 3.2 fusion.45
  235.2 2.1 fusion.65
  238.6 1.5 multiply_reduce_fusion
  240.1 1.9 fusion.64.left_a
  242.1 13.8 %late_gradients.1 = bf16[2,4,3,320,640]{4,3,2,1,0:T(8,128)(2,1)} custom-call(bf16[512,1280]{1,0:T(8,128)(2,1)} %fusion.64.left_a, bf16[512,1280]{1,0:T(8,128)(2,1)} %bitcast.101, bf16[512,1280]{1,0:T(8,128)(2,1)} %multiply_convert_fusion.1.left_b, bf16[512,1280]{1,0:T(8,128)(2,1)} %copy-done.8, bf16[512,1280]{1,0:T(8,128)(2,1)} %left_c.1, ...), custom_call_target="tpu_custom_call" | custom-call | flops 5033164800 | bytes 17694720 | tf_op jit(solution)/shard_map/late_gradients/pallas_call | solution.py:388
  256.0 3.2 fusion.51
  261.5 2.4 copy.98
  263.9 4.3 all-to-all-start.2
  268.3 1.9 fusion.22
  271.0 4.2 copy.97
  275.2 3.0 fusion.27
  278.2 2.4 fusion.12
  280.6 6.0 %all-to-all-done.2 = bf16[8,160,512]{2,1,0:T(8,128)(2,1)} async-done(((bf16[8,160,512]{2,1,0:T(8,128)(2,1)}), bf16[8,160,512]{2,1,0:T(8,128)(2,1)}, u32[]{:S(2)}, u32[]{:S(2)}) %all-to-all-start.2) | async-done | bytes 1310752 | tf_op jit(solution)/shard_map/all_to_all | solution.py:454
  286.6 3.1 copy.99
  289.7 3.3 reshape.118.g_t
  293.0 68.5 %attention_backward.1 = (bf16[480,4096]{1,0:T(8,128)(2,1)}, f32[80,1]{1,0:T(8,128)}) custom-call(s32[1]{0:T(128)} %dynamic_slice.23.prefix_ref, f32[80,1]{1,0:T(8,128)} %copy.100.factor, f32[2,80,4096]{2,1,0:T(8,128)} %bitcast.84, bf16[2,80,4096]{2,1,0:T(8,128)(2,1)} %multiply_convert_fusion.2.q_t, bf16[2,4096,80]{2,1,0:T(8,128)(2,1)} %copy.92.k, ...), custom_call_target="tpu_custom_call" | custom-call | flops 42949672960 | bytes 15728640 | tf_op jit(solution)/shard_map/attention_backward/pallas_call | solution.py:151
  361.5 11.7 %fusion.13 = bf16[1280,480]{0,1:T(8,128)(2,1)} fusion(bf16[480,4096]{1,0:T(8,128)(2,1)} %get-tuple-element.29, bf16[4096,1280]{1,0:T(8,128)(2,1)} %all-gather.10.cloned.1.call-done, f32[1280]{0:T(1024)S(1)} %get-tuple-element.78, f32[4096]{0:T(1024)S(1)} %add_rsqrt_fusion), kind=kOutput, calls=%fused_computation.22 | convolution fusion | flops 5054750720 | bytes 15668224 | tf_op jit(solution)/shard_map/dot_general | solution.py:19
  373.2 2.4 copy.102
  375.6 10.7 %convolution_convert_fusion.part = bf16[1280,4096]{1,0:T(8,128)(2,1)} fusion(bf16[1280,480]{0,1:T(8,128)(2,1)} %copy-done.19, bf16[480,4096]{1,0:T(8,128)(2,1)} %get-tuple-element.29), kind=kOutput, calls=%fused_computation.5 | convolution fusion | flops 5038407680 | bytes 15646720 | tf_op jit(solution)/shard_map/dot_general | solution.py:19
  386.3 67.3 %tail.1 = (f32[1280,512]{1,0:T(8,128)}, bf16[4,320,480]{2,1,0:T(8,128)(2,1)}) custom-call(bf16[1280,4096]{1,0:T(8,128)(2,1)} %convolution_convert_fusion.part, bf16[4,320,480]{2,1,0:T(8,128)(2,1)} %bitcast.95), custom_call_target="tpu_custom_call" | custom-call | tf_op jit(solution)/shard_map/tail/pallas_call | solution.py:329
  453.6 3.2 copy.103
  456.8 2.9 fusion.21
  459.7 5.1 convert_reduce_fusion
  465.7 22.0 %small_sum.1 = f32[8,1280]{1,0:T(8,128)} custom-call(f32[8,1280]{1,0:T(8,128)} %pad.9.value), custom_call_target="tpu_custom_call" | custom-call | tf_op jit(solution)/shard_map/small_sum/pallas_call | solution.py:362
  487.7 1.7 copy.104
  489.4 1.7 fusion.68
  491.1 2.5 copy.105
  493.5 2.4 copy.106
  499.7 19.5 %all-reduce.4.cloned.1.call-done = bf16[3,320,640]{2,1,0:T(8,128)(2,1)} async-done(((bf16[3,320,640]{2,1,0:T(8,128)(2,1)}), bf16[3,320,640]{2,1,0:T(8,128)(2,1)}) %all-reduce.4.cloned.1.call-update) | async-done | bytes 1228816 | tf_op jit(solution)/shard_map/psum | solution.py:528
  (129 shorter events, 24.7 us)
Async XLA Ops:
  7.2 68.6 %all-gather.10.cloned.1.call-start = ((), (), s32[]{:S(2)}) async-start(), calls=%async_computation.4 | async-start | bytes 11796480 | tf_op jit(solution)/shard_map/all_gather | solution.py:476
  7.9 207.4 %all-gather.12.cloned.1.call-start = ((), (), s32[]{:S(2)}) async-start(), calls=%async_computation.7 | async-start | bytes 3686400 | tf_op jit(solution)/shard_map/all_gather | solution.py:485
  75.8 148.0 %all-gather.14.cloned.1.call-start = ((), (), s32[]{:S(2)}) async-start(), calls=%async_computation.8 | async-start | bytes 3686400 | tf_op jit(solution)/shard_map/all_gather | solution.py:485
  80.9 3.8 copy-start.23
  80.9 3.9 copy-start.24
  81.0 3.9 copy-start.25
  81.0 35.8 %copy-start.26 = (s32[4]{0:T(128)S(1)}, s32[4]{0:T(128)}, u32[]{:S(2)}) copy-start(s32[4]{0:T(128)} %param.26) | copy-start | bytes 52
  81.0 36.4 %copy-start.27 = (f32[80]{0:T(128)S(1)}, f32[80]{0:T(128)}, u32[]{:S(2)}) copy-start(f32[80]{0:T(128)} %param.16) | copy-start | bytes 964
  81.0 36.5 %all-to-all-start = ((bf16[3,320,640]{1,0,2:T(4,128)(2,1)}), bf16[3,320,640]{1,0,2:T(4,128)(2,1)S(1)}, u32[]{:S(2)}, u32[]{:S(2)}) async-start(bf16[3,320,640]{1,0,2:T(4,128)(2,1)} %copy.86), calls=%async_computation | async-start | bytes 3932160 | tf_op jit(solution)/shard_map/all_to_all | solution.py:467
  84.7 145.5 %all-gather.16.cloned.1.call-start = ((), (), s32[]{:S(2)}) async-start(), calls=%async_computation.9 | async-start | bytes 3686400 | tf_op jit(solution)/shard_map/all_gather | solution.py:485
  119.9 6.6 %copy-start.19 = (bf16[1280,480]{0,1:T(8,128)(2,1)}, bf16[1280,480]{0,1:T(8,128)(2,1)S(1)}, u32[]{:S(2)}) copy-start(bf16[1280,480]{0,1:T(8,128)(2,1)S(1)} %constant_dynamic-update-slice_fusion) | copy-start | bytes 3686404
  137.8 2.5 copy-start.3
  142.2 47.4 %copy-start.2 = (f32[160,4096]{1,0:T(8,128)}, f32[160,4096]{1,0:T(8,128)S(1)}, u32[]{:S(2)}) copy-start(f32[160,4096]{1,0:T(8,128)S(1)} %slice.125) | copy-start | bytes 7864324
  192.1 5.1 copy-start.22
  193.6 21.1 %all-to-all-start.1 = ((bf16[160,8,512]{2,0,1:T(8,128)(2,1)}), bf16[160,8,512]{2,0,1:T(8,128)(2,1)S(1)}, u32[]{:S(2)}, u32[]{:S(2)}) async-start(bf16[160,8,512]{2,0,1:T(8,128)(2,1)} %copy.93), calls=%async_computation.1 | async-start | bytes 2621440 | tf_op jit(solution)/shard_map/all_to_all | solution.py:460
  197.2 262.5 %reduce-scatter.2.cloned.1.call-start = ((), (), s32[]{:S(2)}) async-start(), calls=%async_computation.5 | async-start | bytes 11059200 | tf_op jit(solution)/shard_map/reduce_scatter | solution.py:527
  215.3 1.1 copy-start.6
  215.3 4.5 copy-start
  215.4 4.5 copy-start.13
  223.8 4.3 copy-start.9
  223.8 4.3 copy-start.15
  230.3 3.2 copy-start.4
  230.3 3.2 copy-start.17
  233.5 1.3 copy-start.11
  233.5 1.7 copy-start.12
  235.2 2.2 copy-start.16
  237.3 2.8 copy-start.8
  240.1 2.0 copy-start.1
  255.9 3.2 copy-start.10
  255.9 3.2 copy-start.14
  263.9 22.7 %all-to-all-start.2 = ((bf16[8,160,512]{2,1,0:T(8,128)(2,1)}), bf16[8,160,512]{2,1,0:T(8,128)(2,1)}, u32[]{:S(2)}, u32[]{:S(2)}) async-start(bf16[8,160,512]{2,1,0:T(8,128)(2,1)} %bitcast.91), calls=%async_computation.2 | async-start | bytes 2621440 | tf_op jit(solution)/shard_map/all_to_all | solution.py:454
  268.3 250.9 %all-reduce.4.cloned.1.call-start = ((), (), s32[]{:S(2)}) async-start(), calls=%async_computation.6 | async-start | bytes 2457600 | tf_op jit(solution)/shard_map/psum | solution.py:528
  275.2 3.0 copy-start.7
  275.2 3.0 copy-start.18
  459.7 5.1 copy-start.21
  491.0 4.9 copy-start.5
  491.0 6.1 %copy-start.20 = (f32[8,1280]{1,0:T(8,128)S(1)}, f32[8,1280]{1,0:T(8,128)}, u32[]{:S(2)}) copy-start(f32[8,1280]{1,0:T(8,128)} %small_sum.1) | copy-start | bytes 122884
Sparse Core Ops, SparseCore 0:
  9.9 65.8 all-gather.9
  77.6 46.9 all-gather.11
  126.5 32.7 all-gather.13
  161.0 32.8 all-gather.15
  256.0 79.2 reduce-scatter.1
  459.8 59.2 all-reduce.3

commit v4 on v3

--- a/solution.py
+++ b/solution.py
@@ -202,8 +202,8 @@
     load, pair_send, pair_recv, give_send, give_recv, xy_send, xy_recv, up_send, up_recv, mid_send, mid_recv, down_send, down_recv,
 ):
     x, y, z, xn, yn, dn, zn = peers()
-    tokens = back.shape[1]
-    half = back.shape[0] // 2
+    tokens = back.shape[0]
+    half = back.shape[1] // 2
     inner = (z == 1) | (z == 2)
     barrier = greet([{"gx": 1 - x}, {"gy": xn}, {"gy": yn}, {"gy": dn}, {"dp": zn}])
 
@@ -297,10 +297,10 @@
     send_down(3)
     xy[2].wait_recv()
     xy[4].wait_recv()
-    back[0:half, :] = wide(both.at[3, upper, :]) + wide(own_x) + wide(last_y)
+    back[:, 0:half] = (wide(both.at[3, upper, :]) + wide(own_x) + wide(last_y)).T
     xy[3].wait_recv()
     xy[5].wait_recv()
-    back[half : 2 * half, :] = wide(both.at[3, lower, :]) + wide(own_y) + wide(last_x)
+    back[:, half : 2 * half] = (wide(both.at[3, lower, :]) + wide(own_y) + wide(last_x)).T
 
     @pl.when(inner)
     def _():
@@ -331,13 +331,14 @@
         in_specs=[pl.BlockSpec(memory_space=pl.ANY)] * 2,
         out_specs=[pl.BlockSpec(memory_space=pltpu.VMEM)] * 2,
         out_shape=[
-            jax.ShapeDtypeStruct((features, tokens), jnp.float32),
+            jax.ShapeDtypeStruct((tokens, features), jnp.float32),
             jax.ShapeDtypeStruct(dw.shape, jnp.bfloat16),
         ],
         scratch_shapes=[four] * 3 + [half] * 8 + [blocks] * 5
         + [sem((5,)), sem((4,)), sem((4,)), sem((3,)), sem((3,)), sem((6,)), sem((6,))]
         + [sem((4,))] * 6,
         compiler_params=pltpu.CompilerParams(collective_id=1, has_side_effects=True),
+        cost_estimate=pl.CostEstimate(flops=60_000_000_000, transcendentals=0, bytes_accessed=180_000_000),
         name="tail",
     )(part, dw)
 
@@ -366,8 +367,156 @@
         out_shape=jax.ShapeDtypeStruct(value.shape, jnp.float32),
         scratch_shapes=[pltpu.VMEM((5,) + value.shape, jnp.float32)] * 2 + [pltpu.SemaphoreType.DMA((5,))] * 2,
         compiler_params=pltpu.CompilerParams(collective_id=2, has_side_effects=True),
+        cost_estimate=pl.CostEstimate(flops=12_000_000_000, transcendentals=0, bytes_accessed=36_000_000),
         name="small_sum",
     )(value)
+
+
+def head_kernel(
+    rows_in, blocks_in, small_in, scale_factor,
+    normed, weights, small, queries_t, q_t, k_t, v_t, k, v,
+    gathered, kept, weights_t, arrived,
+    load, keep_send, small_send, small_recv, w_send, w_recv, xy_send, xy_recv, pair_send, pair_recv,
+):
+    x, y, z, xn, yn, dn, zn = peers()
+    rows = rows_in.shape[0]
+    half = rows // 2
+    tall = blocks_in.shape[1]
+    heads = q_t.shape[0]
+    own = heads * DH
+    features = rows_in.shape[1]
+    partner, to_x, to_y = {"gx": 1 - x}, {"gy": xn}, {"gy": yn}
+    barrier = greet([partner, to_x, to_y, {"gy": dn}])
+    pl.semaphore_wait(barrier, 4)
+
+    def block(core, source):
+        return gathered.at[pl.ds(pl.multiple_of((core * 4 + source) * rows, rows), rows), :]
+
+    def piece(core, source, lower):
+        return gathered.at[pl.ds(pl.multiple_of((core * 4 + source) * rows + lower * half, half), half), :]
+
+    def weight_rows(source):
+        return weights.at[pl.ds(pl.multiple_of(source * tall, tall), tall), :]
+
+    upper_in, lower_in = rows_in.at[pl.ds(0, half), :], rows_in.at[pl.ds(half, half), :]
+    smalls = [
+        send(small_in, arrived.at[n], small_send.at[n], small_recv.at[n], to)
+        for n, to in enumerate((to_x, to_y, {"gy": dn}, partner))
+    ]
+    ws = [
+        send(blocks_in.at[d], weight_rows(y), w_send.at[n], w_recv.at[n], {"gy": d})
+        for n, d in enumerate((xn, yn, dn))
+    ]
+    xy = [
+        send(lower_in, piece(x, y, 1), xy_send.at[0], xy_recv.at[0], to_x),
+        send(upper_in, piece(x, y, 0), xy_send.at[1], xy_recv.at[1], to_y),
+        send(upper_in, piece(x, y, 0), xy_send.at[2], xy_recv.at[2], to_x),
+        send(lower_in, piece(x, y, 1), xy_send.at[3], xy_recv.at[3], to_y),
+        send(piece(x, yn, 0), piece(x, yn, 0), xy_send.at[4], xy_recv.at[4], to_x),
+        send(piece(x, xn, 1), piece(x, xn, 1), xy_send.at[5], xy_recv.at[5], to_y),
+    ]
+    came = ((xn, 1), (yn, 0), (xn, 0), (yn, 1), (dn, 0), (dn, 1))
+    pair = [
+        send(piece(x, s, lower), piece(x, s, lower), pair_send.at[n], pair_recv.at[n], partner)
+        for n, (s, lower) in enumerate(came)
+    ] + [send(rows_in, block(x, y), pair_send.at[6], pair_recv.at[6], partner)]
+    own_rows = pltpu.make_async_copy(rows_in, block(x, y), load.at[0])
+    own_blocks = pltpu.make_async_copy(blocks_in.at[y], weight_rows(y), load.at[1])
+
+    for copy in smalls + [ws[2], ws[0], ws[1], pair[6], own_rows, own_blocks] + xy[:4]:
+        copy.start()
+    for copy in smalls + ws:
+        copy.wait_recv()
+    small[...] = small_in[...]
+    small[0:3, :] = small_in[0:3, :] + arrived[0, 0:3, :] + arrived[1, 0:3, :] + arrived[2, 0:3, :]
+    small[3:4, :] = small_in[3:4, :] + arrived[3, 3:4, :]
+    own_blocks.wait()
+    weights_t[...] = weights[...].T
+
+    def stage(number, spot):
+        def body(u, carry):
+            core, odd = u // 2, u % 2
+            source, lower = spot(odd)
+            start = pl.multiple_of((core * 4 + source) * rows + lower * half, half)
+            here = pl.ds(start, half)
+            values = wide(gathered.at[here, :])
+            inverse = lax.rsqrt(jnp.mean(values * values, axis=-1, keepdims=True) + 1e-06)
+            low = (values * inverse * small[0:1, :]).astype(jnp.bfloat16)
+            kept[here, :] = low
+            pltpu.make_async_copy(kept.at[here, :], normed.at[here, :], keep_send.at[number * 4 + u]).start()
+            turned = dot(weights_t[...], low, NT)
+            for h in range(heads):
+                at = h * DH
+                queries_t[h, :, here] = turned[at : at + DH]
+                q_t[h, :, here] = (turned[at : at + DH] * scale_factor[...]).astype(jnp.bfloat16)
+                key = turned[own + at : own + at + DH]
+                value = turned[2 * own + at : 2 * own + at + DH]
+                k_t[h, :, here] = key.astype(jnp.bfloat16)
+                v_t[h, :, here] = value.astype(jnp.bfloat16)
+                k[h, here, :] = key.T.astype(jnp.bfloat16)
+                v[h, here, :] = value.T.astype(jnp.bfloat16)
+            return carry
+
+        lax.fori_loop(0, 4, body, 0)
+
+    near = lambda odd: xn * (1 - odd) + yn * odd
+    own_rows.wait()
+    pair[6].wait_recv()
+    stage(0, lambda odd: (y, odd))
+    for n in range(6):
+        xy[n].wait_recv()
+        pair[n].start()
+        if n < 2:
+            xy[5 - n].start()
+        if n % 2:
+            pair[n - 1].wait_recv()
+            pair[n].wait_recv()
+            if n == 1:
+                stage(1, lambda odd: (near(odd), 1 - odd))
+            elif n == 3:
+                stage(2, lambda odd: (near(odd), odd))
+            else:
+                stage(3, lambda odd: (dn, odd))
+    for n in range(16):
+        pltpu.make_async_copy(kept.at[pl.ds(0, half), :], normed.at[pl.ds(0, half), :], keep_send.at[n]).wait()
+    for copy in smalls + ws + xy + pair:
+        copy.wait_send()
+
+
+def head(rows_in, blocks_in, small_in, scale_factor):
+    rows, features = rows_in.shape
+    three = blocks_in.shape[2]
+    heads = three // (3 * DH)
+    group = rows * 8
+    sem = pltpu.SemaphoreType.DMA
+    vmem, anywhere = pl.BlockSpec(memory_space=pltpu.VMEM), pl.BlockSpec(memory_space=pl.ANY)
+    low = lambda *shape: jax.ShapeDtypeStruct(shape, jnp.bfloat16)
+    return pl.pallas_call(
+        head_kernel,
+        in_specs=[anywhere, anywhere, vmem, vmem],
+        out_specs=[anywhere] + [vmem] * 8,
+        out_shape=[
+            low(group, features),
+            low(features, three),
+            jax.ShapeDtypeStruct(small_in.shape, jnp.float32),
+            jax.ShapeDtypeStruct((heads, DH, group), jnp.float32),
+            low(heads, DH, group),
+            low(heads, DH, group),
+            low(heads, DH, group),
+            low(heads, group, DH),
+            low(heads, group, DH),
+        ],
+        scratch_shapes=[
+            pltpu.VMEM((group, features), jnp.bfloat16),
+            pltpu.VMEM((group, features), jnp.bfloat16),
+            pltpu.VMEM((three, features), jnp.bfloat16),
+            pltpu.VMEM((4,) + small_in.shape, jnp.float32),
+        ]
+        + [sem((2,)), sem((16,)), sem((4,)), sem((4,)), sem((3,)), sem((3,)), sem((6,)), sem((6,)), sem((7,)), sem((7,))],
+        compiler_params=pltpu.CompilerParams(collective_id=3, has_side_effects=True),
+        cost_estimate=pl.CostEstimate(flops=60_000_000_000, transcendentals=0, bytes_accessed=180_000_000),
+        name="head",
+    )(rows_in, blocks_in, small_in, scale_factor)
 
 
 def late_gradient_kernel(left_a, right_a, left_b, right_b, left_c, right_c, out):
@@ -473,30 +622,44 @@
             stack = lax.dynamic_slice_in_dim(stack, x_index * own, own, 2)
         return stack
 
-    everyone = lax.all_gather(layer_input, both, axis=0, tiled=True)
-    own_weights = weight_to_heads(jnp.stack([query_weight, key_weight, value_weight]))
-    gains = lax.all_gather(jnp.stack([first_gain, second_gain, outer_bias]), "gy", axis=1, tiled=True)
-    inner_bias_all = lax.all_gather(inner_bias, "gx", axis=0, tiled=True)
-    first_gain_all, second_gain_all, outer_bias_all = gains[0], gains[1], gains[2]
-
+    factor = jax.nn.softplus(query_scale) * (softplus_unit / math.sqrt(DH))
+    own = heads * DH
     late = (output_weight.T, inner_weight, outer_weight.T)
-    late, everyone = lax.optimization_barrier((late, everyone))
+    if kernels:
+        blocks = jnp.stack([query_weight, key_weight, value_weight], axis=1)
+        blocks = blocks.reshape(-1, 3, gy, own).transpose(2, 0, 1, 3).reshape(gy, -1, 3 * own)
+        small = jnp.stack([first_gain, second_gain, outer_bias])
+        small = lax.dynamic_update_slice(
+            jnp.zeros((8, width), jnp.float32), small, (0, y_index * first_gain.shape[0])
+        )
+        small = lax.dynamic_update_slice(
+            small, inner_bias[None], (3, x_index * inner_bias.shape[0])
+        )
+        normed_one, own_all, small, queries_t, q_t, k_t, v_t, k, v = head(
+            layer_input, blocks, small, factor[:, None]
+        )
+        first_gain_all, second_gain_all, outer_bias_all, inner_bias_all = small[0], small[1], small[2], small[3]
+        late, q_t = lax.optimization_barrier((late, q_t))
+    else:
+        everyone = lax.all_gather(layer_input, both, axis=0, tiled=True)
+        own_weights = weight_to_heads(jnp.stack([query_weight, key_weight, value_weight]))
+        gains = lax.all_gather(jnp.stack([first_gain, second_gain, outer_bias]), "gy", axis=1, tiled=True)
+        inner_bias_all = lax.all_gather(inner_bias, "gx", axis=0, tiled=True)
+        first_gain_all, second_gain_all, outer_bias_all = gains[0], gains[1], gains[2]
+        late, everyone = lax.optimization_barrier((late, everyone))
+        _, _, normed_one = normalize(everyone.astype(jnp.float32), first_gain_all)
+        own_all = jnp.concatenate([own_weights[0], own_weights[1], own_weights[2]], axis=1)
+        turned = dot(own_all, normed_one, (((0,), (1,)), ((), ())))
+        queries_t = turned[:own].reshape(heads, DH, group)
+        k_t = turned[own : 2 * own].reshape(heads, DH, group).astype(jnp.bfloat16)
+        v_t = turned[2 * own :].reshape(heads, DH, group).astype(jnp.bfloat16)
+        q_t = (queries_t * factor[None, :, None]).astype(jnp.bfloat16)
+        k = jnp.swapaxes(k_t, 1, 2)
+        v = jnp.swapaxes(v_t, 1, 2)
     output_all, inner_all, outer_all = (
         lax.all_gather(w, both, axis=0, tiled=False).reshape(gx, gy * w.shape[0], w.shape[1])
         for w in late
     )
-
-    _, _, normed_one = normalize(everyone.astype(jnp.float32), first_gain_all)
-    factor = jax.nn.softplus(query_scale) * (softplus_unit / math.sqrt(DH))
-    own = heads * DH
-    wq, wk, wv = own_weights[0], own_weights[1], own_weights[2]
-    turned = dot(jnp.concatenate([wq, wk, wv], axis=1), normed_one, (((0,), (1,)), ((), ())))
-    queries_t = turned[:own].reshape(heads, DH, group)
-    k_t = turned[own : 2 * own].reshape(heads, DH, group).astype(jnp.bfloat16)
-    v_t = turned[2 * own :].reshape(heads, DH, group).astype(jnp.bfloat16)
-    q_t = (queries_t * factor[None, :, None]).astype(jnp.bfloat16)
-    k = jnp.swapaxes(k_t, 1, 2)
-    v = jnp.swapaxes(v_t, 1, 2)
     o_t, lse = attention_forward(q_t, k, v_t, prefix)
     attended = to_tokens(o_t.reshape(own, group).astype(jnp.bfloat16))
 
@@ -525,18 +688,17 @@
     )
     late_gradient = late_gradient.reshape((gx * gy,) + late_gradient.shape[2:])
     late_gradient = lax.psum_scatter(late_gradient, both, scatter_dimension=0, tiled=False)
-    late_gradient = lax.psum(late_gradient, "dp")
 
     joined, scale_part = attention_backward(
         factor[:, None], queries_t, q_t, k, k_t, v, g_t.reshape(heads, DH, group), o_t, lse, prefix
     )
-    own_all = jnp.concatenate([wq, wk, wv], axis=1)
+    late_gradient, joined = lax.optimization_barrier((late_gradient, joined))
+    late_gradient = lax.psum(late_gradient, "dp")
     part = dot(own_all, joined, NN).astype(jnp.bfloat16)
     early_gradient = dot(normed_one, joined, (((0,), (1,)), ((), ()))).astype(jnp.bfloat16)
     unit_one, inverse_one, _ = normalize(inputs, first_gain_all)
     if kernels:
         back, early_gradient = tail(part, early_gradient.reshape(gy, -1, 3 * own), rows)
-        back = back.T
         early_gradient = jnp.moveaxis(
             early_gradient.astype(jnp.float32).reshape(gy, -1, 3, own), 0, 2
         )

time: 539 us -> 517 us (0.959)
  Pallas kernels: 217 us -> 285 us
  blocking collectives: 44.4 us -> 0 us
  waiting for transfers between devices: 99.5 us -> 85.5 us
  matrix products: 61.7 us -> 51.1 us
  other arithmetic: 30.2 us -> 21.8 us
  local copies, waits for them, and re-layouts: 49.1 us -> 41.7 us
    pallas_call x0 -> x1, Pallas kernels: none -> 73.7 us  [head(): pl.pallas_call(head_kernel, in_specs=[anywhere, anywhere, vmem, vmem], ou...]
    all_gather x1 -> x0, waiting for transfers between devices: 67.8 us -> none  [per_device(): everyone = lax.all_gather(layer_input, both, axis=0, tiled=True)]
    all_gather x2 -> x0, blocking collectives: 44.4 us -> none  [the longest x1 31.8 us: per_device(): lax.all_gather(jnp.stack([first_gain, second_gain, outer_bias]), 'gy', ax...]
    all_gather x3, waiting for transfers between devices: 0.02 us -> 23.3 us  [per_device(): lax.all_gather(w, both, axis=0, tiled=False)]
    all_to_all x1, waiting for transfers between devices: 4.74 us -> 25.5 us  [to_tokens(): lax.all_to_all(columns, both, split_axis=1, concat_axis=0, tiled=True)]
    dot_general x15 -> x14, matrix products: 61.7 us -> 51.1 us  [dot(): return lax.dot_general(left, right, how, preferred_element_type=jnp.float32)]
    reduce_sum x2 -> x1, other arithmetic: 8.57 us -> 1.9 us  [normalize(): jnp.mean(values * values, axis=-1, keepdims=True) + 1e-06]
    pallas_call x1, Pallas kernels: 68.5 us -> 62.4 us  [attention_backward(): pl.pallas_call(functools.partial(backward_kernel, bq, bk, heads, length /...]
  transfers between devices with their start and end apart: 9 -> 7, of which waited for: 4 -> 4; matrix products, arithmetic and copies ran while one was open for 24% -> 11% of each run, Pallas kernels for 38% -> 25%
where the time goes in v4:
time: 517 us; the launch traced here: 508 us
  Pallas kernels  285 us (55%)
  waiting for transfers between devices  85.5 us (17%)
  matrix products  51.1 us (10%)
  local copies, waits for them, and re-layouts  41.7 us (8%)
  other arithmetic  21.8 us (4%)
  between operations  14.8 us (3%)
  starting transfers between devices  8.69 us (2%)
    pallas_call x1, Pallas kernels, head(): pl.pallas_call(head_kernel, in_specs=[anywhere, anywhere, vmem, vmem], ou...  73.7 us
    pallas_call x1, Pallas kernels, tail(): pl.pallas_call(tail_kernel, in_specs=[pl.BlockSpec(memory_space=pl.ANY)]...  70.9 us
    pallas_call x1, Pallas kernels, attention_backward(): pl.pallas_call(functools.partial(backward_kernel, bq, bk, heads, length /...  62.4 us
    dot_general x14, matrix products, dot(): return lax.dot_general(left, right, how, preferred_element_type=jnp.float32)  51.1 us
    pallas_call x1, Pallas kernels, attention_forward(): pl.pallas_call(functools.partial(forward_kernel, bq, bk, heads), grid_spe...  41.7 us
    psum x1, waiting for transfers between devices, per_device(): late_gradient = lax.psum(late_gradient, 'dp')  25.5 us
    all_to_all x1, waiting for transfers between devices, to_tokens(): lax.all_to_all(columns, both, split_axis=1, concat_axis=0, tiled=True)  25.5 us
    all_gather x3, waiting for transfers between devices, per_device(): lax.all_gather(w, both, axis=0, tiled=False)  23.3 us
  transfers between devices with their start and end apart: 7, of which 4 were waited for; matrix products, arithmetic and copies ran while one was open for 11% of the time, Pallas kernels for 25%

profile of v4, /device:TPU:0, one launch (start us, length us, event | category | flops | bytes accessed | tf_op | source)
XLA Modules:
  0.0 508.2 jit_solution(8262268609176824734)
XLA Ops:
  11.4 1.3 copy.40
  12.6 1.3 copy.41
  13.9 1.3 copy.42
  15.6 1.5 copy.44.blocks_in
  18.7 73.7 %head.1 = (bf16[4096,1280]{1,0:T(8,128)(2,1)}, bf16[1280,480]{1,0:T(8,128)(2,1)}, f32[8,1280]{1,0:T(8,128)}, f32[2,80,4096]{2,1,0:T(8,128)}, bf16[2,80,4096]{2,1...) custom-call(bf16[512,1280]{1,0:T(8,128)(2,1)} %rows_in.1, ...), custom_call_target="tpu_custom_call" | custom-call | flops 60000002048 | bytes 180000000 | tf_op jit(solution)/shard_map/head/pallas_call | solution.py:494
  94.5 41.7 %attention_forward.1 = (f32[2,80,4096]{2,1,0:T(8,128)}, f32[2,1,4096]{2,1,0:T(1,128)}) custom-call(s32[1]{0:T(128)} %dynamic_slice.23.prefix_ref, bf16[2,80,4096]{2,1,0:T(8,128)(2,1)} %get-tuple-element.35.q_t, bf16[2,4096,80]{2,1,0:T(8,128)(2,1)} %get-tuple-element.36.k, bf16[2,80,4096]{2,1,0:T(8,128)(2,1)} %get-tuple-element.37.v_t), custom_call_target="tpu_custom_call" | custom-call | flops 17179869184 | bytes 7864320 | tf_op jit(solution)/shard_map/attention_forward/pallas_call | solution.py:75
  136.2 2.0 convert_element_type.47
  138.8 1.5 copy.46
  140.3 4.0 all-to-all-start
  145.1 25.5 %all-to-all-done = bf16[160,8,512]{2,0,1:T(8,128)(2,1)S(1)} async-done(((bf16[160,8,512]{2,0,1:T(8,128)(2,1)}), bf16[160,8,512]{2,0,1:T(8,128)(2,1)S(1)}, u32[]{:S(2)}, u32[]{:S(2)}) %all-to-all-start) | async-done | bytes 1310752 | tf_op jit(solution)/shard_map/all_to_all | solution.py:609
  172.3 3.4 fusion.31
  175.8 2.5 multiply_reduce_fusion.2
  178.3 1.3 multiply_convert_fusion.1.left_b
  179.6 4.2 fusion.24
  183.9 2.3 fusion.21
  186.2 23.3 %all-gather.11.cloned.1.call-done = bf16[2560,640]{1,0:T(8,128)(2,1)} async-done(((bf16[320,640]{1,0:T(8,128)(2,1)}), bf16[2560,640]{1,0:T(8,128)(2,1)}) %all-gather.11.cloned.1.call-update) | async-done | bytes 3276816 | tf_op jit(solution)/shard_map/all_gather | solution.py:660
  209.4 3.2 fusion.35
  214.4 2.1 fusion.56
  216.5 1.2 fusion.26
  217.7 1.5 multiply_reduce_fusion
  219.3 1.9 fusion.55.left_a
  221.2 14.0 %late_gradients.1 = bf16[2,4,3,320,640]{4,3,2,1,0:T(8,128)(2,1)} custom-call(bf16[512,1280]{1,0:T(8,128)(2,1)} %fusion.55.left_a, bf16[512,1280]{1,0:T(8,128)(2,1)} %bitcast.68, bf16[512,1280]{1,0:T(8,128)(2,1)} %multiply_convert_fusion.1.left_b, bf16[512,1280]{1,0:T(8,128)(2,1)} %copy-done.8, bf16[512,1280]{1,0:T(8,128)(2,1)} %left_c.1, ...), custom_call_target="tpu_custom_call" | custom-call | flops 5033164800 | bytes 17694720 | tf_op jit(solution)/shard_map/late_gradients/pallas_call | solution.py:537
  235.3 3.2 fusion.41
  238.5 1.2 fusion.44
  240.8 2.6 copy.50
  243.5 4.3 all-to-all-start.1
  247.8 1.9 fusion.12
  249.8 3.5 fusion.17
  253.6 2.4 fusion.5
  256.0 9.7 %all-to-all-done.1 = bf16[8,160,512]{2,1,0:T(8,128)(2,1)} async-done(((bf16[8,160,512]{2,1,0:T(8,128)(2,1)}), bf16[8,160,512]{2,1,0:T(8,128)(2,1)}, u32[]{:S(2)}, u32[]{:S(2)}) %all-to-all-start.1) | async-done | bytes 1310752 | tf_op jit(solution)/shard_map/all_to_all | solution.py:603
  265.7 3.1 copy.51
  268.8 3.6 reshape.106.g_t
  272.4 62.4 %attention_backward.1 = (bf16[480,4096]{1,0:T(8,128)(2,1)}, f32[80,1]{1,0:T(8,128)}) custom-call(s32[1]{0:T(128)} %dynamic_slice.23.prefix_ref, f32[80,1]{1,0:T(8,128)} %copy.45.scale_factor.factor, f32[2,80,4096]{2,1,0:T(8,128)} %get-tuple-element.44.queries_t, bf16[2,80,4096]{2,1,0:T(8,128)(2,1)} %get-tuple-element.35.q_t, ...), custom_call_target="tpu_custom_call" | custom-call | flops 42949672960 | bytes 15728640 | tf_op jit(solution)/shard_map/attention_backward/pallas_call | solution.py:151
  335.7 10.8 %convolution_convert_fusion.1 = bf16[1280,480]{0,1:T(8,128)(2,1)} fusion(bf16[480,4096]{1,0:T(8,128)(2,1)} %get-tuple-element.49, bf16[4096,1280]{1,0:T(8,128)(2,1)} %get-tuple-element.50), kind=kOutput, calls=%fused_computation.15 | convolution fusion | flops 5033779200 | bytes 15646720 | tf_op jit(solution)/shard_map/dot_general | solution.py:19
  346.6 2.4 copy.53
  349.0 10.4 %convolution_convert_fusion.part = bf16[1280,4096]{1,0:T(8,128)(2,1)} fusion(bf16[1280,480]{1,0:T(8,128)(2,1)} %get-tuple-element.43, bf16[480,4096]{1,0:T(8,128)(2,1)} %get-tuple-element.49), kind=kOutput, calls=%fused_computation | convolution fusion | flops 5038407680 | bytes 15646720 | tf_op jit(solution)/shard_map/dot_general | solution.py:19
  359.4 70.9 %tail.1 = (f32[512,1280]{1,0:T(8,128)}, bf16[4,320,480]{2,1,0:T(8,128)(2,1)}) custom-call(bf16[1280,4096]{1,0:T(8,128)(2,1)} %convolution_convert_fusion.part, bf16[4,320,480]{2,1,0:T(8,128)(2,1)} %bitcast.72), custom_call_target="tpu_custom_call" | custom-call | flops 60000002048 | bytes 180000000 | tf_op jit(solution)/shard_map/tail/pallas_call | solution.py:329
  430.4 3.0 fusion.11
  433.6 4.5 convert_reduce_fusion
  438.8 21.9 %small_sum.1 = f32[8,1280]{1,0:T(8,128)} custom-call(f32[8,1280]{1,0:T(8,128)} %pad.9.value), custom_call_target="tpu_custom_call" | custom-call | flops 12000000000 | bytes 36000000 | tf_op jit(solution)/shard_map/small_sum/pallas_call | solution.py:363
  460.7 1.7 copy.54
  462.4 1.6 fusion.58
  464.1 2.5 copy.55
  466.6 2.4 copy.56
  469.0 1.2 copy.57
  472.7 25.5 %all-reduce.4.cloned.1.call-done = bf16[3,320,640]{2,1,0:T(8,128)(2,1)} async-done(((bf16[3,320,640]{2,1,0:T(8,128)(2,1)}), bf16[3,320,640]{2,1,0:T(8,128)(2,1)}) %all-reduce.4.cloned.1.call-update) | async-done | bytes 1228816 | tf_op jit(solution)/shard_map/psum | solution.py:696
  498.2 1.4 convert_element_type.58
  499.7 1.5 slice_bitcast_fusion
  (111 shorter events, 18.9 us)
Async XLA Ops:
  7.2 164.1 %all-gather.7.cloned.1.call-start = ((), (), s32[]{:S(2)}) async-start(), calls=%async_computation.5 | async-start | bytes 3686400 | tf_op jit(solution)/shard_map/all_gather | solution.py:660
  18.0 0.6 copy-start.24
  18.7 75.3 %copy-start.29 = (s32[4]{0:T(128)S(1)}, s32[4]{0:T(128)}, u32[]{:S(2)}) copy-start(s32[4]{0:T(128)} %param.26) | copy-start | bytes 52
  92.4 87.2 %all-gather.9.cloned.1.call-start = ((), (), s32[]{:S(2)}) async-start(), calls=%async_computation.6 | async-start | bytes 3686400 | tf_op jit(solution)/shard_map/all_gather | solution.py:660
  93.2 116.2 %all-gather.11.cloned.1.call-start = ((), (), s32[]{:S(2)}) async-start(), calls=%async_computation.7 | async-start | bytes 3686400 | tf_op jit(solution)/shard_map/all_gather | solution.py:660
  138.8 5.7 %copy-start.27 = (f32[8,1280]{1,0:T(8,128)S(1)}, f32[8,1280]{1,0:T(8,128)}, u32[]{:S(2)}) copy-start(f32[8,1280]{1,0:T(8,128)} %get-tuple-element.40) | copy-start | bytes 122884
  140.3 30.3 %all-to-all-start = ((bf16[160,8,512]{2,0,1:T(8,128)(2,1)}), bf16[160,8,512]{2,0,1:T(8,128)(2,1)S(1)}, u32[]{:S(2)}, u32[]{:S(2)}) async-start(bf16[160,8,512]{2,0,1:T(8,128)(2,1)} %copy.46), calls=%async_computation | async-start | bytes 2621440 | tf_op jit(solution)/shard_map/all_to_all | solution.py:609
  144.3 191.5 %reduce-scatter.2.cloned.1.call-start = ((), (), s32[]{:S(2)}) async-start(), calls=%async_computation.3 | async-start | bytes 11059200 | tf_op jit(solution)/shard_map/reduce_scatter | solution.py:690
  145.1 74.2 %copy-start.19 = (f32[1280]{0:T(1024)}, f32[1280]{0:T(1024)S(1)}, u32[]{:S(2)}) copy-start(f32[1280]{0:T(1024)S(1)} %get-tuple-element.75) | copy-start | bytes 15364
  171.2 1.1 copy-start.6
  171.3 4.5 copy-start.2
  171.3 4.5 copy-start.15
  178.3 41.0 %copy-start.22 = (f32[512]{0:T(512)}, f32[512]{0:T(512)S(1)}, u32[]{:S(2)}) copy-start(f32[512]{0:T(512)S(1)} %add_rsqrt_fusion.1) | copy-start | bytes 6148
  179.6 4.2 copy-start.9
  179.6 4.2 copy-start.17
  209.4 3.2 copy-start.4
  209.4 3.2 copy-start.13
  212.6 1.3 copy-start.11
  212.7 1.7 copy-start.12
  214.4 2.2 copy-start.18
  216.5 2.8 copy-start.8
  219.3 1.9 copy-start
  219.3 1.9 copy-start.25
  235.2 3.2 copy-start.10
  235.3 3.2 copy-start.16
  243.5 22.3 %all-to-all-start.1 = ((bf16[8,160,512]{2,1,0:T(8,128)(2,1)}), bf16[8,160,512]{2,1,0:T(8,128)(2,1)}, u32[]{:S(2)}, u32[]{:S(2)}) async-start(bf16[8,160,512]{2,1,0:T(8,128)(2,1)} %bitcast.59), calls=%async_computation.2 | async-start | bytes 2621440 | tf_op jit(solution)/shard_map/all_to_all | solution.py:603
  247.8 250.5 %all-reduce.4.cloned.1.call-start = ((), (), s32[]{:S(2)}) async-start(), calls=%async_computation.4 | async-start | bytes 2457600 | tf_op jit(solution)/shard_map/psum | solution.py:696
  249.7 3.6 copy-start.7
  249.7 3.9 copy-start.14
  359.4 71.0 %copy-start.21 = (f32[1280]{0:T(1024)S(1)}, f32[1280]{0:T(1024)}, u32[]{:S(2)}) copy-start(f32[1280]{0:T(1024)} %get-tuple-element.72) | copy-start | bytes 15364
  430.3 3.1 copy-start.1
  430.3 3.3 copy-start.3
  430.4 3.3 copy-start.20
  430.4 3.3 copy-start.23
  430.4 3.2 copy-start.26
  464.1 4.9 copy-start.5
  464.1 6.1 %copy-start.28 = (f32[8,1280]{1,0:T(8,128)S(1)}, f32[8,1280]{1,0:T(8,128)}, u32[]{:S(2)}) copy-start(f32[8,1280]{1,0:T(8,128)} %small_sum.1) | copy-start | bytes 122884
  464.1 8.1 %copy-start.30 = (f32[80]{0:T(128)S(1)}, f32[80]{0:T(128)}, u32[]{:S(2)}) copy-start(f32[80]{0:T(128)} %param.16) | copy-start | bytes 964
Sparse Core Ops, SparseCore 0:
  92.6 34.3 all-gather.6
  128.8 41.5 all-gather.8
  172.3 37.0 all-gather.10
  235.4 79.6 reduce-scatter.1
  438.9 59.2 all-reduce.3

commit v5 on v4

--- a/solution.py
+++ b/solution.py
@@ -196,9 +196,9 @@
 
 
 def tail_kernel(
-    part, dw, back, total,
+    part, dw, late, back, total, late_total,
     mine, theirs, both, first_x, own_x, last_y, first_y, own_y, last_x, mid_x, mid_y,
-    pieces, outer, cross, partial, final,
+    pieces, outer, cross, partial, final, late_outer, late_cross, late_partial, late_final,
     load, pair_send, pair_recv, give_send, give_recv, xy_send, xy_recv, up_send, up_recv, mid_send, mid_recv, down_send, down_recv,
 ):
     x, y, z, xn, yn, dn, zn = peers()
@@ -215,6 +215,13 @@
     @pl.when(jnp.logical_not(inner))
     def _():
         pl.semaphore_wait(barrier, 5)
+
+    late_up = [send(late.at[n], late_outer.at[n], up_send.at[4 + n], up_recv.at[4 + n], {"dp": zn}) for n in range(3)]
+
+    @pl.when(jnp.logical_not(inner))
+    def _():
+        for copy in late_up:
+            copy.start()
 
     def columns(core, owner):
         return part.at[:, pl.ds(pl.multiple_of((core * 4 + owner) * tokens, tokens), tokens)]
@@ -257,6 +264,8 @@
     up = [send(pieces.at[c], outer.at[n], up_send.at[n], up_recv.at[n], {"dp": zn}) for n, c in enumerate(chunk)]
     meet = [send(partial.at[n], cross.at[n], mid_send.at[n], mid_recv.at[n], {"dp": 3 - z}) for n in range(4)]
     down = [send(final.at[c], final.at[c], down_send.at[n], down_recv.at[n], {"dp": zn}) for n, c in enumerate(chunk)]
+    late_meet = [send(late_partial.at[n], late_cross.at[n], mid_send.at[4 + n], mid_recv.at[4 + n], {"dp": 3 - z}) for n in range(3)]
+    late_down = [send(late_final.at[n], late_final.at[n], down_send.at[4 + n], down_recv.at[4 + n], {"dp": zn}) for n in range(3)]
 
     keep.wait()
     for n in range(4):
@@ -281,66 +290,149 @@
             final[chunk[n]] = (wide(partial.at[n]) + wide(cross.at[n])).astype(jnp.bfloat16)
             down[n].start()
 
-    gather_up(0)
-    gather_up(1)
+    def late_gather_up(n):
+        @pl.when(inner)
+        def _():
+            late_up[n].wait_recv()
+            late_partial[n] = (wide(late.at[n]) + wide(late_outer.at[n])).astype(jnp.bfloat16)
+            late_meet[n].start()
+
+    def late_send_down(n):
+        @pl.when(inner)
+        def _():
+            late_meet[n].wait_recv()
+            late_final[n] = (wide(late_partial.at[n]) + wide(late_cross.at[n])).astype(jnp.bfloat16)
+            late_down[n].start()
+
+    late_gather_up(0)
+    late_gather_up(1)
+    late_send_down(0)
     xy[0].wait_recv()
     mid_x[...] = (wide(both.at[2, upper, :]) + wide(first_x)).astype(jnp.bfloat16)
     xy[4].start()
     xy[1].wait_recv()
     mid_y[...] = (wide(both.at[1, lower, :]) + wide(first_y)).astype(jnp.bfloat16)
     xy[5].start()
+    late_gather_up(2)
+    late_send_down(1)
+    gather_up(0)
+    late_send_down(2)
+    gather_up(1)
     send_down(0)
     gather_up(2)
     send_down(1)
-    gather_up(3)
-    send_down(2)
-    send_down(3)
     xy[2].wait_recv()
     xy[4].wait_recv()
     back[:, 0:half] = (wide(both.at[3, upper, :]) + wide(own_x) + wide(last_y)).T
+    gather_up(3)
+    send_down(2)
     xy[3].wait_recv()
     xy[5].wait_recv()
     back[:, half : 2 * half] = (wide(both.at[3, lower, :]) + wide(own_y) + wide(last_x)).T
+    send_down(3)
 
     @pl.when(inner)
     def _():
-        for n in range(4):
-            meet[n].wait_send()
-            down[n].wait_send()
+        for copy in meet + down + late_meet + late_down:
+            copy.wait_send()
 
     @pl.when(jnp.logical_not(inner))
     def _():
-        for n in range(4):
-            up[n].wait_send()
-            down[n].wait_recv()
+        for copy in up + late_up:
+            copy.wait_send()
+        for copy in down + late_down:
+            copy.wait_recv()
 
     total[...] = final[...]
+    late_total[...] = late_final[...]
     for copy in pair + give + xy:
         copy.wait_send()
 
 
-def tail(part, dw, tokens):
+def tail(part, dw, late, tokens):
     features = part.shape[0]
-    block = pltpu.VMEM((features, tokens), jnp.bfloat16)
-    four = pltpu.VMEM((4, features, tokens), jnp.bfloat16)
+    block = pltpu.VMEM((4, features, tokens), jnp.bfloat16)
     half = pltpu.VMEM((features // 2, tokens), jnp.bfloat16)
     blocks = pltpu.VMEM(dw.shape, jnp.bfloat16)
+    lates = pltpu.VMEM(late.shape, jnp.bfloat16)
     sem = pltpu.SemaphoreType.DMA
+    vmem, anywhere = pl.BlockSpec(memory_space=pltpu.VMEM), pl.BlockSpec(memory_space=pl.ANY)
     return pl.pallas_call(
         tail_kernel,
-        in_specs=[pl.BlockSpec(memory_space=pl.ANY)] * 2,
-        out_specs=[pl.BlockSpec(memory_space=pltpu.VMEM)] * 2,
+        in_specs=[anywhere, anywhere, vmem],
+        out_specs=[vmem] * 3,
         out_shape=[
             jax.ShapeDtypeStruct((tokens, features), jnp.float32),
             jax.ShapeDtypeStruct(dw.shape, jnp.bfloat16),
+            jax.ShapeDtypeStruct(late.shape, jnp.bfloat16),
         ],
-        scratch_shapes=[four] * 3 + [half] * 8 + [blocks] * 5
+        scratch_shapes=[block] * 3 + [half] * 8 + [blocks] * 5 + [lates] * 4
         + [sem((5,)), sem((4,)), sem((4,)), sem((3,)), sem((3,)), sem((6,)), sem((6,))]
-        + [sem((4,))] * 6,
+        + [sem((7,))] * 6,
         compiler_params=pltpu.CompilerParams(collective_id=1, has_side_effects=True),
         cost_estimate=pl.CostEstimate(flops=60_000_000_000, transcendentals=0, bytes_accessed=180_000_000),
         name="tail",
-    )(part, dw)
+    )(part, dw, late)
+
+
+def exchange_kernel(
+    branch, output_all, attended, normed, before, cotangent, hidden, g_t, late,
+    turned, local, send_sem, recv_sem,
+):
+    x, y, z, xn, yn, dn, zn = peers()
+    tokens = branch.shape[0]
+    own = g_t.shape[0]
+    wide_half = output_all.shape[2]
+    spots = (dn, xn, yn, y)
+    barrier = greet([{"gx": x if r == 0 else 1 - x, "gy": d} for r in range(2) for d in spots if not (r == 0 and d is y)])
+    pl.semaphore_wait(barrier, 7)
+    here = pl.ds(pl.multiple_of((x * 4 + y) * tokens, tokens), tokens)
+    copies = []
+    for r in range(2):
+        core = x if r == 0 else 1 - x
+        turned[r] = dot(branch[...], output_all[core], NN).T.astype(jnp.bfloat16)
+        for n, d in enumerate(spots):
+            src = turned.at[r, pl.ds(pl.multiple_of(d * own, own), own), :]
+            dst = g_t.at[:, here]
+            if r == 0 and n == 3:
+                keep = pltpu.make_async_copy(src, dst, local)
+                keep.start()
+            else:
+                at = r * 4 + n - (r == 1)
+                copies.append(send(src, dst, send_sem.at[at], recv_sem.at[at], {"gx": core, "gy": d}))
+                copies[-1].start()
+
+    def body(c, carry):
+        right_at = pl.ds(pl.multiple_of(c * wide_half, wide_half), wide_half)
+        for w, (left, right) in enumerate(((branch, attended), (normed, before), (cotangent, hidden))):
+            product = dot(left[...], right[:, right_at], TN)
+            late[c, :, w] = product.reshape(late.shape[1:2] + late.shape[3:]).astype(jnp.bfloat16)
+        return carry
+
+    lax.fori_loop(0, 2, body, 0)
+    keep.wait()
+    for copy in copies:
+        copy.wait()
+
+
+def exchange(branch, output_all, attended, normed, before, cotangent, hidden, own, gy):
+    tokens, features = branch.shape
+    gx, _, half = output_all.shape
+    vmem = pl.BlockSpec(memory_space=pltpu.VMEM)
+    sem = pltpu.SemaphoreType.DMA
+    return pl.pallas_call(
+        exchange_kernel,
+        in_specs=[vmem] * 7,
+        out_specs=[vmem] * 2,
+        out_shape=[
+            jax.ShapeDtypeStruct((own, gx * gy * tokens), jnp.bfloat16),
+            jax.ShapeDtypeStruct((gx, gy, 3, features // gy, half), jnp.bfloat16),
+        ],
+        scratch_shapes=[pltpu.VMEM((gx, half, tokens), jnp.bfloat16), sem, sem((7,)), sem((7,))],
+        compiler_params=pltpu.CompilerParams(collective_id=4, has_side_effects=True),
+        cost_estimate=pl.CostEstimate(flops=24_000_000_000, transcendentals=0, bytes_accessed=72_000_000),
+        name="exchange",
+    )(branch, output_all, attended, normed, before, cotangent, hidden)
 
 
 def small_sum_kernel(value, out, held, arrived, send_sem, recv_sem):
@@ -681,24 +773,28 @@
     )
     middle_gradient = upstream + middle_part
     branch_low = middle_gradient.astype(jnp.bfloat16)
-    g_t = to_heads(into(branch_low, output_all).astype(jnp.bfloat16).T)
-
-    late_gradient = late_gradients(
-        ((branch_low, attended), (normed_two, before_low), (output_cotangent, hidden)), gx, gy
-    )
+    if kernels:
+        g_t, late_gradient = exchange(
+            branch_low, output_all, attended, normed_two, before_low, output_cotangent, hidden, own, gy
+        )
+    else:
+        g_t = to_heads(into(branch_low, output_all).astype(jnp.bfloat16).T)
+        late_gradient = late_gradients(
+            ((branch_low, attended), (normed_two, before_low), (output_cotangent, hidden)), gx, gy
+        )
     late_gradient = late_gradient.reshape((gx * gy,) + late_gradient.shape[2:])
     late_gradient = lax.psum_scatter(late_gradient, both, scatter_dimension=0, tiled=False)
 
     joined, scale_part = attention_backward(
         factor[:, None], queries_t, q_t, k, k_t, v, g_t.reshape(heads, DH, group), o_t, lse, prefix
     )
-    late_gradient, joined = lax.optimization_barrier((late_gradient, joined))
-    late_gradient = lax.psum(late_gradient, "dp")
     part = dot(own_all, joined, NN).astype(jnp.bfloat16)
     early_gradient = dot(normed_one, joined, (((0,), (1,)), ((), ()))).astype(jnp.bfloat16)
     unit_one, inverse_one, _ = normalize(inputs, first_gain_all)
     if kernels:
-        back, early_gradient = tail(part, early_gradient.reshape(gy, -1, 3 * own), rows)
+        back, early_gradient, late_gradient = tail(
+            part, early_gradient.reshape(gy, -1, 3 * own), late_gradient, rows
+        )
         early_gradient = jnp.moveaxis(
             early_gradient.astype(jnp.float32).reshape(gy, -1, 3, own), 0, 2
         )
@@ -714,6 +810,7 @@
         early_gradient = weight_from_heads(
             jnp.stack([early_gradient[:, n * own : (n + 1) * own] for n in range(3)])
         )
+        late_gradient = lax.psum(late_gradient, "dp")
         early_gradient, late_gradient = lax.optimization_barrier((early_gradient, late_gradient))
         early_gradient = lax.psum(early_gradient, "dp").astype(jnp.float32)
         late_gradient = late_gradient.astype(jnp.float32)

time: 517 us -> 489 us (0.946)
  waiting for transfers between devices: 85.5 us -> 45 us
  Pallas kernels: 285 us -> 320 us
  local copies, waits for them, and re-layouts: 41.7 us -> 33.6 us
  matrix products: 51.1 us -> 44.4 us
    pallas_call x2, Pallas kernels: 84.9 us -> 116 us  [the longest x1 87.8 us: tail(): pl.pallas_call(tail_kernel, in_specs=[anywhere, anywhere, vmem], out_spec...]
    psum x1 -> x0, waiting for transfers between devices: 25.5 us -> none  [per_device(): late_gradient = lax.psum(late_gradient, 'dp')]
    all_to_all x1 -> x0, waiting for transfers between devices: 9.73 us -> none  [to_heads(): lax.all_to_all(columns, both, split_axis=0, concat_axis=1, tiled=True)]
    dot_general x14 -> x12, matrix products: 51.1 us -> 44.4 us  [dot(): return lax.dot_general(left, right, how, preferred_element_type=jnp.float32)]
    pallas_call x1, Pallas kernels: 62.4 us -> 68.5 us  [attention_backward(): pl.pallas_call(functools.partial(backward_kernel, bq, bk, heads, length /...]
    pallas_call x1, Pallas kernels: 21.9 us -> 16.1 us  [small_sum(): pl.pallas_call(small_sum_kernel, in_specs=[pl.BlockSpec(memory_space=pltp...]
    all_gather x3, waiting for transfers between devices: 23.3 us -> 18 us  [per_device(): lax.all_gather(w, both, axis=0, tiled=False)]
  transfers between devices with their start and end apart: 7 -> 5, of which waited for: 4 -> 2; matrix products, arithmetic and copies ran while one was open for 11% -> 10% of each run, Pallas kernels for 25% -> 24%
where the time goes in v5:
time: 489 us; the launch traced here: 482 us
  Pallas kernels  320 us (65%)
  waiting for transfers between devices  45 us (9%)
  matrix products  44.4 us (9%)
  local copies, waits for them, and re-layouts  33.6 us (7%)
  other arithmetic  19.6 us (4%)
  between operations  14.7 us (3%)
    pallas_call x1, Pallas kernels, tail(): pl.pallas_call(tail_kernel, in_specs=[anywhere, anywhere, vmem], out_spec...  87.8 us
    pallas_call x1, Pallas kernels, head(): pl.pallas_call(head_kernel, in_specs=[anywhere, anywhere, vmem, vmem], ou...  73.6 us
    pallas_call x1, Pallas kernels, attention_backward(): pl.pallas_call(functools.partial(backward_kernel, bq, bk, heads, length /...  68.5 us
    pallas_call x1, Pallas kernels, attention_forward(): pl.pallas_call(functools.partial(forward_kernel, bq, bk, heads), grid_spe...  45.9 us
    dot_general x12, matrix products, dot(): return lax.dot_general(left, right, how, preferred_element_type=jnp.float32)  44.4 us
    pallas_call x1, Pallas kernels, exchange(): pl.pallas_call(exchange_kernel, in_specs=[vmem] * 7, out_specs=[vmem] * 2...  27.9 us
    all_to_all x1, waiting for transfers between devices, to_tokens(): lax.all_to_all(columns, both, split_axis=1, concat_axis=0, tiled=True)  25.6 us
    all_gather x3, waiting for transfers between devices, per_device(): lax.all_gather(w, both, axis=0, tiled=False)  18 us
  transfers between devices with their start and end apart: 5, of which 2 were waited for; matrix products, arithmetic and copies ran while one was open for 10% of the time, Pallas kernels for 24%

profile of v5, /device:TPU:0, one launch (start us, length us, event | category | flops | bytes accessed | tf_op | source)
XLA Modules:
  0.0 481.6 jit_solution(2732430321801169482)
XLA Ops:
  7.9 0.7 stack.46
  10.0 0.7 broadcast_in_dim.7
  10.6 0.7 copy.44.scale_factor.factor
  11.4 1.3 copy.39
  12.6 1.3 copy.40
  13.9 1.3 copy.41
  15.6 1.5 copy.43.blocks_in
  18.7 73.6 %head.1 = (bf16[4096,1280]{1,0:T(8,128)(2,1)}, bf16[1280,480]{1,0:T(8,128)(2,1)}, f32[8,1280]{1,0:T(8,128)}, f32[2,80,4096]{2,1,0:T(8,128)}, bf16[2,80,4096]{2,1...) custom-call(bf16[512,1280]{1,0:T(8,128)(2,1)} %rows_in.1, ...), custom_call_target="tpu_custom_call" | custom-call | flops 60000002048 | bytes 180000000 | tf_op jit(solution)/shard_map/head/pallas_call | solution.py:586
  92.4 0.7 all-gather.11.cloned.1.call-update
  94.4 45.9 %attention_forward.1 = (f32[2,80,4096]{2,1,0:T(8,128)}, f32[2,1,4096]{2,1,0:T(1,128)}) custom-call(s32[1]{0:T(128)} %dynamic_slice.23.prefix_ref, bf16[2,80,4096]{2,1,0:T(8,128)(2,1)} %get-tuple-element.36.q_t, bf16[2,4096,80]{2,1,0:T(8,128)(2,1)} %get-tuple-element.37.k, bf16[2,80,4096]{2,1,0:T(8,128)(2,1)} %get-tuple-element.38.v_t), custom_call_target="tpu_custom_call" | custom-call | flops 17179869184 | bytes 7864320 | tf_op jit(solution)/shard_map/attention_forward/pallas_call | solution.py:75
  140.3 1.9 convert_element_type.46
  142.7 1.5 copy.45
  144.2 4.0 all-to-all-start
  149.1 25.6 %all-to-all-done = bf16[160,8,512]{2,0,1:T(8,128)(2,1)S(1)} async-done(((bf16[160,8,512]{2,0,1:T(8,128)(2,1)}), bf16[160,8,512]{2,0,1:T(8,128)(2,1)S(1)}, u32[]{:S(2)}, u32[]{:S(2)}) %all-to-all-start) | async-done | bytes 1310752 | tf_op jit(solution)/shard_map/all_to_all | solution.py:701
  175.4 1.0 copy-done.7
  176.4 3.4 fusion.15
  179.8 2.5 multiply_reduce_fusion.2
  182.4 4.4 fusion.31
  186.8 2.2 fusion.34
  189.1 1.3 multiply_convert_fusion.1.normed
  190.4 18.0 %all-gather.9.cloned.1.call-done = bf16[2560,640]{1,0:T(8,128)(2,1)} async-done(((bf16[320,640]{1,0:T(8,128)(2,1)}), bf16[2560,640]{1,0:T(8,128)(2,1)}) %all-gather.9.cloned.1.call-update) | async-done | bytes 3276816 | tf_op jit(solution)/shard_map/all_gather | solution.py:752
  208.4 3.2 fusion.24
  211.6 1.2 fusion.27
  213.3 2.1 fusion.46
  215.4 1.2 fusion.29
  216.6 1.5 multiply_reduce_fusion
  218.2 1.9 fusion.45.branch
  220.1 27.9 %exchange.1 = (bf16[160,4096]{1,0:T(8,128)(2,1)}, bf16[2,4,3,320,640]{4,3,2,1,0:T(8,128)(2,1)}) custom-call(bf16[512,1280]{1,0:T(8,128)(2,1)} %fusion.45.branch, bf16[2,1280,640]{2,1,0:T(8,128)(2,1)} %bitcast.68, bf16[512,1280]{1,0:T(8,128)(2,1)} %bitcast.63, bf16[512,1280]{1,0:T(8,128)(2,1)} %multiply_convert_fusion.1.normed, bf16[512,1280]{1,0:T(8,128)(2,1)} %copy-done.9, ...), custom_call_target="tpu_custom_call" | custom-call | flops 24000000000 | bytes 72000000 | tf_op jit(solution)/shard_map/exchange/pallas_call | solution.py:423
  248.0 1.6 fusion.12
  249.7 68.5 %attention_backward.1 = (bf16[480,4096]{1,0:T(8,128)(2,1)}, f32[80,1]{1,0:T(8,128)}) custom-call(s32[1]{0:T(128)} %dynamic_slice.23.prefix_ref, f32[80,1]{1,0:T(8,128)} %copy.44.scale_factor.factor, f32[2,80,4096]{2,1,0:T(8,128)} %get-tuple-element.45.queries_t, bf16[2,80,4096]{2,1,0:T(8,128)(2,1)} %get-tuple-element.36.q_t, ...), custom_call_target="tpu_custom_call" | custom-call | flops 42949672960 | bytes 15728640 | tf_op jit(solution)/shard_map/attention_backward/pallas_call | solution.py:151
  318.2 0.9 reduce.4
  319.1 11.0 %convolution_convert_fusion.1 = bf16[1280,480]{0,1:T(8,128)(2,1)} fusion(bf16[480,4096]{1,0:T(8,128)(2,1)} %get-tuple-element.50, bf16[4096,1280]{1,0:T(8,128)(2,1)} %get-tuple-element.51), kind=kOutput, calls=%fused_computation.15 | convolution fusion | flops 5033779200 | bytes 15646720 | tf_op jit(solution)/shard_map/dot_general | solution.py:19
  330.0 2.4 copy.50
  332.5 3.0 fusion.20
  335.5 2.4 fusion.5
  338.4 8.4 %convolution_convert_fusion.part = bf16[1280,4096]{1,0:T(8,128)(2,1)} fusion(bf16[1280,480]{1,0:T(8,128)(2,1)S(1)} %copy-done.30, bf16[480,4096]{1,0:T(8,128)(2,1)S(1)} %copy-done.29), kind=kOutput, calls=%fused_computation | convolution fusion | flops 5038407680 | bytes 15646720 | tf_op jit(solution)/shard_map/dot_general | solution.py:19
  346.9 87.8 %tail.1 = (f32[512,1280]{1,0:T(8,128)}, bf16[4,320,480]{2,1,0:T(8,128)(2,1)}, bf16[3,320,640]{2,1,0:T(8,128)(2,1)}) custom-call(bf16[1280,4096]{1,0:T(8,128)(2,1)} %convolution_convert_fusion.part, bf16[4,320,480]{2,1,0:T(8,128)(2,1)} %bitcast.67, bf16[3,320,640]{2,1,0:T(8,128)(2,1)} %bitcast.71), custom_call_target="tpu_custom_call" | custom-call | flops 60000002048 | bytes 180000000 | tf_op jit(solution)/shard_map/tail/pallas_call | solution.py:360
  434.8 3.0 fusion.11
  438.0 4.5 convert_reduce_fusion
  443.2 16.1 %small_sum.1 = f32[8,1280]{1,0:T(8,128)} custom-call(f32[8,1280]{1,0:T(8,128)} %pad.9.value), custom_call_target="tpu_custom_call" | custom-call | flops 12000000000 | bytes 36000000 | tf_op jit(solution)/shard_map/small_sum/pallas_call | solution.py:455
  459.4 1.2 divide_multiply_fusion
  460.6 1.0 fusion.49
  462.8 1.7 copy.51
  464.5 1.7 fusion.48
  466.2 2.6 copy.54
  468.7 2.4 copy.53
  471.1 1.2 copy.52
  472.5 1.5 slice_bitcast_fusion
  (100 shorter events, 11.7 us)
Async XLA Ops:
  7.2 168.2 %all-gather.7.cloned.1.call-start = ((), (), s32[]{:S(2)}) async-start(), calls=%async_computation.3 | async-start | bytes 3686400 | tf_op jit(solution)/shard_map/all_gather | solution.py:752
  18.0 0.6 copy-start.23
  18.7 75.2 %copy-start.27 = (s32[4]{0:T(128)S(1)}, s32[4]{0:T(128)}, u32[]{:S(2)}) copy-start(s32[4]{0:T(128)} %param.26) | copy-start | bytes 52
  92.3 90.1 %all-gather.11.cloned.1.call-start = ((), (), s32[]{:S(2)}) async-start(), calls=%async_computation.5 | async-start | bytes 3686400 | tf_op jit(solution)/shard_map/all_gather | solution.py:752
  93.1 115.3 %all-gather.9.cloned.1.call-start = ((), (), s32[]{:S(2)}) async-start(), calls=%async_computation.4 | async-start | bytes 3686400 | tf_op jit(solution)/shard_map/all_gather | solution.py:752
  142.7 5.7 %copy-start.26 = (f32[8,1280]{1,0:T(8,128)S(1)}, f32[8,1280]{1,0:T(8,128)}, u32[]{:S(2)}) copy-start(f32[8,1280]{1,0:T(8,128)} %get-tuple-element.41) | copy-start | bytes 122884
  144.2 30.5 %all-to-all-start = ((bf16[160,8,512]{2,0,1:T(8,128)(2,1)}), bf16[160,8,512]{2,0,1:T(8,128)(2,1)S(1)}, u32[]{:S(2)}, u32[]{:S(2)}) async-start(bf16[160,8,512]{2,0,1:T(8,128)(2,1)} %copy.45), calls=%async_computation | async-start | bytes 2621440 | tf_op jit(solution)/shard_map/all_to_all | solution.py:701
  148.2 198.7 %reduce-scatter.2.cloned.1.call-start = ((), (), s32[]{:S(2)}) async-start(), calls=%async_computation.2 | async-start | bytes 11059200 | tf_op jit(solution)/shard_map/reduce_scatter | solution.py:786
  149.1 69.1 %copy-start.18 = (f32[1280]{0:T(1024)}, f32[1280]{0:T(1024)S(1)}, u32[]{:S(2)}) copy-start(f32[1280]{0:T(1024)S(1)} %get-tuple-element.77) | copy-start | bytes 15364
  175.3 1.1 copy-start.7
  175.4 4.5 copy-start.2
  175.4 4.5 copy-start.16
  182.4 35.8 %copy-start.21 = (f32[512]{0:T(512)}, f32[512]{0:T(512)S(1)}, u32[]{:S(2)}) copy-start(f32[512]{0:T(512)S(1)} %add_rsqrt_fusion.1) | copy-start | bytes 6148
  182.4 4.4 copy-start.4
  182.4 4.4 copy-start.14
  208.4 3.2 copy-start.10
  208.4 3.2 copy-start.17
  211.6 1.3 copy-start.11
  211.6 1.7 copy-start.12
  215.4 2.8 copy-start.9
  216.6 1.6 copy-start.5
  218.2 1.9 copy-start
  218.2 1.9 copy-start.24
  332.4 3.0 copy-start.8
  332.5 3.0 copy-start.15
  335.5 2.4 copy-start.29
  335.5 3.0 copy-start.30
  346.9 87.9 %copy-start.20 = (f32[1280]{0:T(1024)S(1)}, f32[1280]{0:T(1024)}, u32[]{:S(2)}) copy-start(f32[1280]{0:T(1024)} %get-tuple-element.74) | copy-start | bytes 15364
  434.8 3.1 copy-start.1
  434.8 3.3 copy-start.3
  434.8 3.3 copy-start.19
  434.8 3.3 copy-start.22
  434.8 3.2 copy-start.25
  443.2 16.1 %copy-start.28 = (f32[80]{0:T(128)S(1)}, f32[80]{0:T(128)}, u32[]{:S(2)}) copy-start(f32[80]{0:T(128)} %param.16) | copy-start | bytes 964
  466.2 5.0 %copy-start.6 = (f32[320,1,4,160]{0,3,1,2:T(8,128)S(1)}, f32[320,1,4,160]{0,3,1,2:T(8,128)}, u32[]{:S(2)}) copy-start(f32[320,1,4,160]{0,3,1,2:T(8,128)} %get-tuple-element.82) | copy-start | bytes 2457604
  466.2 6.2 %copy-start.13 = (bf16[3,320,640]{2,1,0:T(8,128)(2,1)S(1)}, bf16[3,320,640]{2,1,0:T(8,128)(2,1)}, u32[]{:S(2)}) copy-start(bf16[3,320,640]{2,1,0:T(8,128)(2,1)} %get-tuple-element.56) | copy-start | bytes 3686404
Sparse Core Ops, SparseCore 0:
  92.4 34.3 all-gather.6
  128.7 41.1 all-gather.10
  171.8 36.5 all-gather.8
  248.2 78.4 reduce-scatter.1
